TPU v7x, 32 devices: a whole 2x2x4 slice. The times are simulated.
32 devices in a mesh: dp: 16 (over z, x, core), tensor: 2 (over y).
Axes of the slice: x: 2, y: 2, z: 4, core: 2. Of those that a mesh axis runs over, the one named last changes fastest.
Arguments:
- layer_input: bfloat16 [2, 8192, 1024], P(None, ('dp', 'tensor')), may hold values from -6 to 6
- segment_ids: int32 [2, 8192], P(None, 'dp'), may hold values from 0 to 5, as said below
- qkv_weight: bfloat16 [3, 1024, 1024], P(None, 'dp', 'tensor'), may hold values from -0.1875 to 0.1875
- qv_bias: bfloat16 [2, 16, 64], P(None, 'tensor', 'dp'), may hold values from -3 to 3
- out_weight: bfloat16 [1024, 1024], P('tensor', 'dp'), may hold values from -1 to 1
- up_weight: bfloat16 [1024, 4096], P('dp', 'tensor'), may hold values from -0.1875 to 0.1875
- up_bias: bfloat16 [2, 2048], P('tensor', 'dp'), may hold values from -3 to 3
- down_weight: bfloat16 [4096, 1024], P('tensor', 'dp'), may hold values from -0.09375 to 0.09375
- norm_gains: float32 [2, 1024], P(None, ('dp', 'tensor')), may hold values from 0.1 to 1.9
- row_biases: float32 [4, 1024], P(None, ('dp', 'tensor')), may hold values from -2 to 2
- cotangent: bfloat16 [2, 8192, 1024], P(None, ('dp', 'tensor')), may hold values from -6 to 6
Outputs:
- layer_output: bfloat16 [2, 8192, 1024], P(None, ('dp', 'tensor'))
- input_grad: bfloat16 [2, 8192, 1024], P(None, ('dp', 'tensor'))
- qkv_weight_grad: float32 [3, 1024, 1024], P(None, 'dp', 'tensor')
- qv_bias_grad: float32 [2, 16, 64], P(None, 'tensor', 'dp')
- out_weight_grad: float32 [1024, 1024], P('tensor', 'dp')
- up_weight_grad: float32 [1024, 4096], P('dp', 'tensor')
- up_bias_grad: float32 [2, 2048], P('tensor', 'dp')
- down_weight_grad: float32 [4096, 1024], P('tensor', 'dp')
- norm_gains_grad: float32 [2, 1024], P(None, ('dp', 'tensor'))
- row_biases_grad: float32 [4, 1024], P(None, ('dp', 'tensor'))
Inputs may be any that keep to these rules, and one draw needn't show every extreme that they name: `segment_ids`: within every sequence of 512 rows, documents 1 to 5 follow one another in order, each 20 to 100 tokens long, and padding with id 0 fills the rest, 12 tokens or more.
All inputs are finite; a program needn't handle non-finite values.
Results may differ from a plain program's by a relative error of at most 0.02.
Values may be sent and summed in bfloat16 or wider, within the bound.
No kernel may reach another device: no remote copies, remote signals or barrier semaphores. Data moves between devices by JAX's collectives and lax.ppermute only.
A program may use at most 192 MiB of HBM per device.

v0:
```python
import jax
import jax.numpy as jnp
from jax import lax
from jax.sharding import PartitionSpec as P

HEAD_DIM = 64


def gelu_exact(values):
    return jax.nn.gelu(values, approximate=False)


def normalize(rows, gain, shift):
    centered = rows - jnp.mean(rows, axis=-1, keepdims=True)
    variance = jnp.mean(centered * centered, axis=-1, keepdims=True)
    inverse = lax.rsqrt(variance + 1e-05)
    normed = centered * inverse
    return (normed * gain + shift, normed, inverse)


def norm_back(grad, normed, inverse, gain):
    scaled = grad * gain
    return inverse * (
        scaled
        - jnp.mean(scaled, axis=-1, keepdims=True)
        - normed * jnp.mean(scaled * normed, axis=-1, keepdims=True)
    )


def attend(query, keys, values, keep_mask, scale):
    scores = jnp.einsum("qhd,khd->hqk", query, keys, preferred_element_type=jnp.float32) * scale
    masked = jnp.where(keep_mask[None], scores, -1e30)
    highest = jnp.max(masked, axis=-1, keepdims=True)
    shifted = jnp.exp(masked - highest)
    totals = jnp.sum(shifted, axis=-1, keepdims=True)
    probs = (shifted / totals).astype(jnp.bfloat16)
    context = jnp.einsum("hqk,khd->qhd", probs, values, preferred_element_type=jnp.float32)
    return (context, highest + jnp.log(totals))


def attend_back(query, keys, values, keep_mask, logsumexp, grad_context, scale):
    scores = jnp.einsum("qhd,khd->hqk", query, keys, preferred_element_type=jnp.float32) * scale
    masked = jnp.where(keep_mask[None], scores, -1e30)
    probs = jnp.exp(masked - logsumexp)
    probs_low = probs.astype(jnp.bfloat16)
    grad_values = jnp.einsum(
        "hqk,qhd->khd", probs_low, grad_context, preferred_element_type=jnp.float32
    )
    grad_probs = jnp.einsum(
        "qhd,khd->hqk", grad_context, values, preferred_element_type=jnp.float32
    )
    grad_scores = probs * (grad_probs - jnp.sum(probs * grad_probs, axis=-1, keepdims=True))
    grad_low = grad_scores.astype(jnp.bfloat16)
    grad_query = (
        jnp.einsum("hqk,khd->qhd", grad_low, keys, preferred_element_type=jnp.float32) * scale
    )
    grad_keys = (
        jnp.einsum("hqk,qhd->khd", grad_low, query, preferred_element_type=jnp.float32) * scale
    )
    return (grad_query, grad_keys, grad_values)


def local(
    layer_input,
    segment_ids,
    qkv_weight,
    qv_bias,
    out_weight,
    up_weight,
    up_bias,
    down_weight,
    norm_gains,
    row_biases,
    cotangent,
):
    gains_all, biases_all = (
        lax.all_gather(norm_gains, ("dp", "tensor"), axis=1, tiled=True),
        lax.all_gather(row_biases, ("dp", "tensor"), axis=1, tiled=True),
    )
    shards = (qkv_weight, qv_bias, out_weight, up_weight, up_bias, down_weight)
    dp_count = lax.axis_size("dp")
    seq_len = segment_ids.shape[1]
    heads_local = qv_bias.shape[1]
    width_local = heads_local * HEAD_DIM
    scale = HEAD_DIM ** (-0.5)

    def micro_step(carry, inputs):
        rows_in, segments, grad_rows = inputs
        qkv_full, qv_full, out_full, up_full, upb_full, down_full = (
            lax.all_gather(shards[0], "dp", axis=1, tiled=True),
            lax.all_gather(shards[1], "dp", axis=2, tiled=True),
            lax.all_gather(shards[2], "dp", axis=1, tiled=True),
            lax.all_gather(shards[3], "dp", axis=0, tiled=True),
            lax.all_gather(shards[4], "dp", axis=1, tiled=True),
            lax.all_gather(shards[5], "dp", axis=1, tiled=True),
        )
        gathered = lax.all_gather(rows_in, "tensor", axis=0, tiled=True)
        projected = jnp.einsum(
            "rd,kdc->krc", gathered, qkv_full, preferred_element_type=jnp.float32
        )
        bias_flat = qv_full.reshape(2, width_local).astype(jnp.float32)
        split = (seq_len, heads_local, HEAD_DIM)
        query = (projected[0] + bias_flat[0]).astype(jnp.bfloat16).reshape(split)
        keys = projected[1].astype(jnp.bfloat16).reshape(split)
        values = (projected[2] + bias_flat[1]).astype(jnp.bfloat16).reshape(split)
        keep_mask = segments[:, None] == segments[None, :]
        attended, logsumexp = attend(query, keys, values, keep_mask, scale)
        context = attended.reshape(seq_len, width_local).astype(jnp.bfloat16)
        attention = lax.psum_scatter(
            jnp.dot(context, out_full, preferred_element_type=jnp.float32).astype(jnp.bfloat16),
            "tensor",
            scatter_dimension=0,
            tiled=True,
        ).astype(jnp.float32)
        residual_one = rows_in.astype(jnp.float32) + attention + biases_all[0]
        hidden, normed_one, inverse_one = normalize(residual_one, gains_all[0], biases_all[1])
        hidden_rows = lax.all_gather(hidden.astype(jnp.bfloat16), "tensor", axis=0, tiled=True)
        upper = jnp.dot(
            hidden_rows, up_full, preferred_element_type=jnp.float32
        ) + upb_full.reshape(-1).astype(jnp.float32)
        activated = gelu_exact(upper).astype(jnp.bfloat16)
        branch = lax.psum_scatter(
            jnp.dot(activated, down_full, preferred_element_type=jnp.float32).astype(jnp.bfloat16),
            "tensor",
            scatter_dimension=0,
            tiled=True,
        ).astype(jnp.float32)
        residual_two = hidden + branch + biases_all[2]
        result, normed_two, inverse_two = normalize(residual_two, gains_all[1], biases_all[3])
        qkv_back, qv_back, out_back, up_back, upb_back, down_back = (
            lax.all_gather(shards[0], "dp", axis=1, tiled=True),
            lax.all_gather(shards[1], "dp", axis=2, tiled=True),
            lax.all_gather(shards[2], "dp", axis=1, tiled=True),
            lax.all_gather(shards[3], "dp", axis=0, tiled=True),
            lax.all_gather(shards[4], "dp", axis=1, tiled=True),
            lax.all_gather(shards[5], "dp", axis=1, tiled=True),
        )
        grad_output = grad_rows.astype(jnp.float32)
        gain_two_grad = jnp.sum(grad_output * normed_two, axis=0)
        shift_two_grad = jnp.sum(grad_output, axis=0)
        grad_two = norm_back(grad_output, normed_two, inverse_two, gains_all[1])
        down_bias_grad = jnp.sum(grad_two, axis=0)
        branch_rows = lax.all_gather(grad_two.astype(jnp.bfloat16), "tensor", axis=0, tiled=True)
        down_grad = jnp.einsum(
            "rf,rd->fd", activated, branch_rows, preferred_element_type=jnp.float32
        )
        grad_active = jnp.einsum(
            "rd,fd->rf", branch_rows, down_back, preferred_element_type=jnp.float32
        )
        gelu_pull = jax.vjp(gelu_exact, upper)[1]
        grad_upper = gelu_pull(grad_active)[0].astype(jnp.bfloat16)
        up_bias_grad = jnp.sum(grad_upper.astype(jnp.float32), axis=0).reshape(1, -1)
        up_grad = jnp.einsum(
            "rd,rf->df", hidden_rows, grad_upper, preferred_element_type=jnp.float32
        )
        grad_hidden = grad_two + lax.psum_scatter(
            jnp.einsum("rf,df->rd", grad_upper, up_back, preferred_element_type=jnp.float32).astype(
                jnp.bfloat16
            ),
            "tensor",
            scatter_dimension=0,
            tiled=True,
        ).astype(jnp.float32)
        gain_one_grad = jnp.sum(grad_hidden * normed_one, axis=0)
        shift_one_grad = jnp.sum(grad_hidden, axis=0)
        grad_one = norm_back(grad_hidden, normed_one, inverse_one, gains_all[0])
        out_bias_grad = jnp.sum(grad_one, axis=0)
        attention_rows = lax.all_gather(grad_one.astype(jnp.bfloat16), "tensor", axis=0, tiled=True)
        out_grad = jnp.einsum(
            "rc,rd->cd", context, attention_rows, preferred_element_type=jnp.float32
        )
        grad_context = (
            jnp.einsum("rd,cd->rc", attention_rows, out_back, preferred_element_type=jnp.float32)
            .astype(jnp.bfloat16)
            .reshape(split)
        )
        grad_query, grad_keys, grad_values = attend_back(
            query, keys, values, keep_mask, logsumexp, grad_context, scale
        )
        grad_qkv = (
            jnp.stack([grad_query, grad_keys, grad_values])
            .reshape(3, seq_len, width_local)
            .astype(jnp.bfloat16)
        )
        bias_sums = jnp.sum(jnp.stack([grad_qkv[0], grad_qkv[2]]).astype(jnp.float32), axis=1)
        qv_grad = bias_sums.reshape(2, heads_local, HEAD_DIM)
        qkv_grad = jnp.einsum("rd,krc->kdc", gathered, grad_qkv, preferred_element_type=jnp.float32)
        input_grad = (
            grad_one
            + lax.psum_scatter(
                jnp.einsum(
                    "krc,kdc->rd", grad_qkv, qkv_back, preferred_element_type=jnp.float32
                ).astype(jnp.bfloat16),
                "tensor",
                scatter_dimension=0,
                tiled=True,
            ).astype(jnp.float32)
        ).astype(jnp.bfloat16)
        gains_grad = jnp.stack([gain_one_grad, gain_two_grad])
        biases_grad = jnp.stack([out_bias_grad, shift_one_grad, down_bias_grad, shift_two_grad])
        updates = (
            qkv_grad,
            qv_grad,
            out_grad,
            up_grad,
            up_bias_grad,
            down_grad,
            gains_grad,
            biases_grad,
        )
        carry = tuple((total + update for total, update in zip(carry, updates)))
        return (carry, (result.astype(jnp.bfloat16), input_grad))

    initial = (
        jnp.zeros((3, qkv_weight.shape[1] * dp_count, qkv_weight.shape[2]), jnp.float32),
        jnp.zeros((2, qv_bias.shape[1], qv_bias.shape[2] * dp_count), jnp.float32),
        jnp.zeros((out_weight.shape[0], out_weight.shape[1] * dp_count), jnp.float32),
        jnp.zeros((up_weight.shape[0] * dp_count, up_weight.shape[1]), jnp.float32),
        jnp.zeros((1, up_bias.shape[1] * dp_count), jnp.float32),
        jnp.zeros((down_weight.shape[0], down_weight.shape[1] * dp_count), jnp.float32),
        jnp.zeros(gains_all.shape, jnp.float32),
        jnp.zeros(biases_all.shape, jnp.float32),
    )
    totals, (outputs, input_grads) = lax.scan(
        micro_step, initial, (layer_input, segment_ids, cotangent)
    )
    qkv_sum, qv_sum, out_sum, up_sum, upb_sum, down_sum = (
        lax.psum_scatter(
            totals[0].astype(jnp.bfloat16), "dp", scatter_dimension=1, tiled=True
        ).astype(jnp.float32),
        lax.psum_scatter(
            totals[1].astype(jnp.bfloat16), "dp", scatter_dimension=2, tiled=True
        ).astype(jnp.float32),
        lax.psum_scatter(
            totals[2].astype(jnp.bfloat16), "dp", scatter_dimension=1, tiled=True
        ).astype(jnp.float32),
        lax.psum_scatter(
            totals[3].astype(jnp.bfloat16), "dp", scatter_dimension=0, tiled=True
        ).astype(jnp.float32),
        lax.psum_scatter(
            totals[4].astype(jnp.bfloat16), "dp", scatter_dimension=1, tiled=True
        ).astype(jnp.float32),
        lax.psum_scatter(
            totals[5].astype(jnp.bfloat16), "dp", scatter_dimension=1, tiled=True
        ).astype(jnp.float32),
    )
    gains_sum, biases_sum = (
        lax.psum_scatter(totals[6], ("dp", "tensor"), scatter_dimension=1, tiled=True),
        lax.psum_scatter(totals[7], ("dp", "tensor"), scatter_dimension=1, tiled=True),
    )
    return (
        outputs,
        input_grads,
        qkv_sum,
        qv_sum,
        out_sum,
        up_sum,
        upb_sum,
        down_sum,
        gains_sum,
        biases_sum,
    )


def solution(mesh):
    return jax.shard_map(
        local,
        mesh=mesh,
        in_specs=(
            P(None, ("dp", "tensor"), None),
            P(None, "dp"),
            P(None, "dp", "tensor"),
            P(None, "tensor", "dp"),
            P("tensor", "dp"),
            P("dp", "tensor"),
            P("tensor", "dp"),
            P("tensor", "dp"),
            P(None, ("dp", "tensor")),
            P(None, ("dp", "tensor")),
            P(None, ("dp", "tensor"), None),
        ),
        out_specs=(
            P(None, ("dp", "tensor"), None),
            P(None, ("dp", "tensor"), None),
            P(None, "dp", "tensor"),
            P(None, "tensor", "dp"),
            P("tensor", "dp"),
            P("dp", "tensor"),
            P("tensor", "dp"),
            P("tensor", "dp"),
            P(None, ("dp", "tensor")),
            P(None, ("dp", "tensor")),
        ),
        check_vma=False,
    )
```

profile of v0, /device:TPU:0, one launch (start us, length us, event | category | flops | bytes accessed | tf_op | source)
XLA Modules:
  0.0 1590.4 jit_solution(6932965279047940089)
XLA Ops:
  8.8 70.0 %all-gather.2 = f32[32,32,2]{1,2,0:T(2,128)S(1)} all-gather(f32[1,32,2]{1,2,0:T(2,128)} %bitcast.322), channel_id=1, replica_groups=mesh['dp'=16,'tensor'=2] {'dp','tensor'}, dimensions={0}, use_global_device_ids=true | all-gather | bytes 8448 | tf_op jit(solution)/shard_map/all_gather | solution.py:77
  78.8 63.9 %all-gather.1 = f32[32,32,4]{1,2,0:T(4,128)S(1)} all-gather(f32[1,32,4]{1,2,0:T(4,128)} %bitcast.321), channel_id=1, replica_groups=mesh['dp'=16,'tensor'=2] {'dp','tensor'}, dimensions={0}, use_global_device_ids=true | all-gather | bytes 16896 | tf_op jit(solution)/shard_map/all_gather | solution.py:78
  142.9 833.3 %while.29 = (s32[]{:T(128)}, f32[3,1024,512]{1,2,0:T(8,128)}, f32[2,8,64]{2,1,0:T(8,128)S(1)}, f32[512,1024]{1,0:T(8,128)}, f32[1024,2048]{1,0:T(8,128)}, /*inde...) while((s32[]{:T(128)}, f32[3,1024,512]{1,2,0:T(8,128)}, ...), condition=%wide.region_24.25_spmd.clone, body=%wide.region_0.24_spmd.clone.sunk | while | flops 21109161984 | bytes 468527744 | solution.py:224
  147.3 17.2 %all_gather.62 = bf16[2,8,64]{1,0,2:T(2,128)(2,1)S(1)} all-gather(bf16[2,8,4]{1,0,2:T(2,128)(2,1)S(1)} %get-tuple-element.616), channel_id=1, replica_groups=mesh['dp'=16,'tensor'=2] {'dp'}, dimensions={2}, use_global_device_ids=true | all-gather | bytes 2176 | tf_op jit(solution)/shard_map/while/body/eval_jaxpr/all_gather | solution.py:91
  165.4 47.4 %all-gather.17.cloned.1.call-done = bf16[3,1024,512]{2,1,0:T(8,128)(2,1)} async-done(((bf16[3,64,512]{2,1,0:T(8,128)(2,1)}), bf16[3,1024,512]{2,1,0:T(8,128)(2,1)}) %all-gather.17.cloned.1.call-update) | async-done | bytes 3145744 | tf_op jit(solution)/shard_map/while/body/eval_jaxpr/all_gather | solution.py:90
  223.8 28.0 %all-gather.19.cloned.1.call-done = bf16[512,1024]{0,1:T(8,128)(2,1)} async-done(((bf16[512,64]{0,1:T(8,128)(2,1)}), bf16[512,1024]{0,1:T(8,128)(2,1)}) %all-gather.19.cloned.1.call-update) | async-done | bytes 1048592 | tf_op jit(solution)/shard_map/while/body/eval_jaxpr/all_gather | solution.py:92
  255.5 18.7 %reduce-scatter.33.cloned.1.call-done = bf16[256,1024]{1,0:T(8,128)(2,1)} async-done(((bf16[512,1024]{1,0:T(8,128)(2,1)}), bf16[256,1024]{1,0:T(8,128)(2,1)}) %reduce-scatter.33.cloned.1.call-update) | async-done | bytes 524304 | tf_op jit(solution)/shard_map/while/body/eval_jaxpr/reduce_scatter | solution.py:109
  279.9 21.6 %all_gather.60 = bf16[1,2048]{1,0:T(2,128)(2,1)S(1)} all-gather(bf16[1,128]{1,0:T(2,128)(2,1)S(1)} %copy-done.14), channel_id=1, replica_groups=mesh['dp'=16,'tensor'=2] {'dp'}, dimensions={1}, use_global_device_ids=true | all-gather | bytes 4352 | tf_op jit(solution)/shard_map/while/body/eval_jaxpr/all_gather | solution.py:94
  301.5 25.6 %all-gather.23.cloned.1.call-done = bf16[1024,2048]{1,0:T(8,128)(2,1)} async-done(((bf16[64,2048]{1,0:T(8,128)(2,1)}), bf16[1024,2048]{1,0:T(8,128)(2,1)}) %all-gather.23.cloned.1.call-update) | async-done | bytes 4194320 | tf_op jit(solution)/shard_map/while/body/eval_jaxpr/all_gather | solution.py:93
  327.0 21.9 %all-gather.21.cloned.1.call-done = bf16[512,1024]{1,0:T(8,128)(2,1)} async-done(((bf16[256,1024]{1,0:T(8,128)(2,1)}), bf16[512,1024]{1,0:T(8,128)(2,1)}) %all-gather.21.cloned.1.call-update) | async-done | bytes 1048592 | tf_op jit(solution)/shard_map/while/body/eval_jaxpr/all_gather | solution.py:117
  348.9 15.2 multiply_convert_fusion.4
  364.1 37.9 %all-gather.25.cloned.1.call-done = bf16[2048,1024]{0,1:T(8,128)(2,1)} async-done(((bf16[2048,64]{0,1:T(8,128)(2,1)}), bf16[2048,1024]{0,1:T(8,128)(2,1)}) %all-gather.25.cloned.1.call-update) | async-done | bytes 4194320 | tf_op jit(solution)/shard_map/while/body/eval_jaxpr/all_gather | solution.py:95
  402.1 6.2 convolution_convert_fusion.9
  408.4 18.9 %reduce-scatter.35.cloned.1.call-done = bf16[256,1024]{1,0:T(8,128)(2,1)} async-done(((bf16[512,1024]{1,0:T(8,128)(2,1)}), bf16[256,1024]{1,0:T(8,128)(2,1)}) %reduce-scatter.35.cloned.1.call-update) | async-done | bytes 524304 | tf_op jit(solution)/shard_map/while/body/eval_jaxpr/reduce_scatter | solution.py:122
  433.7 21.1 %all-gather.27.cloned.1.call-done = bf16[512,1024]{1,0:T(8,128)(2,1)} async-done(((bf16[256,1024]{1,0:T(8,128)(2,1)}), bf16[512,1024]{1,0:T(8,128)(2,1)}) %all-gather.27.cloned.1.call-update) | async-done | bytes 1048592 | tf_op jit(solution)/shard_map/while/body/eval_jaxpr/all_gather | solution.py:143
  454.8 8.7 convert_reduce_fusion.6
  470.6 18.2 %reduce-scatter.37.cloned.1.call-done = bf16[256,1024]{1,0:T(8,128)(2,1)} async-done(((bf16[512,1024]{1,0:T(8,128)(2,1)}), bf16[256,1024]{1,0:T(8,128)(2,1)}) %reduce-scatter.37.cloned.1.call-update) | async-done | bytes 524304 | tf_op jit(solution)/shard_map/while/body/eval_jaxpr/reduce_scatter | solution.py:156
  494.4 7.7 select_add_fusion.11
  502.1 5.7 select_add_fusion.10
  507.8 7.4 all-gather.29.cloned.1.call-done
  543.1 12.2 reduce-scatter.39.cloned.1.call-done
  561.3 21.4 %all_gather.62 = bf16[2,8,64]{1,0,2:T(2,128)(2,1)S(1)} all-gather(bf16[2,8,4]{1,0,2:T(2,128)(2,1)S(1)} %get-tuple-element.616), channel_id=1, replica_groups=mesh['dp'=16,'tensor'=2] {'dp'}, dimensions={2}, use_global_device_ids=true | all-gather | bytes 2176 | tf_op jit(solution)/shard_map/while/body/eval_jaxpr/all_gather | solution.py:91
  583.1 45.9 %all-gather.17.cloned.1.call-done = bf16[3,1024,512]{2,1,0:T(8,128)(2,1)} async-done(((bf16[3,64,512]{2,1,0:T(8,128)(2,1)}), bf16[3,1024,512]{2,1,0:T(8,128)(2,1)}) %all-gather.17.cloned.1.call-update) | async-done | bytes 3145744 | tf_op jit(solution)/shard_map/while/body/eval_jaxpr/all_gather | solution.py:90
  640.0 27.8 %all-gather.19.cloned.1.call-done = bf16[512,1024]{0,1:T(8,128)(2,1)} async-done(((bf16[512,64]{0,1:T(8,128)(2,1)}), bf16[512,1024]{0,1:T(8,128)(2,1)}) %all-gather.19.cloned.1.call-update) | async-done | bytes 1048592 | tf_op jit(solution)/shard_map/while/body/eval_jaxpr/all_gather | solution.py:92
  671.5 18.7 %reduce-scatter.33.cloned.1.call-done = bf16[256,1024]{1,0:T(8,128)(2,1)} async-done(((bf16[512,1024]{1,0:T(8,128)(2,1)}), bf16[256,1024]{1,0:T(8,128)(2,1)}) %reduce-scatter.33.cloned.1.call-update) | async-done | bytes 524304 | tf_op jit(solution)/shard_map/while/body/eval_jaxpr/reduce_scatter | solution.py:109
  695.9 21.5 %all_gather.60 = bf16[1,2048]{1,0:T(2,128)(2,1)S(1)} all-gather(bf16[1,128]{1,0:T(2,128)(2,1)S(1)} %copy-done.14), channel_id=1, replica_groups=mesh['dp'=16,'tensor'=2] {'dp'}, dimensions={1}, use_global_device_ids=true | all-gather | bytes 4352 | tf_op jit(solution)/shard_map/while/body/eval_jaxpr/all_gather | solution.py:94
  717.4 25.6 %all-gather.23.cloned.1.call-done = bf16[1024,2048]{1,0:T(8,128)(2,1)} async-done(((bf16[64,2048]{1,0:T(8,128)(2,1)}), bf16[1024,2048]{1,0:T(8,128)(2,1)}) %all-gather.23.cloned.1.call-update) | async-done | bytes 4194320 | tf_op jit(solution)/shard_map/while/body/eval_jaxpr/all_gather | solution.py:93
  743.0 21.9 %all-gather.21.cloned.1.call-done = bf16[512,1024]{1,0:T(8,128)(2,1)} async-done(((bf16[256,1024]{1,0:T(8,128)(2,1)}), bf16[512,1024]{1,0:T(8,128)(2,1)}) %all-gather.21.cloned.1.call-update) | async-done | bytes 1048592 | tf_op jit(solution)/shard_map/while/body/eval_jaxpr/all_gather | solution.py:117
  764.9 15.2 multiply_convert_fusion.4
  780.1 37.9 %all-gather.25.cloned.1.call-done = bf16[2048,1024]{0,1:T(8,128)(2,1)} async-done(((bf16[2048,64]{0,1:T(8,128)(2,1)}), bf16[2048,1024]{0,1:T(8,128)(2,1)}) %all-gather.25.cloned.1.call-update) | async-done | bytes 4194320 | tf_op jit(solution)/shard_map/while/body/eval_jaxpr/all_gather | solution.py:95
  818.1 6.2 convolution_convert_fusion.9
  824.4 18.9 %reduce-scatter.35.cloned.1.call-done = bf16[256,1024]{1,0:T(8,128)(2,1)} async-done(((bf16[512,1024]{1,0:T(8,128)(2,1)}), bf16[256,1024]{1,0:T(8,128)(2,1)}) %reduce-scatter.35.cloned.1.call-update) | async-done | bytes 524304 | tf_op jit(solution)/shard_map/while/body/eval_jaxpr/reduce_scatter | solution.py:122
  849.8 21.0 %all-gather.27.cloned.1.call-done = bf16[512,1024]{1,0:T(8,128)(2,1)} async-done(((bf16[256,1024]{1,0:T(8,128)(2,1)}), bf16[512,1024]{1,0:T(8,128)(2,1)}) %all-gather.27.cloned.1.call-update) | async-done | bytes 1048592 | tf_op jit(solution)/shard_map/while/body/eval_jaxpr/all_gather | solution.py:143
  870.8 8.7 convert_reduce_fusion.6
  886.6 18.2 %reduce-scatter.37.cloned.1.call-done = bf16[256,1024]{1,0:T(8,128)(2,1)} async-done(((bf16[512,1024]{1,0:T(8,128)(2,1)}), bf16[256,1024]{1,0:T(8,128)(2,1)}) %reduce-scatter.37.cloned.1.call-update) | async-done | bytes 524304 | tf_op jit(solution)/shard_map/while/body/eval_jaxpr/reduce_scatter | solution.py:156
  909.9 10.1 select_add_fusion.11
  920.1 9.1 select_add_fusion.10
  955.3 7.7 bitcast_add_fusion.2
  962.9 8.3 reduce-scatter.39.cloned.1.call-done
  986.6 6.0 convert_element_type.143
  992.8 7.4 copy.56
  1002.0 61.3 %all-reduce = bf16[2,8,64]{1,2,0:T(8,128)(2,1)S(1)} all-reduce(bf16[2,8,64]{1,2,0:T(8,128)(2,1)S(1)} %copy.54), channel_id=8, replica_groups=mesh['dp'=16,'tensor'=2] {'dp'}, use_global_device_ids=true, to_apply=%region_26.27.clone | all-reduce | flops 1024 | bytes 4096
  1065.3 107.1 %reduce-scatter.29.cloned.1.call-done = f32[32,2]{1,0:T(8,128)} async-done(((f32[1024,2]{1,0:T(8,128)}), f32[32,2]{1,0:T(8,128)}) %reduce-scatter.29.cloned.1.call-update) | async-done | bytes 272
  1173.8 130.2 %reduce-scatter.31.cloned.1.call-done = f32[32,4]{1,0:T(8,128)} async-done(((f32[1024,4]{1,0:T(8,128)}), f32[32,4]{1,0:T(8,128)}) %reduce-scatter.31.cloned.1.call-update) | async-done | bytes 528
  1305.4 56.0 %reduce-scatter.21.cloned.1.call-done = bf16[512,64]{0,1:T(8,128)(2,1)} async-done(((bf16[512,1024]{0,1:T(8,128)(2,1)}), bf16[512,64]{0,1:T(8,128)(2,1)}) %reduce-scatter.21.cloned.1.call-update) | async-done | bytes 65552 | tf_op jit(solution)/shard_map/reduce_scatter | solution.py:234
  1362.9 67.5 %reduce-scatter.19.cloned.1.call-done = bf16[3,64,512]{2,1,0:T(8,128)(2,1)} async-done(((bf16[3,1024,512]{2,1,0:T(8,128)(2,1)}), bf16[3,64,512]{2,1,0:T(8,128)(2,1)}) %reduce-scatter.19.cloned.1.call-update) | async-done | bytes 196624 | tf_op jit(solution)/shard_map/reduce_scatter | solution.py:228
  1432.1 73.4 %reduce-scatter.23.cloned.1.call-done = bf16[64,2048]{1,0:T(8,128)(2,1)} async-done(((bf16[1024,2048]{1,0:T(8,128)(2,1)}), bf16[64,2048]{1,0:T(8,128)(2,1)}) %reduce-scatter.23.cloned.1.call-update) | async-done | bytes 262160 | tf_op jit(solution)/shard_map/reduce_scatter | solution.py:237
  1507.3 73.6 %reduce-scatter.25.cloned.1.call-done = bf16[2048,64]{0,1:T(8,128)(2,1)} async-done(((bf16[2048,1024]{0,1:T(8,128)(2,1)}), bf16[2048,64]{0,1:T(8,128)(2,1)}) %reduce-scatter.25.cloned.1.call-update) | async-done | bytes 262160 | tf_op jit(solution)/shard_map/reduce_scatter | solution.py:243
  (286 shorter events, 169.0 us)
Async XLA Ops:
  143.1 22.3 %all-gather.15.cloned.1.call-start = ((), (), s32[]{:S(2)}) async-start(), calls=%async_computation.18 | async-start | bytes 1572864 | tf_op jit(solution)/shard_map/while/body/eval_jaxpr/all_gather | solution.py:97
  145.1 67.8 %all-gather.17.cloned.1.call-start = ((), (), s32[]{:S(2)}) async-start(), calls=%async_computation.19 | async-start | bytes 3342336 | tf_op jit(solution)/shard_map/while/body/eval_jaxpr/all_gather | solution.py:90
  145.8 106.0 %all-gather.19.cloned.1.call-start = ((), (), s32[]{:S(2)}) async-start(), calls=%async_computation.20 | async-start | bytes 1114112 | tf_op jit(solution)/shard_map/while/body/eval_jaxpr/all_gather | solution.py:92
  146.6 127.6 %reduce-scatter.33.cloned.1.call-start = ((), (), s32[]{:S(2)}) async-start(), calls=%async_computation.21 | async-start | bytes 1572864 | tf_op jit(solution)/shard_map/while/body/eval_jaxpr/reduce_scatter | solution.py:109
  223.8 55.3 %copy-start.12 = (bf16[8,64,512]{2,1,0:T(8,128)(2,1)}, bf16[8,64,512]{2,1,0:T(8,128)(2,1)S(1)}, u32[]{:S(2)}) copy-start(bf16[8,64,512]{2,1,0:T(8,128)(2,1)S(1)} %fusion.158) | copy-start | bytes 1572868 | tf_op jit(solution)/shard_map/while
  223.8 50.4 %copy-start.2 = (bf16[2,256,1024]{2,1,0:T(8,128)(2,1)S(1)}, bf16[2,256,1024]{2,1,0:T(8,128)(2,1)}, u32[]{:S(2)}) copy-start(bf16[2,256,1024]{2,1,0:T(8,128)(2,1)} %get-tuple-element.613) | copy-start | bytes 3145732 | tf_op jit(solution)/shard_map/while
  251.8 28.1 %copy-start.14 = (bf16[1,128]{1,0:T(2,128)(2,1)S(1)}, bf16[1,128]{1,0:T(2,128)(2,1)}, u32[]{:S(2)}) copy-start(bf16[1,128]{1,0:T(2,128)(2,1)} %get-tuple-element.621) | copy-start | bytes 772 | tf_op jit(solution)/shard_map/while
  254.8 72.2 %all-gather.23.cloned.1.call-start = ((), (), s32[]{:S(2)}) async-start(), calls=%async_computation.23 | async-start | bytes 4456448 | tf_op jit(solution)/shard_map/while/body/eval_jaxpr/all_gather | solution.py:93
  255.4 93.5 %all-gather.21.cloned.1.call-start = ((), (), s32[]{:S(2)}) async-start(), calls=%async_computation.22 | async-start | bytes 1572864 | tf_op jit(solution)/shard_map/while/body/eval_jaxpr/all_gather | solution.py:117
  279.1 123.0 %all-gather.25.cloned.1.call-start = ((), (), s32[]{:S(2)}) async-start(), calls=%async_computation.24 | async-start | bytes 4456448 | tf_op jit(solution)/shard_map/while/body/eval_jaxpr/all_gather | solution.py:95
  279.8 147.5 %reduce-scatter.35.cloned.1.call-start = ((), (), s32[]{:S(2)}) async-start(), calls=%async_computation.25 | async-start | bytes 1572864 | tf_op jit(solution)/shard_map/while/body/eval_jaxpr/reduce_scatter | solution.py:122
  402.0 25.2 %copy-start.1 = (bf16[256,1024]{1,0:T(8,128)(2,1)S(1)}, bf16[256,1024]{1,0:T(8,128)(2,1)}, u32[]{:S(2)}) copy-start(bf16[256,1024]{1,0:T(8,128)(2,1)} %reduce-scatter.33.cloned.1.call-done) | copy-start | bytes 1572868 | tf_op jit(solution)/shard_map/while
  408.3 46.5 %all-gather.27.cloned.1.call-start = ((), (), s32[]{:S(2)}) async-start(), calls=%async_computation.26 | async-start | bytes 1572864 | tf_op jit(solution)/shard_map/while/body/eval_jaxpr/all_gather | solution.py:143
  433.3 55.5 %reduce-scatter.37.cloned.1.call-start = ((), (), s32[]{:S(2)}) async-start(), calls=%async_computation.27 | async-start | bytes 1572864 | tf_op jit(solution)/shard_map/while/body/eval_jaxpr/reduce_scatter | solution.py:156
  454.8 10.1 copy-start.15
  468.3 46.8 %all-gather.29.cloned.1.call-start = ((), (), s32[]{:S(2)}) async-start(), calls=%async_computation.28 | async-start | bytes 1572864 | tf_op jit(solution)/shard_map/while/body/eval_jaxpr/all_gather | solution.py:168
  493.7 61.5 %reduce-scatter.39.cloned.1.call-start = ((), (), s32[]{:S(2)}) async-start(), calls=%async_computation.29 | async-start | bytes 1572864 | tf_op jit(solution)/shard_map/while/body/eval_jaxpr/reduce_scatter | solution.py:190
  494.4 7.7 copy-start.8
  502.1 13.0 copy-start.17
  517.1 9.9 slice-start
  557.4 25.7 %all-gather.15.cloned.1.call-start = ((), (), s32[]{:S(2)}) async-start(), calls=%async_computation.18 | async-start | bytes 1572864 | tf_op jit(solution)/shard_map/while/body/eval_jaxpr/all_gather | solution.py:97
  559.4 69.6 %all-gather.17.cloned.1.call-start = ((), (), s32[]{:S(2)}) async-start(), calls=%async_computation.19 | async-start | bytes 3342336 | tf_op jit(solution)/shard_map/while/body/eval_jaxpr/all_gather | solution.py:90
  559.9 107.9 %all-gather.19.cloned.1.call-start = ((), (), s32[]{:S(2)}) async-start(), calls=%async_computation.20 | async-start | bytes 1114112 | tf_op jit(solution)/shard_map/while/body/eval_jaxpr/all_gather | solution.py:92
  560.5 129.7 %reduce-scatter.33.cloned.1.call-start = ((), (), s32[]{:S(2)}) async-start(), calls=%async_computation.21 | async-start | bytes 1572864 | tf_op jit(solution)/shard_map/while/body/eval_jaxpr/reduce_scatter | solution.py:109
  640.0 55.1 %copy-start.12 = (bf16[8,64,512]{2,1,0:T(8,128)(2,1)}, bf16[8,64,512]{2,1,0:T(8,128)(2,1)S(1)}, u32[]{:S(2)}) copy-start(bf16[8,64,512]{2,1,0:T(8,128)(2,1)S(1)} %fusion.158) | copy-start | bytes 1572868 | tf_op jit(solution)/shard_map/while
  640.0 50.2 %copy-start.2 = (bf16[2,256,1024]{2,1,0:T(8,128)(2,1)S(1)}, bf16[2,256,1024]{2,1,0:T(8,128)(2,1)}, u32[]{:S(2)}) copy-start(bf16[2,256,1024]{2,1,0:T(8,128)(2,1)} %get-tuple-element.613) | copy-start | bytes 3145732 | tf_op jit(solution)/shard_map/while
  667.8 28.1 %copy-start.14 = (bf16[1,128]{1,0:T(2,128)(2,1)S(1)}, bf16[1,128]{1,0:T(2,128)(2,1)}, u32[]{:S(2)}) copy-start(bf16[1,128]{1,0:T(2,128)(2,1)} %get-tuple-element.621) | copy-start | bytes 772 | tf_op jit(solution)/shard_map/while
  670.8 72.2 %all-gather.23.cloned.1.call-start = ((), (), s32[]{:S(2)}) async-start(), calls=%async_computation.23 | async-start | bytes 4456448 | tf_op jit(solution)/shard_map/while/body/eval_jaxpr/all_gather | solution.py:93
  671.4 93.5 %all-gather.21.cloned.1.call-start = ((), (), s32[]{:S(2)}) async-start(), calls=%async_computation.22 | async-start | bytes 1572864 | tf_op jit(solution)/shard_map/while/body/eval_jaxpr/all_gather | solution.py:117
  695.1 123.0 %all-gather.25.cloned.1.call-start = ((), (), s32[]{:S(2)}) async-start(), calls=%async_computation.24 | async-start | bytes 4456448 | tf_op jit(solution)/shard_map/while/body/eval_jaxpr/all_gather | solution.py:95
  695.8 147.5 %reduce-scatter.35.cloned.1.call-start = ((), (), s32[]{:S(2)}) async-start(), calls=%async_computation.25 | async-start | bytes 1572864 | tf_op jit(solution)/shard_map/while/body/eval_jaxpr/reduce_scatter | solution.py:122
  818.1 25.2 %copy-start.1 = (bf16[256,1024]{1,0:T(8,128)(2,1)S(1)}, bf16[256,1024]{1,0:T(8,128)(2,1)}, u32[]{:S(2)}) copy-start(bf16[256,1024]{1,0:T(8,128)(2,1)} %reduce-scatter.33.cloned.1.call-done) | copy-start | bytes 1572868 | tf_op jit(solution)/shard_map/while
  824.3 46.5 %all-gather.27.cloned.1.call-start = ((), (), s32[]{:S(2)}) async-start(), calls=%async_computation.26 | async-start | bytes 1572864 | tf_op jit(solution)/shard_map/while/body/eval_jaxpr/all_gather | solution.py:143
  849.3 55.5 %reduce-scatter.37.cloned.1.call-start = ((), (), s32[]{:S(2)}) async-start(), calls=%async_computation.27 | async-start | bytes 1572864 | tf_op jit(solution)/shard_map/while/body/eval_jaxpr/reduce_scatter | solution.py:156
  870.8 10.1 copy-start.15
  884.3 46.8 %all-gather.29.cloned.1.call-start = ((), (), s32[]{:S(2)}) async-start(), calls=%async_computation.28 | async-start | bytes 1572864 | tf_op jit(solution)/shard_map/while/body/eval_jaxpr/all_gather | solution.py:168
  909.7 61.6 %reduce-scatter.39.cloned.1.call-start = ((), (), s32[]{:S(2)}) async-start(), calls=%async_computation.29 | async-start | bytes 1572864 | tf_op jit(solution)/shard_map/while/body/eval_jaxpr/reduce_scatter | solution.py:190
  909.9 10.1 copy-start.8
  909.9 10.1 copy-start.10
  920.0 11.1 copy-start.17
  933.2 9.9 slice-start
  976.2 87.7 %reduce-scatter.27.cloned.1.call-start = ((), (), s32[]{:S(2)}) async-start(), calls=%async_computation.15 | async-start | bytes 557056
  977.4 195.1 %reduce-scatter.29.cloned.1.call-start = ((), (), s32[]{:S(2)}) async-start(), calls=%async_computation.16 | async-start | bytes 540672
  978.5 325.5 %reduce-scatter.31.cloned.1.call-start = ((), (), s32[]{:S(2)}) async-start(), calls=%async_computation.17 | async-start | bytes 540672
  979.6 381.8 %reduce-scatter.21.cloned.1.call-start = ((), (), s32[]{:S(2)}) async-start(), calls=%async_computation.12 | async-start | bytes 1114112 | tf_op jit(solution)/shard_map/reduce_scatter | solution.py:234
  981.1 449.3 %reduce-scatter.19.cloned.1.call-start = ((), (), s32[]{:S(2)}) async-start(), calls=%async_computation.11 | async-start | bytes 3342336 | tf_op jit(solution)/shard_map/reduce_scatter | solution.py:228
  986.6 519.0 %reduce-scatter.23.cloned.1.call-start = ((), (), s32[]{:S(2)}) async-start(), calls=%async_computation.13 | async-start | bytes 4456448 | tf_op jit(solution)/shard_map/reduce_scatter | solution.py:237
  992.7 588.2 %reduce-scatter.25.cloned.1.call-start = ((), (), s32[]{:S(2)}) async-start(), calls=%async_computation.14 | async-start | bytes 4456448 | tf_op jit(solution)/shard_map/reduce_scatter | solution.py:243
  (23 other events, 73.5 us)
Sparse Core Ops, SparseCore 0:
  146.1 19.2 all-gather.14
  167.6 45.1 all-gather.16
  215.0 36.7 all-gather.18
  254.9 19.2 reduce-scatter.32
  276.4 50.5 all-gather.22
  329.1 19.7 all-gather.20
  351.3 50.7 all-gather.24
  408.4 18.7 reduce-scatter.34
  433.4 21.3 all-gather.26
  468.4 20.3 reduce-scatter.36
  493.8 21.2 all-gather.28
  534.9 20.3 reduce-scatter.38
  560.4 21.2 all-gather.14
  583.8 45.1 all-gather.16
  631.0 36.7 all-gather.18
  670.9 19.2 reduce-scatter.32
  692.4 50.5 all-gather.22
  745.1 19.7 all-gather.20
  767.3 50.7 all-gather.24
  824.5 18.7 reduce-scatter.34
  849.4 21.3 all-gather.26
  884.4 20.3 reduce-scatter.36
  909.8 21.2 all-gather.28
  950.9 20.3 reduce-scatter.38
Sparse Core Ops, SparseCore 1:
  980.8 55.8 reduce-scatter.26
  1039.4 132.9 reduce-scatter.28
  1174.5 129.4 reduce-scatter.30
  1308.1 53.2 reduce-scatter.20
  1365.2 65.1 reduce-scatter.18
  1434.3 71.2 reduce-scatter.22
  1509.8 71.1 reduce-scatter.24
where the time goes:
time: 1590 us
  waiting for transfers between devices  1020 us (64%)
  blocking collectives  277 us (17%)
  matrix products  174 us (11%)
  other arithmetic  62.4 us (4%)
  local copies, waits for them, and re-layouts  35.9 us (2%)
  between operations  16.7 us (1%)
    unnamed x10, waiting for transfers between devices  237 us
    all_gather x2, waiting for transfers between devices, micro_step(): lax.all_gather(shards[0], 'dp', axis=1, tiled=True)  93.3 us
    all_gather x2, waiting for transfers between devices, micro_step(): lax.all_gather(shards[5], 'dp', axis=1, tiled=True)  75.8 us
    reduce_scatter x1, waiting for transfers between devices, local(): lax.psum_scatter(totals[5].astype(jnp.bfloat16), 'dp', scatter_dimension=...  73.6 us
    reduce_scatter x1, waiting for transfers between devices, local(): lax.psum_scatter(totals[3].astype(jnp.bfloat16), 'dp', scatter_dimension=...  73.4 us
    all_gather x1, blocking collectives, local(): lax.all_gather(norm_gains, ('dp', 'tensor'), axis=1, tiled=True)  70 us
    reduce_scatter x1, waiting for transfers between devices, local(): lax.psum_scatter(totals[0].astype(jnp.bfloat16), 'dp', scatter_dimension=...  67.5 us
    all_gather x1, blocking collectives, local(): lax.all_gather(row_biases, ('dp', 'tensor'), axis=1, tiled=True)  63.9 us
  transfers between devices with their start and end apart: 31, of which 29 were waited for; matrix products, arithmetic and copies ran while one was open for 9% of the time, Pallas kernels for 0%

commit v1 on v0

--- a/solution.py
+++ b/solution.py
@@ -1,6 +1,8 @@
 import jax
 import jax.numpy as jnp
 from jax import lax
+from jax.experimental import pallas as pl
+from jax.experimental.pallas import tpu as pltpu
 from jax.sharding import PartitionSpec as P
 
 HEAD_DIM = 64
@@ -60,7 +62,7 @@
     return (grad_query, grad_keys, grad_values)
 
 
-def local(
+def tensor_split(
     layer_input,
     segment_ids,
     qkv_weight,
@@ -262,34 +264,364 @@
     )
 
 
+NEGATIVE = -1e30
+LANES = 2 * HEAD_DIM
+
+
+def half_mask(shape, half):
+    lane = lax.broadcasted_iota(jnp.int32, shape, 1)
+    return (lane // HEAD_DIM) == half
+
+
+def attend_kernel(q_ref, k_ref, v_ref, row_ref, col_ref, context_ref, stats_ref):
+    query, keys, values = q_ref[...], k_ref[...], v_ref[...]
+    keep = col_ref[...] == row_ref[...]
+    total = jnp.zeros(context_ref.shape, jnp.float32)
+    for half in range(2):
+        own = half_mask(query.shape, half)
+        masked_query = jnp.where(own, query, 0) * jnp.asarray(HEAD_DIM**-0.5, query.dtype)
+        scores = lax.dot_general(
+            keys, masked_query, (((1,), (1,)), ((), ())), preferred_element_type=jnp.float32
+        )
+        scores = jnp.where(keep, scores, NEGATIVE)
+        highest = jnp.max(scores, axis=0, keepdims=True)
+        shifted = jnp.exp(scores - highest)
+        sums = jnp.sum(shifted, axis=0, keepdims=True)
+        probs = (shifted * (1.0 / sums)).astype(jnp.bfloat16)
+        own_values = jnp.where(own, values, 0)
+        total += lax.dot_general(
+            probs, own_values, (((0,), (0,)), ((), ())), preferred_element_type=jnp.float32
+        )
+        stats_ref[0, half : half + 1, :] = highest + jnp.log(sums)
+    context_ref[...] = total.astype(context_ref.dtype)
+
+
+def attend_back_kernel(
+    q_ref, k_ref, v_ref, grad_ref, row_ref, col_ref, stats_ref, dq_ref, dk_ref, dv_ref
+):
+    query, keys, values, grad = q_ref[...], k_ref[...], v_ref[...], grad_ref[...]
+    scale = jnp.asarray(HEAD_DIM**-0.5, query.dtype)
+    keep = col_ref[...] == row_ref[...]
+    zero = jnp.zeros(dq_ref.shape, jnp.float32)
+    grad_query, grad_keys, grad_values = zero, zero, zero
+    for half in range(2):
+        own = half_mask(query.shape, half)
+        own_query = jnp.where(own, query, 0) * scale
+        own_keys = jnp.where(own, keys, 0) * scale
+        own_grad = jnp.where(own, grad, 0)
+        contract_last = (((1,), (1,)), ((), ()))
+        scores = lax.dot_general(
+            keys, own_query, contract_last, preferred_element_type=jnp.float32
+        )
+        scores = jnp.where(keep, scores, NEGATIVE)
+        probs = jnp.exp(scores - stats_ref[0, half : half + 1, :])
+        grad_values += jnp.dot(
+            probs.astype(jnp.bfloat16), own_grad, preferred_element_type=jnp.float32
+        )
+        grad_probs = lax.dot_general(
+            values, own_grad, contract_last, preferred_element_type=jnp.float32
+        )
+        weighted = probs * grad_probs
+        grad_scores = (weighted - probs * jnp.sum(weighted, axis=0, keepdims=True)).astype(
+            jnp.bfloat16
+        )
+        grad_keys += jnp.dot(grad_scores, own_query, preferred_element_type=jnp.float32)
+        grad_query += lax.dot_general(
+            grad_scores, own_keys, (((0,), (0,)), ((), ())), preferred_element_type=jnp.float32
+        )
+    dq_ref[...] = grad_query.astype(dq_ref.dtype)
+    dk_ref[...] = grad_keys.astype(dk_ref.dtype)
+    dv_ref[...] = grad_values.astype(dv_ref.dtype)
+
+
+def attention_specs(rows, pairs):
+    def column(offset):
+        return pl.BlockSpec((rows, LANES), lambda i, offset=offset: (0, offset + i))
+
+    row_ids = pl.BlockSpec((1, rows), lambda i: (0, 0))
+    column_ids = pl.BlockSpec((rows, 1), lambda i: (0, 0))
+    stats = pl.BlockSpec((1, 2, rows), lambda i: (i, 0, 0))
+    return column, row_ids, column_ids, stats
+
+
+def attend_call(projected, segments):
+    rows, width = projected.shape[0], projected.shape[1] // 3
+    pairs = width // LANES
+    column, row_ids, column_ids, stats = attention_specs(rows, pairs)
+    return pl.pallas_call(
+        attend_kernel,
+        grid=(pairs,),
+        in_specs=[column(0), column(pairs), column(2 * pairs), row_ids, column_ids],
+        out_specs=[column(0), stats],
+        out_shape=[
+            jax.ShapeDtypeStruct((rows, width), jnp.bfloat16),
+            jax.ShapeDtypeStruct((pairs, 2, rows), jnp.float32),
+        ],
+        compiler_params=pltpu.CompilerParams(vmem_limit_bytes=48 * 1024 * 1024),
+        cost_estimate=pl.CostEstimate(
+            flops=8 * pairs * rows * rows * LANES,
+            bytes_accessed=8 * rows * width,
+            transcendentals=2 * pairs * rows * rows,
+        ),
+        name="attend",
+    )(projected, projected, projected, segments[None, :], segments[:, None])
+
+
+def attend_back_call(projected, grad, segments, stats_in):
+    rows, width = grad.shape
+    pairs = width // LANES
+    column, row_ids, column_ids, stats = attention_specs(rows, pairs)
+    shape = jax.ShapeDtypeStruct((rows, width), jnp.bfloat16)
+    return pl.pallas_call(
+        attend_back_kernel,
+        grid=(pairs,),
+        in_specs=[
+            column(0),
+            column(pairs),
+            column(2 * pairs),
+            column(0),
+            row_ids,
+            column_ids,
+            stats,
+        ],
+        out_specs=[column(0)] * 3,
+        out_shape=[shape] * 3,
+        compiler_params=pltpu.CompilerParams(vmem_limit_bytes=48 * 1024 * 1024),
+        cost_estimate=pl.CostEstimate(
+            flops=20 * pairs * rows * rows * LANES,
+            bytes_accessed=14 * rows * width,
+            transcendentals=2 * pairs * rows * rows,
+        ),
+        name="attend_back",
+    )(projected, projected, projected, grad, segments[None, :], segments[:, None], stats_in)
+
+
+def dot_nn(a, b):
+    return jnp.dot(a, b, preferred_element_type=jnp.float32)
+
+
+def dot_nt(a, b):
+    return lax.dot_general(a, b, (((1,), (1,)), ((), ())), preferred_element_type=jnp.float32)
+
+
+def dot_tn(a, b):
+    return lax.dot_general(a, b, (((0,), (0,)), ((), ())), preferred_element_type=jnp.float32)
+
+
+def gelu_pair(values):
+    cdf = 0.5 * (1.0 + lax.erf(values * (0.5**0.5)))
+    density = jnp.exp(-0.5 * values * values) * (0.5 / jnp.pi) ** 0.5
+    return values * cdf, cdf + values * density
+
+
+def sequence_parallel(
+    layer_input,
+    segment_ids,
+    qkv_weight,
+    qv_bias,
+    out_weight,
+    up_weight,
+    up_bias,
+    down_weight,
+    norm_gains,
+    row_biases,
+    cotangent,
+):
+    low = jnp.bfloat16
+    parts = lax.axis_size("tensor")
+    dp_count = lax.axis_size("dp")
+    mine = lax.axis_index("tensor")
+    swap = [(i, (i + 1) % parts) for i in range(parts)]
+    half = layer_input.shape[1]
+    width = layer_input.shape[2]
+    heads_local = qv_bias.shape[1]
+    width_local = heads_local * HEAD_DIM
+
+    def own_sequence(rows):
+        kept = lax.dynamic_index_in_dim(rows, mine, 0, keepdims=False)
+        sent = lax.dynamic_index_in_dim(rows, 1 - mine, 0, keepdims=False)
+        return jnp.concatenate([kept, lax.ppermute(sent, "tensor", swap)], axis=0)
+
+    def own_rows(rows):
+        received = lax.ppermute(rows[half:], "tensor", swap)
+        first = jnp.where(mine == 0, rows[:half], received)
+        second = jnp.where(mine == 0, received, rows[:half])
+        return jnp.stack([first, second])
+
+    everything = ("tensor", "dp")
+    rows_in = own_sequence(layer_input)
+    segments = lax.dynamic_index_in_dim(segment_ids, mine, 0, keepdims=False)
+    segments = jnp.where(mine == 0, segments, jnp.roll(segments, -half))
+
+    small = jnp.concatenate(
+        [
+            qv_bias.astype(jnp.float32).reshape(-1),
+            up_bias.astype(jnp.float32).reshape(-1),
+            norm_gains.reshape(-1),
+            row_biases.reshape(-1),
+        ]
+    )
+    small_all = lax.all_gather(small, everything, axis=0, tiled=False)
+    small_all = small_all.reshape(parts, dp_count, small.shape[0])
+    sizes = [qv_bias.size, up_bias.size, norm_gains.size, row_biases.size]
+    starts = [0, sizes[0], sum(sizes[:2]), sum(sizes[:3])]
+    qv_all, upb_all, gains_all, biases_all = (
+        small_all[:, :, a : a + n] for a, n in zip(starts, sizes)
+    )
+    qv_all = qv_all.reshape((parts, dp_count) + qv_bias.shape).transpose(2, 0, 3, 1, 4)
+    qv_all = qv_all.reshape(2, parts, width_local)
+    upb_all = upb_all.reshape(parts, -1)
+
+    def whole_rows(values, shard):
+        values = values.reshape((parts, dp_count) + shard.shape).transpose(2, 1, 0, 3)
+        return values.reshape(shard.shape[0], width)
+
+    gains_all = whole_rows(gains_all, norm_gains)
+    biases_all = whole_rows(biases_all, row_biases)
+
+    def gather(piece):
+        return lax.all_gather(piece, everything, axis=0, tiled=True).reshape(
+            parts, width, piece.shape[1]
+        )
+
+    def scatter(blocks):
+        flat = blocks.reshape(parts * width, blocks.shape[2])
+        return lax.psum_scatter(flat, everything, scatter_dimension=0, tiled=True)
+
+    packed = jnp.concatenate(
+        [
+            qkv_weight[0],
+            qkv_weight[1],
+            qkv_weight[2],
+            out_weight.T,
+            up_weight,
+            down_weight.T,
+        ],
+        axis=1,
+    )
+    gathered = gather(packed)
+    wide = 3 * width_local
+    edges = [wide, wide + width_local, wide + width_local + up_weight.shape[1]]
+    qkv_full = gathered[:, :, : edges[0]]
+    out_full = gathered[:, :, edges[0] : edges[1]]
+    up_full = gathered[:, :, edges[1] : edges[2]]
+    down_full = gathered[:, :, edges[2] :]
+    span = range(parts)
+
+    rows_wide = rows_in.astype(jnp.float32)
+    none = jnp.zeros((width_local,), jnp.float32)
+    projected, contexts, stats = [], [], []
+    for t in span:
+        bias = jnp.concatenate([qv_all[0, t], none, qv_all[1, t]])
+        projected.append((dot_nn(rows_in, qkv_full[t]) + bias).astype(low))
+        context, stat = attend_call(projected[t], segments)
+        contexts.append(context)
+        stats.append(stat)
+    attention = sum(dot_nt(contexts[t], out_full[t]) for t in span)
+    residual_one = rows_wide + attention + biases_all[0]
+    hidden, normed_one, inverse_one = normalize(residual_one, gains_all[0], biases_all[1])
+    hidden_low = hidden.astype(low)
+    activated, slopes = [], []
+    for t in span:
+        value, slope = gelu_pair(dot_nn(hidden_low, up_full[t]) + upb_all[t])
+        activated.append(value.astype(low))
+        slopes.append(slope)
+    branch = sum(dot_nt(activated[t], down_full[t]) for t in span)
+    residual_two = hidden + branch + biases_all[2]
+    result, normed_two, inverse_two = normalize(residual_two, gains_all[1], biases_all[3])
+    outputs = own_rows(result.astype(low))
+
+    grad_output = own_sequence(cotangent).astype(jnp.float32)
+    gain_two_grad = jnp.sum(grad_output * normed_two, axis=0)
+    shift_two_grad = jnp.sum(grad_output, axis=0)
+    grad_two = norm_back(grad_output, normed_two, inverse_two, gains_all[1])
+    down_bias_grad = jnp.sum(grad_two, axis=0)
+    branch_grad = grad_two.astype(low)
+    down_grad = jnp.stack([dot_tn(branch_grad, activated[t]).astype(low) for t in span])
+    down_sum = scatter(down_grad)
+    grad_upper = [(dot_nn(branch_grad, down_full[t]) * slopes[t]).astype(low) for t in span]
+    upb_grad = jnp.stack([jnp.sum(grad_upper[t].astype(jnp.float32), axis=0) for t in span])
+    up_grad = jnp.stack([dot_tn(hidden_low, grad_upper[t]).astype(low) for t in span])
+    up_sum = scatter(up_grad)
+    grad_hidden = grad_two + sum(dot_nt(grad_upper[t], up_full[t]) for t in span)
+    gain_one_grad = jnp.sum(grad_hidden * normed_one, axis=0)
+    shift_one_grad = jnp.sum(grad_hidden, axis=0)
+    grad_one = norm_back(grad_hidden, normed_one, inverse_one, gains_all[0])
+    out_bias_grad = jnp.sum(grad_one, axis=0)
+    attention_grad = grad_one.astype(low)
+    last, qv_grads, input_grad = [], [], grad_one
+    for t in span:
+        out_grad = dot_tn(attention_grad, contexts[t]).astype(low)
+        grad_context = dot_nn(attention_grad, out_full[t]).astype(low)
+        triple = attend_back_call(projected[t], grad_context, segments, stats[t])
+        grad_qkv = jnp.concatenate(triple, axis=1)
+        qv_grads.append(
+            jnp.stack([jnp.sum(triple[j].astype(jnp.float32), axis=0) for j in (0, 2)])
+        )
+        qkv_grad = dot_tn(rows_in, grad_qkv).astype(low)
+        last.append(jnp.concatenate([qkv_grad, out_grad], axis=1))
+        input_grad = input_grad + dot_nt(grad_qkv, qkv_full[t])
+    last_sum = scatter(jnp.stack(last))
+    input_grads = own_rows(input_grad.astype(low))
+
+    qv_grads = jnp.stack(qv_grads).reshape(parts, 2, heads_local, dp_count, -1)
+    qv_grads = qv_grads.transpose(0, 3, 1, 2, 4).reshape(parts, dp_count, -1)
+    upb_grad = upb_grad.reshape(parts, dp_count, -1)
+
+    def split_rows(rows):
+        rows = rows.reshape(rows.shape[0], dp_count, parts, -1).transpose(2, 1, 0, 3)
+        return rows.reshape(parts, dp_count, -1)
+
+    gains_grad = jnp.stack([gain_one_grad, gain_two_grad])
+    biases_grad = jnp.stack([out_bias_grad, shift_one_grad, down_bias_grad, shift_two_grad])
+    small_grad = jnp.concatenate(
+        [qv_grads, upb_grad, split_rows(gains_grad), split_rows(biases_grad)], axis=2
+    )
+    small_grad = small_grad.reshape(parts * dp_count, -1)
+    exchanged = lax.all_to_all(small_grad, everything, 0, 0, tiled=True)
+    small_sum = jnp.sum(exchanged, axis=0)
+    qv_sum, upb_sum, gains_sum, biases_sum = (
+        small_sum[a : a + n] for a, n in zip(starts, sizes)
+    )
+    wide_sums = (last_sum.astype(jnp.float32), up_sum, down_sum)
+    qkv_sum = wide_sums[0][:, :wide].reshape(-1, 3, width_local).transpose(1, 0, 2)
+    return (
+        outputs,
+        input_grads,
+        qkv_sum,
+        qv_sum.reshape(qv_bias.shape),
+        wide_sums[0][:, wide:].T,
+        up_sum.astype(jnp.float32),
+        upb_sum.reshape(up_bias.shape),
+        down_sum.astype(jnp.float32).T,
+        gains_sum.reshape(norm_gains.shape),
+        biases_sum.reshape(row_biases.shape),
+    )
+
+
 def solution(mesh):
-    return jax.shard_map(
-        local,
-        mesh=mesh,
-        in_specs=(
-            P(None, ("dp", "tensor"), None),
-            P(None, "dp"),
-            P(None, "dp", "tensor"),
-            P(None, "tensor", "dp"),
-            P("tensor", "dp"),
-            P("dp", "tensor"),
-            P("tensor", "dp"),
-            P("tensor", "dp"),
-            P(None, ("dp", "tensor")),
-            P(None, ("dp", "tensor")),
-            P(None, ("dp", "tensor"), None),
-        ),
-        out_specs=(
-            P(None, ("dp", "tensor"), None),
-            P(None, ("dp", "tensor"), None),
-            P(None, "dp", "tensor"),
-            P(None, "tensor", "dp"),
-            P("tensor", "dp"),
-            P("dp", "tensor"),
-            P("tensor", "dp"),
-            P("tensor", "dp"),
-            P(None, ("dp", "tensor")),
-            P(None, ("dp", "tensor")),
-        ),
-        check_vma=False,
-    )
+    whole = ("dp", "tensor")
+    rows, vectors = P(None, whole, None), P(None, whole)
+    weights = (
+        P(None, "dp", "tensor"),
+        P(None, "tensor", "dp"),
+        P("tensor", "dp"),
+        P("dp", "tensor"),
+        P("tensor", "dp"),
+        P("tensor", "dp"),
+        vectors,
+        vectors,
+    )
+
+    def program(*arrays):
+        micro = arrays[0].shape[0]
+        fits = micro == 2 and mesh.shape["tensor"] == 2
+        return jax.shard_map(
+            sequence_parallel if fits else tensor_split,
+            mesh=mesh,
+            in_specs=(rows, P(None, "dp")) + weights + (rows,),
+            out_specs=(rows, rows) + weights,
+            check_vma=False,
+        )(*arrays)
+
+    return program

time: 1590 us -> 742 us (0.47)
  waiting for transfers between devices: 1020 us -> 488 us
  blocking collectives: 277 us -> 43.1 us
  matrix products: 174 us -> 96.9 us
  Pallas kernels: 0 us -> 28.9 us
  other arithmetic: 62.4 us -> 37.8 us
    all_gather x16 -> x1, waiting for transfers between devices: 372 us -> 111 us  [gather(): lax.all_gather(piece, everything, axis=0, tiled=True)]
    unnamed x10 -> x4, waiting for transfers between devices: 237 us -> 0.07 us
    all_gather x6 -> x1, blocking collectives: 216 us -> 43.1 us  [sequence_parallel(): small_all = lax.all_gather(small, everything, axis=0, tiled=False)]
    dot_general x36 -> x24, matrix products: 174 us -> 96.9 us  [the longest x8 34.5 us: dot_nt(): lax.dot_general(a, b, (((1,), (1,)), ((), ())), preferred_element_type=jn...]
    unnamed x1 -> x0, blocking collectives: 61.3 us -> none
    reduce_scatter x12 -> x3, waiting for transfers between devices: 403 us -> 346 us  [scatter(): return lax.psum_scatter(flat, everything, scatter_dimension=0, tiled=True)]
    ppermute x0 -> x4, waiting for transfers between devices: none -> 30.7 us  [the longest x2 30.7 us: own_rows(): received = lax.ppermute(rows[half:], 'tensor', swap)]
    pallas_call x0 -> x4, Pallas kernels: none -> 28.9 us  [the longest x2 15.5 us: attend_back_call(): pl.pallas_call(attend_back_kernel, grid=(pairs,), in_specs=[column(0), co...]
  transfers between devices with their start and end apart: 31 -> 9, of which waited for: 29 -> 6; matrix products, arithmetic and copies ran while one was open for 9% -> 13% of each run, Pallas kernels for 0% -> 2%
where the time goes in v1:
time: 742 us; the launch traced here: 738 us
  waiting for transfers between devices  488 us (66%)
  matrix products  96.9 us (13%)
  blocking collectives  43.1 us (6%)
  other arithmetic  37.8 us (5%)
  Pallas kernels  28.9 us (4%)
  local copies, waits for them, and re-layouts  20.5 us (3%)
  between operations  15 us (2%)
  starting transfers between devices  8.42 us (1%)
    reduce_scatter x3, waiting for transfers between devices, scatter(): return lax.psum_scatter(flat, everything, scatter_dimension=0, tiled=True)  346 us
    all_gather x1, waiting for transfers between devices, gather(): lax.all_gather(piece, everything, axis=0, tiled=True)  111 us
    all_gather x1, blocking collectives, sequence_parallel(): small_all = lax.all_gather(small, everything, axis=0, tiled=False)  43.1 us
    dot_general x8, matrix products, dot_nt(): lax.dot_general(a, b, (((1,), (1,)), ((), ())), preferred_element_type=jn...  34.5 us
    dot_general x8, matrix products, dot_nn(): return jnp.dot(a, b, preferred_element_type=jnp.float32)  33.2 us
    ppermute x2, waiting for transfers between devices, own_rows(): received = lax.ppermute(rows[half:], 'tensor', swap)  30.7 us
    dot_general x8, matrix products, dot_tn(): lax.dot_general(a, b, (((0,), (0,)), ((), ())), preferred_element_type=jn...  29.1 us
    pallas_call x2, Pallas kernels, attend_back_call(): pl.pallas_call(attend_back_kernel, grid=(pairs,), in_specs=[column(0), co...  15.5 us
  transfers between devices with their start and end apart: 9, of which 6 were waited for; matrix products, arithmetic and copies ran while one was open for 13% of the time, Pallas kernels for 2%

profile of v1, /device:TPU:0, one launch (start us, length us, event | category | flops | bytes accessed | tf_op | source)
XLA Modules:
  0.0 738.3 jit_solution(7651592156564131510)
XLA Ops:
  10.8 1.0 constant_dynamic-update-slice_fusion
  11.8 1.0 bitcast_dynamic-update-slice_fusion
  13.9 3.0 collective-permute-start
  18.2 43.1 %all-gather.1 = f32[32,1,384]{2,1,0:T(1,128)S(1)} all-gather(f32[1,1,384]{2,1,0:T(1,128)S(1)} %reshape.280), channel_id=2, replica_groups=mesh['dp'=16,'tensor'=2] {'tensor','dp'}, dimensions={0}, use_global_device_ids=true | all-gather | bytes 50688 | tf_op jit(solution)/shard_map/all_gather | solution.py:464
  63.4 111.0 %all-gather.4.cloned.1.call-done = bf16[2048,6144]{1,0:T(8,128)(2,1)} async-done(((bf16[64,6144]{1,0:T(8,128)(2,1)}), bf16[2048,6144]{1,0:T(8,128)(2,1)}) %all-gather.4.cloned.1.call-update) | async-done | bytes 25165840 | tf_op jit(solution)/shard_map/all_gather | solution.py:483
  174.4 3.9 fusion.20.q_ref.k_ref.v_ref
  178.3 6.8 attend.2
  185.1 2.0 fusion.32
  187.1 3.9 fusion.21.q_ref.k_ref.v_ref
  191.0 6.5 attend.3
  197.5 2.3 fusion.46
  200.6 4.9 multiply_convert_fusion.1
  205.5 5.3 fusion.15
  210.9 5.1 multiply_convert_fusion
  215.9 5.6 fusion.47
  222.9 1.7 fusion.37
  224.9 5.7 convert_reduce_fusion.1
  230.6 5.3 fusion.12
  235.9 5.3 convert_reduce_fusion
  241.3 6.0 multiply_reduce_fusion
  248.2 2.5 convolution_convert_fusion.5.grad_ref
  250.7 1.9 convolution_convert_fusion.4.grad_ref
  254.2 7.8 %attend_back.2 = (bf16[512,512]{1,0:T(8,128)(2,1)S(1)}, bf16[512,512]{1,0:T(8,128)(2,1)S(1)}, bf16[512,512]{1,0:T(8,128)(2,1)S(1)}) custom-call(bf16[512,1536]{1,0:T(8,128)(2,1)S(1)} %fusion.20.q_ref.k_ref.v_ref, bf16[512,1536]{1,0:T(8,128)(2,1)S(1)} %fusion.20.q_ref.k_ref.v_ref, bf16[512,1536]{1,0:T(8,128)(2,1)S(1)} %fusion.20.q_ref.k_ref.v_ref, ...), custom_call_target="tpu_custom_call" | custom-call | flops 2684354560 | bytes 3670016 | tf_op jit(solution)/shard_map/attend_back/pallas_call | solution.py:375
  262.0 7.8 %attend_back.3 = (bf16[512,512]{1,0:T(8,128)(2,1)S(1)}, bf16[512,512]{1,0:T(8,128)(2,1)S(1)}, bf16[512,512]{1,0:T(8,128)(2,1)S(1)}) custom-call(bf16[512,1536]{1,0:T(8,128)(2,1)S(1)} %fusion.21.q_ref.k_ref.v_ref, bf16[512,1536]{1,0:T(8,128)(2,1)S(1)} %fusion.21.q_ref.k_ref.v_ref, bf16[512,1536]{1,0:T(8,128)(2,1)S(1)} %fusion.21.q_ref.k_ref.v_ref, ...), custom_call_target="tpu_custom_call" | custom-call | flops 2684354560 | bytes 3670016 | tf_op jit(solution)/shard_map/attend_back/pallas_call | solution.py:375
  270.9 3.2 convolution_convert_fusion.1
  274.2 2.9 convolution_convert_fusion
  277.1 3.8 maximum_bitcast_fusion
  280.8 7.4 %pad_maximum_fusion = bf16[2,1024,2048]{2,1,0:T(8,128)(2,1)} fusion(bf16[1,1024,2048]{2,1,0:T(8,128)(2,1)} %get-tuple-element.135, bf16[1,1024,2048]{2,1,0:T(8,128)(2,1)} %get-tuple-element.134), kind=kLoop, calls=%fused_computation | loop fusion | flops 4194304 | bytes 16777216 | tf_op jit(solution)/shard_map/stack | solution.py:564
  288.6 6.4 convert_bitcast_fusion.2
  295.0 4.3 convert_bitcast_fusion.3
  299.3 7.6 %pad_maximum_fusion.1 = bf16[2,1024,2048]{2,1,0:T(8,128)(2,1)} fusion(bf16[1,1024,2048]{2,1,0:T(8,128)(2,1)} %convert_bitcast_fusion.2, bf16[1,1024,2048]{2,1,0:T(8,128)(2,1)} %convert_bitcast_fusion.3), kind=kLoop, calls=%fused_computation.1 | loop fusion | flops 4194304 | bytes 16777216 | tf_op jit(solution)/shard_map/stack | solution.py:544
  307.0 6.5 convert_bitcast_fusion
  313.5 4.4 convert_bitcast_fusion.1
  317.8 7.6 %pad_maximum_fusion.2 = bf16[2,1024,2048]{2,1,0:T(8,128)(2,1)} fusion(bf16[1,1024,2048]{2,1,0:T(8,128)(2,1)} %convert_bitcast_fusion, bf16[1,1024,2048]{2,1,0:T(8,128)(2,1)} %convert_bitcast_fusion.1), kind=kLoop, calls=%fused_computation.2 | loop fusion | flops 4194304 | bytes 16777216 | tf_op jit(solution)/shard_map/stack | solution.py:540
  328.6 3.0 all-to-all-start
  331.6 4.3 fusion.25
  335.9 3.8 add_convert_fusion
  340.5 1.8 collective-permute-start.3
  346.2 14.0 %collective-permute-done.3 = bf16[256,1024]{1,0:T(8,128)(2,1)S(1)} collective-permute-done((bf16[256,1024]{1,0:T(8,128)(2,1)}, bf16[256,1024]{1,0:T(8,128)(2,1)S(1)}, u32[]{:S(2)}, u32[]{:S(2)}) %collective-permute-start.3) | collective-permute-done | bytes 524320 | tf_op jit(solution)/shard_map/ppermute | solution.py:446
  360.1 16.7 %collective-permute-done.1 = bf16[256,1024]{1,0:T(8,128)(2,1)S(1)} collective-permute-done((bf16[256,1024]{1,0:T(8,128)(2,1)}, bf16[256,1024]{1,0:T(8,128)(2,1)S(1)}, u32[]{:S(2)}, u32[]{:S(2)}) %collective-permute-start.1) | collective-permute-done | bytes 524320 | tf_op jit(solution)/shard_map/ppermute | solution.py:446
  377.0 1.1 pad_maximum_fusion.4
  378.0 1.1 pad_maximum_fusion.6
  379.1 56.4 %reduce-scatter.4.cloned.1.call-done = bf16[64,2048]{1,0:T(8,128)(2,1)} async-done(((bf16[2048,2048]{1,0:T(8,128)(2,1)}), bf16[64,2048]{1,0:T(8,128)(2,1)}) %reduce-scatter.4.cloned.1.call-update) | async-done | bytes 262160 | tf_op jit(solution)/shard_map/reduce_scatter | solution.py:489
  435.5 1.0 slice.242
  437.8 144.9 %reduce-scatter.6.cloned.1.call-done = bf16[64,2048]{1,0:T(8,128)(2,1)} async-done(((bf16[2048,2048]{1,0:T(8,128)(2,1)}), bf16[64,2048]{1,0:T(8,128)(2,1)}) %reduce-scatter.6.cloned.1.call-update) | async-done | bytes 262160 | tf_op jit(solution)/shard_map/reduce_scatter | solution.py:489
  582.7 1.8 convert_element_type.124
  585.1 144.7 %reduce-scatter.8.cloned.1.call-done = bf16[64,2048]{1,0:T(8,128)(2,1)} async-done(((bf16[2048,2048]{1,0:T(8,128)(2,1)}), bf16[64,2048]{1,0:T(8,128)(2,1)}) %reduce-scatter.8.cloned.1.call-update) | async-done | bytes 262160 | tf_op jit(solution)/shard_map/reduce_scatter | solution.py:489
  729.8 1.8 convert_bitcast_fusion.4
  (174 shorter events, 23.7 us)
Async XLA Ops:
  7.2 6.5 copy-start.10
  7.2 167.2 %all-gather.4.cloned.1.call-start = ((), (), s32[]{:S(2)}) async-start(), calls=%async_computation.4 | async-start | bytes 25952256 | tf_op jit(solution)/shard_map/all_gather | solution.py:483
  9.0 7.9 %copy-start.11 = (bf16[2,256,1024]{2,1,0:T(8,128)(2,1)S(1)}, bf16[2,256,1024]{2,1,0:T(8,128)(2,1)}, u32[]{:S(2)}) copy-start(bf16[2,256,1024]{2,1,0:T(8,128)(2,1)} %param.21) | copy-start | bytes 3145732
  12.7 0.9 copy-start.12
  13.6 421.9 %reduce-scatter.4.cloned.1.call-start = ((), (), s32[]{:S(2)}) async-start(), calls=%async_computation.5 | async-start | bytes 8650752 | tf_op jit(solution)/shard_map/reduce_scatter | solution.py:489
  13.7 4.1 copy-start.18
  13.7 4.2 copy-start.19
  13.7 4.2 copy-start.17
  13.7 4.4 copy-start.20
  13.8 183.7 %copy-start.2 = (bf16[256,1024]{1,0:T(8,128)(2,1)}, bf16[256,1024]{1,0:T(8,128)(2,1)S(1)}, u32[]{:S(2)}) copy-start(bf16[256,1024]{1,0:T(8,128)(2,1)S(1)} %get-tuple-element.89) | copy-start | bytes 1572868
  13.8 48.4 %copy-start.16 = (s32[2,512]{1,0:T(2,128)S(1)}, s32[2,512]{1,0:T(2,128)}, u32[]{:S(2)}) copy-start(s32[2,512]{1,0:T(2,128)} %param.12) | copy-start | bytes 12292
  13.9 49.5 %collective-permute-start = (bf16[256,1024]{1,0:T(8,128)(2,1)S(1)}, bf16[256,1024]{1,0:T(8,128)(2,1)}, u32[]{:S(2)}, u32[]{:S(2)}) collective-permute-start(bf16[256,1024]{1,0:T(8,128)(2,1)S(1)} %get-tuple-element.90), channel_id=1, source_target_pairs={{0,1},{1,0},{2,3},{3,2},{4,5},{5,4},{6,7},{7,6},{8,9},{9,8},{10,11... | collective-permute-start | bytes 1572872 | tf_op jit(solution)/shard_map/ppermute | solution.py:443
  17.8 204.2 %collective-permute-start.2 = (bf16[256,1024]{1,0:T(8,128)(2,1)}, bf16[256,1024]{1,0:T(8,128)(2,1)S(1)}, u32[]{:S(2)}, u32[]{:S(2)}) collective-permute-start(bf16[256,1024]{1,0:T(8,128)(2,1)} %get-tuple-element.88), channel_id=1, source_target_pairs={{0,1},{1,0},{2,3},{3,2},{4,5},{5,4},{6,7},{7,6},{8,9},{9,8},{10,11... | collective-permute-start | bytes 1572872 | tf_op jit(solution)/shard_map/ppermute | solution.py:443
  200.6 10.3 %copy-start.8 = (bf16[512,1024]{1,0:T(8,128)(2,1)}, bf16[512,1024]{1,0:T(8,128)(2,1)S(1)}, u32[]{:S(2)}) copy-start(bf16[512,1024]{1,0:T(8,128)(2,1)S(1)} %fusion.31) | copy-start | bytes 3145732
  205.5 5.3 copy-start.21
  215.9 5.6 copy-start.23
  221.9 1.0 copy-start.4
  224.9 11.1 %copy-start.6 = (bf16[512,1024]{1,0:T(8,128)(2,1)}, bf16[512,1024]{1,0:T(8,128)(2,1)S(1)}, u32[]{:S(2)}) copy-start(bf16[512,1024]{1,0:T(8,128)(2,1)S(1)} %convert_element_type.104) | copy-start | bytes 3145732
  230.6 5.3 copy-start.24
  241.3 6.0 copy-start.26
  248.0 2.7 copy-start
  269.8 1.1 copy-start.3
  269.9 4.3 copy-start.13
  270.9 3.2 copy-start.14
  288.3 294.4 %reduce-scatter.6.cloned.1.call-start = ((), (), s32[]{:S(2)}) async-start(), calls=%async_computation.6 | async-start | bytes 8650752 | tf_op jit(solution)/shard_map/reduce_scatter | solution.py:489
  288.6 6.4 copy-start.9
  288.6 6.4 copy-start.25
  306.9 422.9 %reduce-scatter.8.cloned.1.call-start = ((), (), s32[]{:S(2)}) async-start(), calls=%async_computation.7 | async-start | bytes 8650752 | tf_op jit(solution)/shard_map/reduce_scatter | solution.py:489
  307.0 6.5 copy-start.7
  307.0 6.5 copy-start.22
  328.6 14.8 %all-to-all-start = ((f32[32,1,384]{2,1,0:T(1,128)}), f32[32,1,384]{2,1,0:T(1,128)S(1)}, u32[]{:S(2)}, u32[]{:S(2)}) async-start(f32[32,1,384]{2,1,0:T(1,128)} %copy.72), calls=%async_computation.1 | async-start | bytes 98304 | tf_op jit(solution)/shard_map/all_to_all | solution.py:581
  331.5 4.4 copy-start.1
  331.5 4.4 copy-start.15
  340.5 19.6 %collective-permute-start.3 = (bf16[256,1024]{1,0:T(8,128)(2,1)}, bf16[256,1024]{1,0:T(8,128)(2,1)S(1)}, u32[]{:S(2)}, u32[]{:S(2)}) collective-permute-start(bf16[256,1024]{1,0:T(8,128)(2,1)} %slice.241), channel_id=1, source_target_pairs={{0,1},{1,0},{2,3},{3,2},{4,5},{5,4},{6,7},{7,6},{8,9},{9,8},{10,11... | collective-permute-start | bytes 1572872 | tf_op jit(solution)/shard_map/ppermute | solution.py:446
  343.2 33.6 %collective-permute-start.1 = (bf16[256,1024]{1,0:T(8,128)(2,1)}, bf16[256,1024]{1,0:T(8,128)(2,1)S(1)}, u32[]{:S(2)}, u32[]{:S(2)}) collective-permute-start(bf16[256,1024]{1,0:T(8,128)(2,1)} %slice.239), channel_id=1, source_target_pairs={{0,1},{1,0},{2,3},{3,2},{4,5},{5,4},{6,7},{7,6},{8,9},{9,8},{10,11... | collective-permute-start | bytes 1572872 | tf_op jit(solution)/shard_map/ppermute | solution.py:446
  435.5 2.2 copy-start.5
Sparse Core Ops, SparseCore 0:
  13.8 160.6 all-gather.3
  288.4 147.0 reduce-scatter.3
  437.8 144.7 reduce-scatter.5
  584.8 144.8 reduce-scatter.7

commit v2 on v1

--- a/solution.py
+++ b/solution.py
@@ -1,8 +1,11 @@
+import functools
+
 import jax
 import jax.numpy as jnp
 from jax import lax
 from jax.experimental import pallas as pl
 from jax.experimental.pallas import tpu as pltpu
+from jax.sharding import Mesh
 from jax.sharding import PartitionSpec as P
 
 HEAD_DIM = 64
@@ -297,12 +300,12 @@
 
 
 def attend_back_kernel(
-    q_ref, k_ref, v_ref, grad_ref, row_ref, col_ref, stats_ref, dq_ref, dk_ref, dv_ref
+    q_ref, k_ref, v_ref, grad_ref, row_ref, col_ref, stats_ref, d_ref
 ):
     query, keys, values, grad = q_ref[...], k_ref[...], v_ref[...], grad_ref[...]
     scale = jnp.asarray(HEAD_DIM**-0.5, query.dtype)
     keep = col_ref[...] == row_ref[...]
-    zero = jnp.zeros(dq_ref.shape, jnp.float32)
+    zero = jnp.zeros(query.shape, jnp.float32)
     grad_query, grad_keys, grad_values = zero, zero, zero
     for half in range(2):
         own = half_mask(query.shape, half)
@@ -329,9 +332,10 @@
         grad_query += lax.dot_general(
             grad_scores, own_keys, (((0,), (0,)), ((), ())), preferred_element_type=jnp.float32
         )
-    dq_ref[...] = grad_query.astype(dq_ref.dtype)
-    dk_ref[...] = grad_keys.astype(dk_ref.dtype)
-    dv_ref[...] = grad_values.astype(dv_ref.dtype)
+    pair, width = pl.program_id(0), d_ref.shape[1] // 3
+    for place, value in enumerate((grad_query, grad_keys, grad_values)):
+        start = pl.multiple_of(place * width + pair * LANES, LANES)
+        d_ref[:, pl.ds(start, LANES)] = value.astype(d_ref.dtype)
 
 
 def attention_specs(rows, pairs):
@@ -371,7 +375,7 @@
     rows, width = grad.shape
     pairs = width // LANES
     column, row_ids, column_ids, stats = attention_specs(rows, pairs)
-    shape = jax.ShapeDtypeStruct((rows, width), jnp.bfloat16)
+    whole = pl.BlockSpec((rows, 3 * width), lambda i: (0, 0))
     return pl.pallas_call(
         attend_back_kernel,
         grid=(pairs,),
@@ -384,8 +388,8 @@
             column_ids,
             stats,
         ],
-        out_specs=[column(0)] * 3,
-        out_shape=[shape] * 3,
+        out_specs=whole,
+        out_shape=jax.ShapeDtypeStruct((rows, 3 * width), jnp.bfloat16),
         compiler_params=pltpu.CompilerParams(vmem_limit_bytes=48 * 1024 * 1024),
         cost_estimate=pl.CostEstimate(
             flops=20 * pairs * rows * rows * LANES,
@@ -412,6 +416,140 @@
     cdf = 0.5 * (1.0 + lax.erf(values * (0.5**0.5)))
     density = jnp.exp(-0.5 * values * values) * (0.5 / jnp.pi) ** 0.5
     return values * cdf, cdf + values * density
+
+
+VMEM_BYTES = 56 * 1024 * 1024
+
+
+def gradient_kernel(row_ref, part_ref, *refs, blocks, pairs, added):
+    lefts, rights = refs[:pairs], refs[pairs : 3 * pairs]
+    received = refs[3 * pairs : 3 * pairs + added]
+    outs = refs[3 * pairs + added :]
+    step = pl.program_id(0)
+    size = outs[0].shape[0]
+    start = pl.multiple_of(row_ref[step] * size, size)
+
+    def products(part):
+        pieces = [
+            dot_tn(lefts[i][:, pl.ds(start, size)], rights[2 * i + part][...])
+            for i in range(pairs)
+        ]
+        total = pieces[0] if pairs == 1 else jnp.concatenate(pieces, axis=1)
+        if added:
+            total = total + received[0][...].astype(jnp.float32)
+        total = total.astype(jnp.bfloat16)
+        if len(outs) == 1:
+            outs[0][...] = total
+        else:
+            for out, (low, high) in zip(outs, blocks):
+                @pl.when((step >= low) & (step < high))
+                def _(out=out):
+                    out[...] = total
+
+    for part in range(2):
+        pl.when(part_ref[step] == part)(functools.partial(products, part))
+
+
+def gradient_blocks(rows, parts, lefts, rights, received=None):
+    count = rows.shape[0]
+    size = lefts[0].shape[1] // count
+    width = sum(pair[0].shape[1] for pair in rights)
+    flat = [item for pair in rights for item in pair]
+    spans = ((0, 2), (2, 3), (3, 4))
+    whole = [
+        pl.BlockSpec(item.shape, lambda i, *_: (0, 0), pipeline_mode=pl.Buffered(1))
+        for item in list(lefts) + flat
+    ]
+    block = pl.BlockSpec((size, width), lambda i, *_: (i, 0))
+    in_specs, operands = whole, list(lefts) + flat
+    if received is None:
+        out_shape = [jax.ShapeDtypeStruct((count * size, width), jnp.bfloat16)]
+        out_specs = [block]
+    else:
+        in_specs, operands = whole + [block], operands + [received]
+        out_shape = [
+            jax.ShapeDtypeStruct(((high - low) * size, width), jnp.bfloat16)
+            for low, high in spans
+        ]
+        out_specs = [
+            pl.BlockSpec(
+                (size, width),
+                lambda i, *_, low=low, high=high: (jnp.clip(i, low, high - 1) - low, 0),
+            )
+            for low, high in spans
+        ]
+    return pl.pallas_call(
+        functools.partial(
+            gradient_kernel,
+            blocks=spans,
+            pairs=len(lefts),
+            added=0 if received is None else 1,
+        ),
+        grid_spec=pltpu.PrefetchScalarGridSpec(
+            num_scalar_prefetch=2,
+            grid=(count,),
+            in_specs=in_specs,
+            out_specs=out_specs,
+        ),
+        out_shape=out_shape,
+        compiler_params=pltpu.CompilerParams(vmem_limit_bytes=VMEM_BYTES),
+        cost_estimate=pl.CostEstimate(
+            flops=2 * count * size * lefts[0].shape[0] * width,
+            bytes_accessed=6 * count * size * width,
+            transcendentals=0,
+        ),
+        name="gradient_blocks",
+    )(rows, parts, *operands)
+
+
+def permutes():
+    def index(x, c, y):
+        return (x * 2 + c) * 2 + y
+
+    cells = [(x, y) for x in range(2) for y in range(2)]
+    along = [(index(x, 0, y), index(1 - x, 0, y)) for x, y in cells]
+    along += [(index(x, 1, y), index(x, 1, 1 - y)) for x, y in cells]
+    cross = [(index(x, 0, y), index(1 - x, 1, y)) for x, y in cells]
+    cross += [(index(x, 1, y), index(x, 0, 1 - y)) for x, y in cells]
+    return along, cross
+
+
+PLANE = ("x", "c", "y")
+EVERY = ("y", "x", "c", "z")
+SWAP = [(0, 1), (1, 0)]
+
+
+def block_tables(x, c, y):
+    def kept(core):
+        first = jnp.stack([2 - 2 * x, 3 - 2 * x, 2 - 2 * x, 2 * x])
+        second = jnp.stack([2 * x, 2 * x + 1, 3 - 2 * x, 2 * x + 1])
+        parts_first = jnp.stack([y, y, 1 - y, y])
+        parts_second = jnp.stack([1 - y, 1 - y, 1 - y, y])
+        return jnp.where(core == 0, first, second), jnp.where(
+            core == 0, parts_first, parts_second
+        )
+
+    return kept(c), kept(1 - c)
+
+
+def reduce_gradient(lefts, rights, tables, core):
+    own, other = tables
+    sent = gradient_blocks(*other, lefts, rights)[0]
+    received = lax.ppermute(sent, "c", SWAP)
+    main, diagonal, home = gradient_blocks(*own, lefts, rights, received)
+    along, cross = permutes()
+    arrived = lax.ppermute(diagonal, PLANE, cross)
+    size, width = diagonal.shape
+    halves = main.reshape(2, size, width)
+    aimed = lax.broadcasted_iota(jnp.int32, (2, 1, 1), 0) == 1 - core
+    halves = jnp.where(
+        aimed, (halves.astype(jnp.float32) + arrived.astype(jnp.float32)).astype(main.dtype), halves
+    )
+    landed = lax.ppermute(halves, PLANE, along)
+    passed = lax.ppermute(lax.dynamic_index_in_dim(landed, 1 - core, 0, False), "c", SWAP)
+    kept = lax.dynamic_index_in_dim(landed, core, 0, False)
+    total = home.astype(jnp.float32) + kept.astype(jnp.float32) + passed.astype(jnp.float32)
+    return lax.psum_scatter(total.astype(jnp.bfloat16), "z", scatter_dimension=0, tiled=True)
 
 
 def sequence_parallel(
@@ -428,65 +566,34 @@
     cotangent,
 ):
     low = jnp.bfloat16
-    parts = lax.axis_size("tensor")
-    dp_count = lax.axis_size("dp")
-    mine = lax.axis_index("tensor")
-    swap = [(i, (i + 1) % parts) for i in range(parts)]
-    half = layer_input.shape[1]
-    width = layer_input.shape[2]
+    parts = lax.axis_size("y")
+    grid = tuple(lax.axis_size(name) for name in ("x", "c", "z"))
+    dp_count = grid[0] * grid[1] * grid[2]
+    mine = lax.axis_index("y")
+    core = lax.axis_index("c")
+    tables = block_tables(lax.axis_index("x"), core, mine)
+    half, width = layer_input.shape[1:]
     heads_local = qv_bias.shape[1]
     width_local = heads_local * HEAD_DIM
+    span = range(parts)
+
+    source = jnp.arange(width).reshape(grid[2], grid[0], grid[1], -1)
+    source = source.transpose(1, 2, 0, 3).reshape(-1)
+    chosen = lax.broadcasted_iota(jnp.int32, (width, width), 0) == source[None, :]
+    order = chosen.astype(low)
 
     def own_sequence(rows):
         kept = lax.dynamic_index_in_dim(rows, mine, 0, keepdims=False)
         sent = lax.dynamic_index_in_dim(rows, 1 - mine, 0, keepdims=False)
-        return jnp.concatenate([kept, lax.ppermute(sent, "tensor", swap)], axis=0)
+        rows = jnp.concatenate([kept, lax.ppermute(sent, "y", SWAP)], axis=0)
+        return dot_nn(rows, order).astype(low)
 
     def own_rows(rows):
-        received = lax.ppermute(rows[half:], "tensor", swap)
+        rows = dot_nt(rows.astype(low), order).astype(low)
+        received = lax.ppermute(rows[half:], "y", SWAP)
         first = jnp.where(mine == 0, rows[:half], received)
         second = jnp.where(mine == 0, received, rows[:half])
         return jnp.stack([first, second])
-
-    everything = ("tensor", "dp")
-    rows_in = own_sequence(layer_input)
-    segments = lax.dynamic_index_in_dim(segment_ids, mine, 0, keepdims=False)
-    segments = jnp.where(mine == 0, segments, jnp.roll(segments, -half))
-
-    small = jnp.concatenate(
-        [
-            qv_bias.astype(jnp.float32).reshape(-1),
-            up_bias.astype(jnp.float32).reshape(-1),
-            norm_gains.reshape(-1),
-            row_biases.reshape(-1),
-        ]
-    )
-    small_all = lax.all_gather(small, everything, axis=0, tiled=False)
-    small_all = small_all.reshape(parts, dp_count, small.shape[0])
-    sizes = [qv_bias.size, up_bias.size, norm_gains.size, row_biases.size]
-    starts = [0, sizes[0], sum(sizes[:2]), sum(sizes[:3])]
-    qv_all, upb_all, gains_all, biases_all = (
-        small_all[:, :, a : a + n] for a, n in zip(starts, sizes)
-    )
-    qv_all = qv_all.reshape((parts, dp_count) + qv_bias.shape).transpose(2, 0, 3, 1, 4)
-    qv_all = qv_all.reshape(2, parts, width_local)
-    upb_all = upb_all.reshape(parts, -1)
-
-    def whole_rows(values, shard):
-        values = values.reshape((parts, dp_count) + shard.shape).transpose(2, 1, 0, 3)
-        return values.reshape(shard.shape[0], width)
-
-    gains_all = whole_rows(gains_all, norm_gains)
-    biases_all = whole_rows(biases_all, row_biases)
-
-    def gather(piece):
-        return lax.all_gather(piece, everything, axis=0, tiled=True).reshape(
-            parts, width, piece.shape[1]
-        )
-
-    def scatter(blocks):
-        flat = blocks.reshape(parts * width, blocks.shape[2])
-        return lax.psum_scatter(flat, everything, scatter_dimension=0, tiled=True)
 
     packed = jnp.concatenate(
         [
@@ -499,14 +606,44 @@
         ],
         axis=1,
     )
-    gathered = gather(packed)
+    gathered = lax.all_gather(packed, EVERY, axis=0, tiled=True).reshape(parts, width, -1)
     wide = 3 * width_local
     edges = [wide, wide + width_local, wide + width_local + up_weight.shape[1]]
     qkv_full = gathered[:, :, : edges[0]]
     out_full = gathered[:, :, edges[0] : edges[1]]
     up_full = gathered[:, :, edges[1] : edges[2]]
     down_full = gathered[:, :, edges[2] :]
-    span = range(parts)
+
+    rows_in = own_sequence(layer_input)
+    segments = lax.dynamic_index_in_dim(segment_ids, mine, 0, keepdims=False)
+    segments = jnp.where(mine == 0, segments, jnp.roll(segments, -half))
+
+    small = jnp.concatenate(
+        [
+            qv_bias.astype(jnp.float32).reshape(-1),
+            up_bias.astype(jnp.float32).reshape(-1),
+            norm_gains.reshape(-1),
+            row_biases.reshape(-1),
+        ]
+    )
+    copies = jnp.broadcast_to(small[None], (parts * dp_count, small.shape[0]))
+    small_all = lax.all_to_all(copies, EVERY, 0, 0, tiled=True)
+    small_all = small_all.reshape((parts,) + grid + (small.shape[0],))
+    sizes = [qv_bias.size, up_bias.size, norm_gains.size, row_biases.size]
+    starts = [0, sizes[0], sum(sizes[:2]), sum(sizes[:3])]
+
+    def section(i, shard):
+        values = small_all[..., starts[i] : starts[i] + sizes[i]]
+        return values.reshape((parts,) + grid + shard.shape)
+
+    qv_all = section(0, qv_bias).transpose(4, 0, 5, 3, 1, 2, 6).reshape(2, parts, width_local)
+    upb_all = section(1, up_bias).transpose(0, 3, 1, 2, 4, 5).reshape(parts, -1)
+
+    def whole_rows(i, shard):
+        values = section(i, shard).transpose(4, 1, 2, 3, 0, 5)
+        return values.reshape(shard.shape[0], width)
+
+    gains_all, biases_all = whole_rows(2, norm_gains), whole_rows(3, row_biases)
 
     rows_wide = rows_in.astype(jnp.float32)
     none = jnp.zeros((width_local,), jnp.float32)
@@ -529,7 +666,6 @@
     branch = sum(dot_nt(activated[t], down_full[t]) for t in span)
     residual_two = hidden + branch + biases_all[2]
     result, normed_two, inverse_two = normalize(residual_two, gains_all[1], biases_all[3])
-    outputs = own_rows(result.astype(low))
 
     grad_output = own_sequence(cotangent).astype(jnp.float32)
     gain_two_grad = jnp.sum(grad_output * normed_two, axis=0)
@@ -537,60 +673,63 @@
     grad_two = norm_back(grad_output, normed_two, inverse_two, gains_all[1])
     down_bias_grad = jnp.sum(grad_two, axis=0)
     branch_grad = grad_two.astype(low)
-    down_grad = jnp.stack([dot_tn(branch_grad, activated[t]).astype(low) for t in span])
-    down_sum = scatter(down_grad)
+    down_sum = reduce_gradient([branch_grad], [activated], tables, core)
+    outputs = own_rows(result)
     grad_upper = [(dot_nn(branch_grad, down_full[t]) * slopes[t]).astype(low) for t in span]
     upb_grad = jnp.stack([jnp.sum(grad_upper[t].astype(jnp.float32), axis=0) for t in span])
-    up_grad = jnp.stack([dot_tn(hidden_low, grad_upper[t]).astype(low) for t in span])
-    up_sum = scatter(up_grad)
+    up_sum = reduce_gradient([hidden_low], [grad_upper], tables, core)
     grad_hidden = grad_two + sum(dot_nt(grad_upper[t], up_full[t]) for t in span)
     gain_one_grad = jnp.sum(grad_hidden * normed_one, axis=0)
     shift_one_grad = jnp.sum(grad_hidden, axis=0)
     grad_one = norm_back(grad_hidden, normed_one, inverse_one, gains_all[0])
     out_bias_grad = jnp.sum(grad_one, axis=0)
     attention_grad = grad_one.astype(low)
-    last, qv_grads, input_grad = [], [], grad_one
+    grad_projected, qv_grads, input_grad = [], [], grad_one
     for t in span:
-        out_grad = dot_tn(attention_grad, contexts[t]).astype(low)
         grad_context = dot_nn(attention_grad, out_full[t]).astype(low)
-        triple = attend_back_call(projected[t], grad_context, segments, stats[t])
-        grad_qkv = jnp.concatenate(triple, axis=1)
-        qv_grads.append(
-            jnp.stack([jnp.sum(triple[j].astype(jnp.float32), axis=0) for j in (0, 2)])
-        )
-        qkv_grad = dot_tn(rows_in, grad_qkv).astype(low)
-        last.append(jnp.concatenate([qkv_grad, out_grad], axis=1))
-        input_grad = input_grad + dot_nt(grad_qkv, qkv_full[t])
-    last_sum = scatter(jnp.stack(last))
-    input_grads = own_rows(input_grad.astype(low))
-
-    qv_grads = jnp.stack(qv_grads).reshape(parts, 2, heads_local, dp_count, -1)
-    qv_grads = qv_grads.transpose(0, 3, 1, 2, 4).reshape(parts, dp_count, -1)
-    upb_grad = upb_grad.reshape(parts, dp_count, -1)
+        grad_projected.append(attend_back_call(projected[t], grad_context, segments, stats[t]))
+        sums = jnp.sum(grad_projected[t].astype(jnp.float32), axis=0).reshape(3, width_local)
+        qv_grads.append(jnp.stack([sums[0], sums[2]]))
+    last_sum = reduce_gradient(
+        [rows_in, attention_grad], [grad_projected, contexts], tables, core
+    )
+    for t in span:
+        input_grad = input_grad + dot_nt(grad_projected[t], qkv_full[t])
+    input_grads = own_rows(input_grad)
+
+    dp_order = (grid[2], grid[0], grid[1])
+    qv_grads = jnp.stack(qv_grads).reshape((parts, 2, heads_local) + dp_order + (-1,))
+    qv_grads = qv_grads.transpose(0, 4, 5, 3, 1, 2, 6).reshape(parts * dp_count, -1)
+    upb_grad = upb_grad.reshape((parts,) + dp_order + (-1,))
+    upb_grad = upb_grad.transpose(0, 2, 3, 1, 4).reshape(parts * dp_count, -1)
 
     def split_rows(rows):
-        rows = rows.reshape(rows.shape[0], dp_count, parts, -1).transpose(2, 1, 0, 3)
-        return rows.reshape(parts, dp_count, -1)
-
-    gains_grad = jnp.stack([gain_one_grad, gain_two_grad])
-    biases_grad = jnp.stack([out_bias_grad, shift_one_grad, down_bias_grad, shift_two_grad])
+        count = len(rows)
+        rows = jnp.stack(rows).reshape((count,) + grid + (parts, -1))
+        return rows.transpose(4, 1, 2, 3, 0, 5).reshape(parts * dp_count, -1)
+
     small_grad = jnp.concatenate(
-        [qv_grads, upb_grad, split_rows(gains_grad), split_rows(biases_grad)], axis=2
-    )
-    small_grad = small_grad.reshape(parts * dp_count, -1)
-    exchanged = lax.all_to_all(small_grad, everything, 0, 0, tiled=True)
+        [
+            qv_grads,
+            upb_grad,
+            split_rows([gain_one_grad, gain_two_grad]),
+            split_rows([out_bias_grad, shift_one_grad, down_bias_grad, shift_two_grad]),
+        ],
+        axis=1,
+    )
+    exchanged = lax.all_to_all(small_grad, EVERY, 0, 0, tiled=True)
     small_sum = jnp.sum(exchanged, axis=0)
     qv_sum, upb_sum, gains_sum, biases_sum = (
         small_sum[a : a + n] for a, n in zip(starts, sizes)
     )
-    wide_sums = (last_sum.astype(jnp.float32), up_sum, down_sum)
-    qkv_sum = wide_sums[0][:, :wide].reshape(-1, 3, width_local).transpose(1, 0, 2)
+    last_sum = last_sum.astype(jnp.float32)
+    qkv_sum = last_sum[:, :wide].reshape(-1, 3, width_local).transpose(1, 0, 2)
     return (
         outputs,
         input_grads,
         qkv_sum,
         qv_sum.reshape(qv_bias.shape),
-        wide_sums[0][:, wide:].T,
+        last_sum[:, wide:].T,
         up_sum.astype(jnp.float32),
         upb_sum.reshape(up_bias.shape),
         down_sum.astype(jnp.float32).T,
@@ -600,26 +739,34 @@
 
 
 def solution(mesh):
-    whole = ("dp", "tensor")
-    rows, vectors = P(None, whole, None), P(None, whole)
-    weights = (
-        P(None, "dp", "tensor"),
-        P(None, "tensor", "dp"),
-        P("tensor", "dp"),
-        P("dp", "tensor"),
-        P("tensor", "dp"),
-        P("tensor", "dp"),
-        vectors,
-        vectors,
-    )
+    groups = mesh.shape["dp"]
+    parts = mesh.shape["tensor"]
 
     def program(*arrays):
-        micro = arrays[0].shape[0]
-        fits = micro == 2 and mesh.shape["tensor"] == 2
+        micro, width = arrays[0].shape[0], arrays[0].shape[2]
+        fits = micro == 2 and parts == 2 and groups % 4 == 0 and width % (groups * 16) == 0
+        if fits:
+            dp, place = ("z", "x", "c"), "y"
+            shape = (groups // 4, 2, 2, 2)
+            used = Mesh(mesh.devices.reshape(shape), dp + (place,))
+        else:
+            dp, place, used = ("dp",), "tensor", mesh
+        whole = dp + (place,)
+        rows, vectors = P(None, whole, None), P(None, whole)
+        weights = (
+            P(None, dp, place),
+            P(None, place, dp),
+            P(place, dp),
+            P(dp, place),
+            P(place, dp),
+            P(place, dp),
+            vectors,
+            vectors,
+        )
         return jax.shard_map(
             sequence_parallel if fits else tensor_split,
-            mesh=mesh,
-            in_specs=(rows, P(None, "dp")) + weights + (rows,),
+            mesh=used,
+            in_specs=(rows, P(None, dp)) + weights + (rows,),
             out_specs=(rows, rows) + weights,
             check_vma=False,
         )(*arrays)

time: 742 us -> 480 us (0.65)
  waiting for transfers between devices: 488 us -> 213 us
  Pallas kernels: 28.9 us -> 80.5 us
  blocking collectives: 43.1 us -> 0 us
  starting transfers between devices: 8.42 us -> 28.4 us
  matrix products: 96.9 us -> 80.7 us
  other arithmetic: 37.8 us -> 26.8 us
  local copies, waits for them, and re-layouts: 20.5 us -> 31 us
    reduce_scatter x3, waiting for transfers between devices: 346 us -> 0.3 us  [reduce_gradient(): lax.psum_scatter(total.astype(jnp.bfloat16), 'z', scatter_dimension=0, ti...]
    ppermute x4 -> x16, waiting for transfers between devices: 30.7 us -> 82.6 us  [the longest x3 45.5 us: reduce_gradient(): landed = lax.ppermute(halves, PLANE, along)]
    pallas_call x0 -> x6, Pallas kernels: none -> 51.6 us  [gradient_blocks(): pl.pallas_call(functools.partial(gradient_kernel, blocks=spans, pairs=len...]
    all_gather x1 -> x0, blocking collectives: 43.1 us -> none  [sequence_parallel(): small_all = lax.all_gather(small, everything, axis=0, tiled=False)]
    dot_general x8 -> x0, matrix products: 29.1 us -> none  [dot_tn(): lax.dot_general(a, b, (((0,), (0,)), ((), ())), preferred_element_type=jn...]
    another operation x5 -> x0, other arithmetic: 26.4 us -> none  [the longest x2 11.2 us: sequence_parallel(): last_sum = scatter(jnp.stack(last))]
    all_gather x1, waiting for transfers between devices: 111 us -> 128 us  [sequence_parallel(): lax.all_gather(packed, EVERY, axis=0, tiled=True).reshape(parts, width, -1)]
    ppermute x4 -> x16, starting transfers between devices: 5.09 us -> 17.9 us  [the longest x3 5.1 us: reduce_gradient(): lax.ppermute(lax.dynamic_index_in_dim(landed, 1 - core, 0, False), 'c', S...]
  transfers between devices with their start and end apart: 9 -> 22, of which waited for: 6 -> 11; matrix products, arithmetic and copies ran while one was open for 13% -> 19% of each run, Pallas kernels for 2% -> 14%
where the time goes in v2:
time: 480 us; the launch traced here: 475 us
  waiting for transfers between devices  213 us (44%)
  matrix products  80.7 us (17%)
  Pallas kernels  80.5 us (17%)
  local copies, waits for them, and re-layouts  31 us (6%)
  starting transfers between devices  28.4 us (6%)
  other arithmetic  26.8 us (6%)
  between operations  15 us (3%)
    all_gather x1, waiting for transfers between devices, sequence_parallel(): lax.all_gather(packed, EVERY, axis=0, tiled=True).reshape(parts, width, -1)  128 us
    pallas_call x6, Pallas kernels, gradient_blocks(): pl.pallas_call(functools.partial(gradient_kernel, blocks=spans, pairs=len...  51.6 us
    ppermute x3, waiting for transfers between devices, reduce_gradient(): landed = lax.ppermute(halves, PLANE, along)  45.5 us
    dot_general x9, matrix products, dot_nt(): lax.dot_general(a, b, (((1,), (1,)), ((), ())), preferred_element_type=jn...  42.3 us
    dot_general x10, matrix products, dot_nn(): return jnp.dot(a, b, preferred_element_type=jnp.float32)  38.4 us
    pallas_call x2, Pallas kernels, attend_back_call(): pl.pallas_call(attend_back_kernel, grid=(pairs,), in_specs=[column(0), co...  15.3 us
    ppermute x3, waiting for transfers between devices, reduce_gradient(): arrived = lax.ppermute(diagonal, PLANE, cross)  14.1 us
    pallas_call x2, Pallas kernels, attend_call(): pl.pallas_call(attend_kernel, grid=(pairs,), in_specs=[column(0), column(...  13.6 us
  transfers between devices with their start and end apart: 22, of which 11 were waited for; matrix products, arithmetic and copies ran while one was open for 19% of the time, Pallas kernels for 14%

profile of v2, /device:TPU:0, one launch (start us, length us, event | category | flops | bytes accessed | tf_op | source)
XLA Modules:
  0.0 475.3 jit_solution(10894576385188515036)
XLA Ops:
  14.8 7.3 %all-to-all-start = ((f32[32,1,384]{2,1,0:T(1,128)}), f32[32,1,384]{2,1,0:T(1,128)S(1)}, u32[]{:S(2)}, u32[]{:S(2)}) async-start(f32[32,1,384]{2,1,0:T(1,128)} %broadcast_in_dim.15), calls=%async_computation | async-start | bytes 98304 | tf_op jit(solution)/shard_map/all_to_all | solution.py:630
  27.2 2.3 all-to-all-done
  31.4 12.8 %collective-permute-done = bf16[256,1024]{1,0:T(8,128)(2,1)} collective-permute-done((bf16[256,1024]{1,0:T(8,128)(2,1)}, bf16[256,1024]{1,0:T(8,128)(2,1)}, u32[]{:S(2)}, u32[]{:S(2)}) %collective-permute-start) | collective-permute-done | bytes 524320 | tf_op jit(solution)/shard_map/ppermute | solution.py:588
  44.2 2.4 fusion.49.refs_0_
  46.5 127.7 %all-gather.2.cloned.1.call-done = bf16[2048,6144]{1,0:T(8,128)(2,1)} async-done(((bf16[64,6144]{1,0:T(8,128)(2,1)}), bf16[2048,6144]{1,0:T(8,128)(2,1)}) %all-gather.2.cloned.1.call-update) | async-done | bytes 25165840 | tf_op jit(solution)/shard_map/all_gather | solution.py:609
  174.2 3.7 fusion.27.q_ref.k_ref.v_ref
  177.9 7.1 %attend.2 = (bf16[512,512]{1,0:T(8,128)(2,1)S(1)}, f32[4,2,512]{2,1,0:T(2,128)S(1)}) custom-call(bf16[512,1536]{1,0:T(8,128)(2,1)S(1)} %fusion.27.q_ref.k_ref.v_ref, bf16[512,1536]{1,0:T(8,128)(2,1)S(1)} %fusion.27.q_ref.k_ref.v_ref, bf16[512,1536]{1,0:T(8,128)(2,1)S(1)} %fusion.27.q_ref.k_ref.v_ref, s32[1,512]{1,0:T(1,128)S(1)} %get-tuple-element.120.row_ref, ...), custom_call_target="tpu_custom_call" | custom-call | flops 1073741824 | bytes 2097152 | tf_op jit(solution)/shard_map/attend/pallas_call | solution.py:355
  185.0 2.2 fusion.63
  187.2 3.7 fusion.28.q_ref.k_ref.v_ref
  190.9 6.5 %attend.3 = (bf16[512,512]{1,0:T(8,128)(2,1)S(1)}, f32[4,2,512]{2,1,0:T(2,128)S(1)}) custom-call(bf16[512,1536]{1,0:T(8,128)(2,1)S(1)} %fusion.28.q_ref.k_ref.v_ref, bf16[512,1536]{1,0:T(8,128)(2,1)S(1)} %fusion.28.q_ref.k_ref.v_ref, bf16[512,1536]{1,0:T(8,128)(2,1)S(1)} %fusion.28.q_ref.k_ref.v_ref, s32[1,512]{1,0:T(1,128)S(1)} %get-tuple-element.120.row_ref, ...), custom_call_target="tpu_custom_call" | custom-call | flops 1073741824 | bytes 2097152 | tf_op jit(solution)/shard_map/attend/pallas_call | solution.py:355
  197.4 2.3 fusion.82
  200.6 4.9 %multiply_convert_fusion.1 = (bf16[512,2048]{1,0:T(8,128)(2,1)S(1)}, f32[512,2048]{1,0:T(8,128)S(1)}) fusion(f32[2048]{0:T(1024)S(1)} %bitcast.193, bf16[512,1024]{1,0:T(8,128)(2,1)S(1)} %fusion.48.refs_0_, bf16[2,1024,6144]{2,1,0:T(8,128)(2,1)} %bitcast.177), kind=kOutput, calls=%fused_computation.25 | convolution fusion | flops 2153775104 | bytes 11542528 | tf_op jit(solution)/shard_map/dot_general | solution.py:404
  205.5 5.3 %fusion.19 = f32[512,1024]{1,0:T(8,128)S(1)} fusion(bf16[512,2048]{1,0:T(8,128)(2,1)S(1)} %get-tuple-element.134.refs_1_, bf16[2,1024,6144]{2,1,0:T(8,128)(2,1)} %bitcast.178), kind=kOutput, calls=%fused_computation.35 | convolution fusion | flops 2147483648 | bytes 8388608 | tf_op jit(solution)/shard_map/dot_general | solution.py:408
  210.8 4.7 multiply_convert_fusion
  215.6 5.8 %fusion.83 = (f32[512]{0:T(512)S(1)}, f32[512,1024]{1,0:T(8,128)S(1)}) fusion(f32[1024]{0:T(1024)S(1)} %add.252, f32[512,1024]{1,0:T(8,128)S(1)} %fusion.19, bf16[512,2048]{1,0:T(8,128)(2,1)S(1)} %get-tuple-element.136.refs_2_, bf16[2,1024,6144]{2,1,0:T(8,128)(2,1)} %bitcast.180, f32[1024]{0:T(1024)S(1)} %add.239, f32[1024]{0:T(1024)S(1)} %mul.163, ...), kind=kOutput, calls=%fused_computation.183 | convolution fusion | flops 2151677440 | bytes 12601344 | tf_op jit(solution)/shard_map/dot_general | solution.py:408
  221.8 3.3 fusion.37
  226.0 5.7 %convert_reduce_fusion.1 = (f32[2048]{0:T(1024)S(1)}, bf16[512,2048]{1,0:T(8,128)(2,1)S(1)}) fusion(f32[512,2048]{1,0:T(8,128)S(1)} %get-tuple-element.135, f32[2048]{0:T(1024)S(1)} %bitcast.194, bf16[512,1024]{1,0:T(8,128)(2,1)S(1)} %convert_element_type.162.refs_0_, bf16[2,1024,6144]{2,1,0:T(8,128)(2,1)} %bitcast.181), kind=kOutput, calls=%fused_computation.21 | convolution fusion | flops 2161113088 | bytes 11550720 | tf_op jit(solution)/shard_map/dot_general | solution.py:404
  231.7 5.3 %fusion.16 = f32[512,1024]{1,0:T(8,128)S(1)} fusion(bf16[512,2048]{1,0:T(8,128)(2,1)S(1)} %get-tuple-element.145.refs_1_, bf16[2,1024,6144]{2,1,0:T(8,128)(2,1)} %bitcast.182), kind=kOutput, calls=%fused_computation.32 | convolution fusion | flops 2147483648 | bytes 8388608 | tf_op jit(solution)/shard_map/dot_general | solution.py:408
  237.0 5.3 %convert_reduce_fusion = (f32[2048]{0:T(1024)S(1)}, bf16[512,2048]{1,0:T(8,128)(2,1)S(1)}) fusion(f32[512,2048]{1,0:T(8,128)S(1)} %get-tuple-element.137, f32[2048]{0:T(1024)S(1)} %bitcast.196, bf16[512,1024]{1,0:T(8,128)(2,1)S(1)} %convert_element_type.162.refs_0_, bf16[2,1024,6144]{2,1,0:T(8,128)(2,1)} %bitcast.183), kind=kOutput, calls=%fused_computation.20 | convolution fusion | flops 2161113088 | bytes 11550720 | tf_op jit(solution)/shard_map/dot_general | solution.py:404
  242.4 5.8 %multiply_reduce_fusion = (f32[1024]{0:T(1024)S(1)}, f32[512]{0:T(512)S(1)}, f32[512]{0:T(512)S(1)}, f32[1024]{0:T(1024)S(1)}, f32[512,1024]{1,0:T(8,128)S(1)}) fusion(f32[512,1024]{1,0:T(8,128)S(1)} %get-tuple-element.133, f32[512]{0:T(512)S(1)} %add_rsqrt_fusion.1, f32[512]{0:T(512)S(1)} %broadcast_multiply_fusion.5, f32[1024]{0:T(1024)S(1)} %mul.163, ...), kind=kOutput, calls=%fused_computation.72 | convolution fusion | flops 2153247744 | bytes 14700544 | tf_op jit(solution)/shard_map/dot_general | solution.py:408
  249.2 2.8 convolution_convert_fusion.1.grad_ref
  251.9 1.9 convolution_convert_fusion.grad_ref
  253.9 7.5 %gradient_blocks.10 = bf16[1024,2048]{1,0:T(8,128)(2,1)} custom-call(s32[4]{0:T(128)} %get-tuple-element.88.row_ref, s32[4]{0:T(128)} %broadcast_select_fusion.2.part_ref, bf16[512,1024]{1,0:T(8,128)(2,1)} %copy-done.6, bf16[512,2048]{1,0:T(8,128)(2,1)} %copy-done.10, bf16[512,2048]{1,0:T(8,128)(2,1)} %copy-done.11), custom_call_target="tpu_custom_call" | custom-call | flops 2147483648 | bytes 12582912 | tf_op jit(solution)/shard_map/gradient_blocks/pallas_call | solution.py:481
  261.4 7.5 %gradient_blocks.8 = bf16[1024,2048]{1,0:T(8,128)(2,1)} custom-call(s32[4]{0:T(128)} %get-tuple-element.88.row_ref, s32[4]{0:T(128)} %broadcast_select_fusion.2.part_ref, bf16[512,1024]{1,0:T(8,128)(2,1)} %copy-done.7, bf16[512,2048]{1,0:T(8,128)(2,1)} %copy-done.12, bf16[512,2048]{1,0:T(8,128)(2,1)} %copy-done.13), custom_call_target="tpu_custom_call" | custom-call | flops 2147483648 | bytes 12582912 | tf_op jit(solution)/shard_map/gradient_blocks/pallas_call | solution.py:481
  269.4 7.6 %attend_back.2.refs_2_ = bf16[512,1536]{1,0:T(8,128)(2,1)S(1)} custom-call(bf16[512,1536]{1,0:T(8,128)(2,1)S(1)} %fusion.27.q_ref.k_ref.v_ref, bf16[512,1536]{1,0:T(8,128)(2,1)S(1)} %fusion.27.q_ref.k_ref.v_ref, bf16[512,1536]{1,0:T(8,128)(2,1)S(1)} %fusion.27.q_ref.k_ref.v_ref, bf16[512,512]{1,0:T(8,128)(2,1)S(1)} %convolution_convert_fusion.1.grad_ref, ...), custom_call_target="tpu_custom_call" | custom-call | flops 2684354560 | bytes 3670016 | tf_op jit(solution)/shard_map/attend_back/pallas_call | solution.py:379
  278.2 7.6 %attend_back.3.refs_3_ = bf16[512,1536]{1,0:T(8,128)(2,1)S(1)} custom-call(bf16[512,1536]{1,0:T(8,128)(2,1)S(1)} %fusion.28.q_ref.k_ref.v_ref, bf16[512,1536]{1,0:T(8,128)(2,1)S(1)} %fusion.28.q_ref.k_ref.v_ref, bf16[512,1536]{1,0:T(8,128)(2,1)S(1)} %fusion.28.q_ref.k_ref.v_ref, bf16[512,512]{1,0:T(8,128)(2,1)S(1)} %convolution_convert_fusion.grad_ref, ...), custom_call_target="tpu_custom_call" | custom-call | flops 2684354560 | bytes 3670016 | tf_op jit(solution)/shard_map/attend_back/pallas_call | solution.py:379
  287.0 7.7 %gradient_blocks.6 = bf16[1024,2048]{1,0:T(8,128)(2,1)} custom-call(s32[4]{0:T(128)} %get-tuple-element.88.row_ref, s32[4]{0:T(128)} %broadcast_select_fusion.2.part_ref, bf16[512,1024]{1,0:T(8,128)(2,1)} %copy-done.9, bf16[512,1024]{1,0:T(8,128)(2,1)} %copy-done.8, bf16[512,1536]{1,0:T(8,128)(2,1)} %copy-done.2, bf16[512,1536]{1,0:T(8,128)(2,1)} %copy-done, ...), custom_call_target="tpu_custom_call" | custom-call | flops 2147483648 | bytes 12582912 | tf_op jit(solution)/shard_map/gradient_blocks/pallas_call | solution.py:481
  295.5 9.8 %gradient_blocks.11 = (bf16[512,2048]{1,0:T(8,128)(2,1)}, bf16[256,2048]{1,0:T(8,128)(2,1)}, bf16[256,2048]{1,0:T(8,128)(2,1)}) custom-call(s32[4]{0:T(128)} %get-tuple-element.149.row_ref, s32[4]{0:T(128)} %get-tuple-element.148.part_ref, bf16[512,1024]{1,0:T(8,128)(2,1)} %copy-done.6, bf16[512,2048]{1,0:T(8,128)(2,1)} %copy-done.10, ...), custom_call_target="tpu_custom_call" | custom-call | flops 2147483648 | bytes 12582912 | tf_op jit(solution)/shard_map/gradient_blocks/pallas_call | solution.py:481
  306.7 9.4 %gradient_blocks.9 = (bf16[512,2048]{1,0:T(8,128)(2,1)}, bf16[256,2048]{1,0:T(8,128)(2,1)}, bf16[256,2048]{1,0:T(8,128)(2,1)}) custom-call(s32[4]{0:T(128)} %get-tuple-element.149.row_ref, s32[4]{0:T(128)} %get-tuple-element.148.part_ref, bf16[512,1024]{1,0:T(8,128)(2,1)} %copy-done.7, bf16[512,2048]{1,0:T(8,128)(2,1)} %copy-done.12, ...), custom_call_target="tpu_custom_call" | custom-call | flops 2147483648 | bytes 12582912 | tf_op jit(solution)/shard_map/gradient_blocks/pallas_call | solution.py:481
  316.5 9.7 %gradient_blocks.7 = (bf16[512,2048]{1,0:T(8,128)(2,1)}, bf16[256,2048]{1,0:T(8,128)(2,1)}, bf16[256,2048]{1,0:T(8,128)(2,1)}) custom-call(s32[4]{0:T(128)} %get-tuple-element.149.row_ref, s32[4]{0:T(128)} %get-tuple-element.148.part_ref, bf16[512,1024]{1,0:T(8,128)(2,1)} %copy-done.9, bf16[512,1024]{1,0:T(8,128)(2,1)} %copy-done.8, ...), custom_call_target="tpu_custom_call" | custom-call | flops 2147483648 | bytes 12582912 | tf_op jit(solution)/shard_map/gradient_blocks/pallas_call | solution.py:481
  327.9 3.1 collective-permute-done.9
  331.2 11.0 %collective-permute-done.5 = bf16[256,2048]{1,0:T(8,128)(2,1)S(1)} collective-permute-done((bf16[256,2048]{1,0:T(8,128)(2,1)}, bf16[256,2048]{1,0:T(8,128)(2,1)S(1)}, u32[]{:S(2)}, u32[]{:S(2)}) %collective-permute-start.5) | collective-permute-done | bytes 1048608 | tf_op jit(solution)/shard_map/ppermute | solution.py:541
  342.5 4.1 fusion.26
  348.7 24.3 %collective-permute-done.6 = bf16[2,256,2048]{2,1,0:T(8,128)(2,1)} collective-permute-done((bf16[2,256,2048]{2,1,0:T(8,128)(2,1)}, bf16[2,256,2048]{2,1,0:T(8,128)(2,1)}, u32[]{:S(2)}, u32[]{:S(2)}) %collective-permute-start.6) | collective-permute-done | bytes 2097184 | tf_op jit(solution)/shard_map/ppermute | solution.py:548
  373.0 2.3 dynamic-slice_bitcast_fusion.2
  375.3 3.0 collective-permute-done.7
  378.3 3.1 fusion.43
  383.1 12.3 %collective-permute-done.10 = bf16[2,256,2048]{2,1,0:T(8,128)(2,1)S(1)} collective-permute-done((bf16[2,256,2048]{2,1,0:T(8,128)(2,1)}, bf16[2,256,2048]{2,1,0:T(8,128)(2,1)S(1)}, u32[]{:S(2)}, u32[]{:S(2)}) %collective-permute-start.10) | collective-permute-done | bytes 2097184 | tf_op jit(solution)/shard_map/ppermute | solution.py:548
  397.1 3.2 fusion.50
  405.7 3.0 fusion.41
  409.0 8.9 %collective-permute-done.14 = bf16[2,256,2048]{2,1,0:T(8,128)(2,1)} collective-permute-done((bf16[2,256,2048]{2,1,0:T(8,128)(2,1)}, bf16[2,256,2048]{2,1,0:T(8,128)(2,1)}, u32[]{:S(2)}, u32[]{:S(2)}) %collective-permute-start.14) | collective-permute-done | bytes 2097184 | tf_op jit(solution)/shard_map/ppermute | solution.py:548
  417.9 2.3 dynamic-slice_bitcast_fusion
  420.2 5.1 %collective-permute-start.15 = (bf16[256,2048]{1,0:T(8,128)(2,1)}, bf16[256,2048]{1,0:T(8,128)(2,1)}, u32[]{:S(2)}, u32[]{:S(2)}) collective-permute-start(bf16[256,2048]{1,0:T(8,128)(2,1)} %dynamic-slice_bitcast_fusion), channel_id=1, source_target_pairs={{0,2},{2,0},{1,3},{3,1},{4,6},{6,4},{5,7},{7,5},{8,10},{10,8},{9,1... | collective-permute-start | bytes 3145736 | tf_op jit(solution)/shard_map/ppermute | solution.py:549
  427.1 2.8 all-to-all-start.1
  430.0 5.2 %fusion.32 = f32[512,1024]{1,0:T(8,128)} fusion(bf16[512,1536]{1,0:T(8,128)(2,1)S(1)} %copy-done.3, bf16[2,1024,6144]{2,1,0:T(8,128)(2,1)} %bitcast.187), kind=kOutput, calls=%fused_computation.57 | convolution fusion | flops 1610612736 | bytes 6815744 | tf_op jit(solution)/shard_map/dot_general | solution.py:408
  435.2 3.0 fusion.39
  438.3 7.2 %fusion.52 = bf16[512,1024]{1,0:T(8,128)(2,1)} fusion(s32[1024]{0:T(1024)S(1)} %reshape.412, f32[512,1024]{1,0:T(8,128)} %copy-done.14, f32[512,1024]{1,0:T(8,128)} %fusion.32, bf16[512,1536]{1,0:T(8,128)(2,1)S(1)} %copy-done.1, bf16[2,1024,6144]{2,1,0:T(8,128)(2,1)} %bitcast.188), kind=kOutput, calls=%fused_computation.94 | convolution fusion | flops 2687500288 | bytes 9965568 | tf_op jit(solution)/shard_map/dot_general | solution.py:408
  453.4 7.2 %collective-permute-done.3 = bf16[256,1024]{1,0:T(8,128)(2,1)S(1)} collective-permute-done((bf16[256,1024]{1,0:T(8,128)(2,1)S(1)}, bf16[256,1024]{1,0:T(8,128)(2,1)S(1)}, u32[]{:S(2)}, u32[]{:S(2)}) %collective-permute-start.3) | collective-permute-done | bytes 524320 | tf_op jit(solution)/shard_map/ppermute | solution.py:593
  (228 shorter events, 53.5 us)
Async XLA Ops:
  7.2 6.5 %copy-start.33 = (f32[4,32]{1,0:T(4,128)S(1)}, f32[4,32]{1,0:T(4,128)}, u32[]{:S(2)}) copy-start(f32[4,32]{1,0:T(4,128)} %param.20) | copy-start | bytes 1540
  7.2 6.6 %copy-start.34 = (f32[2,32]{1,0:T(2,128)S(1)}, f32[2,32]{1,0:T(2,128)}, u32[]{:S(2)}) copy-start(f32[2,32]{1,0:T(2,128)} %param.19) | copy-start | bytes 772
  7.2 6.7 %copy-start.32 = (bf16[2,8,4]{1,2,0:T(4,128)(2,1)S(1)}, bf16[2,8,4]{1,2,0:T(4,128)(2,1)}, u32[]{:S(2)}) copy-start(bf16[2,8,4]{1,2,0:T(4,128)(2,1)} %param.14) | copy-start | bytes 388
  7.2 6.8 %copy-start.35 = (bf16[1,128]{1,0:T(2,128)(2,1)S(1)}, bf16[1,128]{1,0:T(2,128)(2,1)}, u32[]{:S(2)}) copy-start(bf16[1,128]{1,0:T(2,128)(2,1)} %param.17) | copy-start | bytes 772
  7.2 14.9 %copy-start.27 = (bf16[2,256,1024]{2,1,0:T(8,128)(2,1)S(1)}, bf16[2,256,1024]{2,1,0:T(8,128)(2,1)}, u32[]{:S(2)}) copy-start(bf16[2,256,1024]{2,1,0:T(8,128)(2,1)} %param.11) | copy-start | bytes 3145732
  7.2 167.0 %all-gather.2.cloned.1.call-start = ((), (), s32[]{:S(2)}) async-start(), calls=%async_computation.5 | async-start | bytes 25952256 | tf_op jit(solution)/shard_map/all_gather | solution.py:609
  10.7 14.3 %copy-start.28 = (bf16[2,256,1024]{2,1,0:T(8,128)(2,1)S(1)}, bf16[2,256,1024]{2,1,0:T(8,128)(2,1)}, u32[]{:S(2)}) copy-start(bf16[2,256,1024]{2,1,0:T(8,128)(2,1)} %param.21) | copy-start | bytes 3145732
  14.8 14.7 %all-to-all-start = ((f32[32,1,384]{2,1,0:T(1,128)}), f32[32,1,384]{2,1,0:T(1,128)S(1)}, u32[]{:S(2)}, u32[]{:S(2)}) async-start(f32[32,1,384]{2,1,0:T(1,128)} %broadcast_in_dim.15), calls=%async_computation | async-start | bytes 98304 | tf_op jit(solution)/shard_map/all_to_all | solution.py:630
  22.1 439.7 %reduce-scatter.4.cloned.1.call-start = ((), (), s32[]{:S(2)}) async-start(), calls=%async_computation.6 | async-start | bytes 1310720 | tf_op jit(solution)/shard_map/reduce_scatter | solution.py:552
  22.2 3.3 copy-start.31
  23.2 21.0 %collective-permute-start = (bf16[256,1024]{1,0:T(8,128)(2,1)}, bf16[256,1024]{1,0:T(8,128)(2,1)}, u32[]{:S(2)}, u32[]{:S(2)}) collective-permute-start(bf16[256,1024]{1,0:T(8,128)(2,1)} %get-tuple-element.98), channel_id=1, source_target_pairs={{0,1},{1,0},{2,3},{3,2},{4,5},{5,4},{6,7},{7,6},{8,9},{9,8},{10,11... | collective-permute-start | bytes 1572872 | tf_op jit(solution)/shard_map/ppermute | solution.py:588
  25.1 19.1 %copy-start.30 = (bf16[256,1024]{1,0:T(8,128)(2,1)S(1)}, bf16[256,1024]{1,0:T(8,128)(2,1)}, u32[]{:S(2)}) copy-start(bf16[256,1024]{1,0:T(8,128)(2,1)} %get-tuple-element.97) | copy-start | bytes 1572868
  25.1 196.6 %collective-permute-start.2 = (bf16[256,1024]{1,0:T(8,128)(2,1)S(1)}, bf16[256,1024]{1,0:T(8,128)(2,1)}, u32[]{:S(2)}, u32[]{:S(2)}) collective-permute-start(bf16[256,1024]{1,0:T(8,128)(2,1)S(1)} %get-tuple-element.96), channel_id=1, source_target_pairs={{0,1},{1,0},{2,3},{3,2},{4,5},{5,4},{6,7},{7,6},{8,9},{9,8},{10,11... | collective-permute-start | bytes 1572872 | tf_op jit(solution)/shard_map/ppermute | solution.py:588
  46.5 150.9 %copy-start.9 = (bf16[512,1024]{1,0:T(8,128)(2,1)}, bf16[512,1024]{1,0:T(8,128)(2,1)S(1)}, u32[]{:S(2)}) copy-start(bf16[512,1024]{1,0:T(8,128)(2,1)S(1)} %fusion.49.refs_0_) | copy-start | bytes 3145732
  185.0 5.9 %copy-start.4 = (bf16[512,512]{1,0:T(8,128)(2,1)}, bf16[512,512]{1,0:T(8,128)(2,1)S(1)}, u32[]{:S(2)}) copy-start(bf16[512,512]{1,0:T(8,128)(2,1)S(1)} %get-tuple-element.23.refs_4_) | copy-start | bytes 1572868
  200.6 10.3 %copy-start.7 = (bf16[512,1024]{1,0:T(8,128)(2,1)}, bf16[512,1024]{1,0:T(8,128)(2,1)S(1)}, u32[]{:S(2)}) copy-start(bf16[512,1024]{1,0:T(8,128)(2,1)S(1)} %fusion.48.refs_0_) | copy-start | bytes 3145732
  205.5 5.3 %copy-start.10 = (bf16[512,2048]{1,0:T(8,128)(2,1)}, bf16[512,2048]{1,0:T(8,128)(2,1)S(1)}, u32[]{:S(2)}) copy-start(bf16[512,2048]{1,0:T(8,128)(2,1)S(1)} %get-tuple-element.134.refs_1_) | copy-start | bytes 6291460
  215.6 5.8 %copy-start.11 = (bf16[512,2048]{1,0:T(8,128)(2,1)}, bf16[512,2048]{1,0:T(8,128)(2,1)S(1)}, u32[]{:S(2)}) copy-start(bf16[512,2048]{1,0:T(8,128)(2,1)S(1)} %get-tuple-element.136.refs_2_) | copy-start | bytes 6291460
  221.4 3.7 copy-start.15
  226.0 11.1 %copy-start.6 = (bf16[512,1024]{1,0:T(8,128)(2,1)}, bf16[512,1024]{1,0:T(8,128)(2,1)S(1)}, u32[]{:S(2)}) copy-start(bf16[512,1024]{1,0:T(8,128)(2,1)S(1)} %convert_element_type.162.refs_0_) | copy-start | bytes 3145732
  231.7 5.3 %copy-start.12 = (bf16[512,2048]{1,0:T(8,128)(2,1)}, bf16[512,2048]{1,0:T(8,128)(2,1)S(1)}, u32[]{:S(2)}) copy-start(bf16[512,2048]{1,0:T(8,128)(2,1)S(1)} %get-tuple-element.145.refs_1_) | copy-start | bytes 6291460
  242.4 5.9 %copy-start.13 = (bf16[512,2048]{1,0:T(8,128)(2,1)}, bf16[512,2048]{1,0:T(8,128)(2,1)S(1)}, u32[]{:S(2)}) copy-start(bf16[512,2048]{1,0:T(8,128)(2,1)S(1)} %get-tuple-element.143.refs_2_) | copy-start | bytes 6291460
  249.1 4.7 copy-start.8
  268.9 26.6 %collective-permute-start.12 = (bf16[1024,2048]{1,0:T(8,128)(2,1)}, bf16[1024,2048]{1,0:T(8,128)(2,1)}, u32[]{:S(2)}, u32[]{:S(2)}) collective-permute-start(bf16[1024,2048]{1,0:T(8,128)(2,1)} %gradient_blocks.10), channel_id=1, source_target_pairs={{0,2},{2,0},{1,3},{3,1},{4,6},{6,4},{5,7},{7,5},{8,10},{10,8},{9,1... | collective-permute-start | bytes 12582920 | tf_op jit(solution)/shard_map/ppermute | solution.py:538
  269.1 37.5 %collective-permute-start.8 = (bf16[1024,2048]{1,0:T(8,128)(2,1)}, bf16[1024,2048]{1,0:T(8,128)(2,1)}, u32[]{:S(2)}, u32[]{:S(2)}) collective-permute-start(bf16[1024,2048]{1,0:T(8,128)(2,1)} %gradient_blocks.8), channel_id=1, source_target_pairs={{0,2},{2,0},{1,3},{3,1},{4,6},{6,4},{5,7},{7,5},{8,10},{10,8},{9,1... | collective-permute-start | bytes 12582920 | tf_op jit(solution)/shard_map/ppermute | solution.py:538
  294.8 21.7 %collective-permute-start.4 = (bf16[1024,2048]{1,0:T(8,128)(2,1)}, bf16[1024,2048]{1,0:T(8,128)(2,1)}, u32[]{:S(2)}, u32[]{:S(2)}) collective-permute-start(bf16[1024,2048]{1,0:T(8,128)(2,1)} %gradient_blocks.6), channel_id=1, source_target_pairs={{0,2},{2,0},{1,3},{3,1},{4,6},{6,4},{5,7},{7,5},{8,10},{10,8},{9,1... | collective-permute-start | bytes 12582920 | tf_op jit(solution)/shard_map/ppermute | solution.py:538
  305.3 22.3 %collective-permute-start.13 = (bf16[256,2048]{1,0:T(8,128)(2,1)}, bf16[256,2048]{1,0:T(8,128)(2,1)S(1)}, u32[]{:S(2)}, u32[]{:S(2)}) collective-permute-start(bf16[256,2048]{1,0:T(8,128)(2,1)} %get-tuple-element.35), channel_id=1, source_target_pairs={{0,6},{1,7},{4,2},{5,3},{2,1},{3,0},{6,5},{7,4},{8,14},{9,15},{12,... | collective-permute-start | bytes 3145736 | tf_op jit(solution)/shard_map/ppermute | solution.py:541
  316.0 14.9 %collective-permute-start.9 = (bf16[256,2048]{1,0:T(8,128)(2,1)}, bf16[256,2048]{1,0:T(8,128)(2,1)S(1)}, u32[]{:S(2)}, u32[]{:S(2)}) collective-permute-start(bf16[256,2048]{1,0:T(8,128)(2,1)} %get-tuple-element.32), channel_id=1, source_target_pairs={{0,6},{1,7},{4,2},{5,3},{2,1},{3,0},{6,5},{7,4},{8,14},{9,15},{12,... | collective-permute-start | bytes 3145736 | tf_op jit(solution)/shard_map/ppermute | solution.py:541
  326.2 16.0 %collective-permute-start.5 = (bf16[256,2048]{1,0:T(8,128)(2,1)}, bf16[256,2048]{1,0:T(8,128)(2,1)S(1)}, u32[]{:S(2)}, u32[]{:S(2)}) collective-permute-start(bf16[256,2048]{1,0:T(8,128)(2,1)} %get-tuple-element.29), channel_id=1, source_target_pairs={{0,6},{1,7},{4,2},{5,3},{2,1},{3,0},{6,5},{7,4},{8,14},{9,15},{12,... | collective-permute-start | bytes 3145736 | tf_op jit(solution)/shard_map/ppermute | solution.py:541
  331.0 11.5 %copy-start.19 = (bf16[512,2048]{1,0:T(8,128)(2,1)S(1)}, bf16[512,2048]{1,0:T(8,128)(2,1)}, u32[]{:S(2)}) copy-start(bf16[512,2048]{1,0:T(8,128)(2,1)} %get-tuple-element.31) | copy-start | bytes 6291460
  331.0 11.5 %copy-start.20 = (bf16[512,2048]{1,0:T(8,128)(2,1)S(1)}, bf16[512,2048]{1,0:T(8,128)(2,1)}, u32[]{:S(2)}) copy-start(bf16[512,2048]{1,0:T(8,128)(2,1)} %get-tuple-element.28) | copy-start | bytes 6291460
  331.2 11.3 %copy-start.18 = (bf16[512,2048]{1,0:T(8,128)(2,1)S(1)}, bf16[512,2048]{1,0:T(8,128)(2,1)}, u32[]{:S(2)}) copy-start(bf16[512,2048]{1,0:T(8,128)(2,1)} %get-tuple-element.34) | copy-start | bytes 6291460
  346.6 31.7 %copy-start.23 = (bf16[256,2048]{1,0:T(8,128)(2,1)S(1)}, bf16[256,2048]{1,0:T(8,128)(2,1)}, u32[]{:S(2)}) copy-start(bf16[256,2048]{1,0:T(8,128)(2,1)} %get-tuple-element.27) | copy-start | bytes 3145732
  346.6 26.4 %collective-permute-start.6 = (bf16[2,256,2048]{2,1,0:T(8,128)(2,1)}, bf16[2,256,2048]{2,1,0:T(8,128)(2,1)}, u32[]{:S(2)}, u32[]{:S(2)}) collective-permute-start(bf16[2,256,2048]{2,1,0:T(8,128)(2,1)} %get-tuple-element.131), channel_id=1, source_target_pairs={{0,4},{1,5},{4,0},{5,1},{2,3},{3,2},{6,7},{7,6},{8,12},{9,13},{12,... | collective-permute-start | bytes 6291464 | tf_op jit(solution)/shard_map/ppermute | solution.py:548
  348.1 47.3 %collective-permute-start.10 = (bf16[2,256,2048]{2,1,0:T(8,128)(2,1)}, bf16[2,256,2048]{2,1,0:T(8,128)(2,1)S(1)}, u32[]{:S(2)}, u32[]{:S(2)}) collective-permute-start(bf16[2,256,2048]{2,1,0:T(8,128)(2,1)} %get-tuple-element.130), channel_id=1, source_target_pairs={{0,4},{1,5},{4,0},{5,1},{2,3},{3,2},{6,7},{7,6},{8,12},{9,13},{12,... | collective-permute-start | bytes 6291464 | tf_op jit(solution)/shard_map/ppermute | solution.py:548
  375.3 3.0 collective-permute-start.7
  381.4 82.7 %reduce-scatter.6.cloned.1.call-start = ((), (), s32[]{:S(2)}) async-start(), calls=%async_computation.7 | async-start | bytes 1310720 | tf_op jit(solution)/shard_map/reduce_scatter | solution.py:552
  381.6 36.3 %collective-permute-start.14 = (bf16[2,256,2048]{2,1,0:T(8,128)(2,1)}, bf16[2,256,2048]{2,1,0:T(8,128)(2,1)}, u32[]{:S(2)}, u32[]{:S(2)}) collective-permute-start(bf16[2,256,2048]{2,1,0:T(8,128)(2,1)} %get-tuple-element.129), channel_id=1, source_target_pairs={{0,4},{1,5},{4,0},{5,1},{2,3},{3,2},{6,7},{7,6},{8,12},{9,13},{12,... | collective-permute-start | bytes 6291464 | tf_op jit(solution)/shard_map/ppermute | solution.py:548
  396.5 8.2 %collective-permute-start.11 = (bf16[256,2048]{1,0:T(8,128)(2,1)}, bf16[256,2048]{1,0:T(8,128)(2,1)}, u32[]{:S(2)}, u32[]{:S(2)}) collective-permute-start(bf16[256,2048]{1,0:T(8,128)(2,1)} %dynamic-slice_bitcast_fusion.1), channel_id=1, source_target_pairs={{0,2},{2,0},{1,3},{3,1},{4,6},{6,4},{5,7},{7,5},{8,10},{10,8},{9,1... | collective-permute-start | bytes 3145736 | tf_op jit(solution)/shard_map/ppermute | solution.py:549
  397.1 7.1 %copy-start.1 = (bf16[512,1536]{1,0:T(8,128)(2,1)S(1)}, bf16[512,1536]{1,0:T(8,128)(2,1)}, u32[]{:S(2)}) copy-start(bf16[512,1536]{1,0:T(8,128)(2,1)} %copy-done) | copy-start | bytes 4718596
  402.1 49.1 %collective-permute-start.1 = (bf16[256,1024]{1,0:T(8,128)(2,1)}, bf16[256,1024]{1,0:T(8,128)(2,1)}, u32[]{:S(2)}, u32[]{:S(2)}) collective-permute-start(bf16[256,1024]{1,0:T(8,128)(2,1)} %slice.277), channel_id=1, source_target_pairs={{0,1},{1,0},{2,3},{3,2},{4,5},{5,4},{6,7},{7,6},{8,9},{9,8},{10,11... | collective-permute-start | bytes 1572872 | tf_op jit(solution)/shard_map/ppermute | solution.py:593
  420.2 15.0 %collective-permute-start.15 = (bf16[256,2048]{1,0:T(8,128)(2,1)}, bf16[256,2048]{1,0:T(8,128)(2,1)}, u32[]{:S(2)}, u32[]{:S(2)}) collective-permute-start(bf16[256,2048]{1,0:T(8,128)(2,1)} %dynamic-slice_bitcast_fusion), channel_id=1, source_target_pairs={{0,2},{2,0},{1,3},{3,1},{4,6},{6,4},{5,7},{7,5},{8,10},{10,8},{9,1... | collective-permute-start | bytes 3145736 | tf_op jit(solution)/shard_map/ppermute | solution.py:549
  427.1 21.2 %all-to-all-start.1 = ((f32[32,1,384]{2,1,0:T(1,128)}), f32[32,1,384]{2,1,0:T(1,128)S(1)}, u32[]{:S(2)}, u32[]{:S(2)}) async-start(f32[32,1,384]{2,1,0:T(1,128)} %copy.70), calls=%async_computation.2 | async-start | bytes 98304 | tf_op jit(solution)/shard_map/all_to_all | solution.py:720
  429.9 36.9 %reduce-scatter.8.cloned.1.call-start = ((), (), s32[]{:S(2)}) async-start(), calls=%async_computation.8 | async-start | bytes 1310720 | tf_op jit(solution)/shard_map/reduce_scatter | solution.py:552
  430.0 5.2 %copy-start.22 = (bf16[256,2048]{1,0:T(8,128)(2,1)S(1)}, bf16[256,2048]{1,0:T(8,128)(2,1)}, u32[]{:S(2)}) copy-start(bf16[256,2048]{1,0:T(8,128)(2,1)} %get-tuple-element.33) | copy-start | bytes 3145732
  438.3 12.9 %copy-start.25 = (bf16[512,1024]{1,0:T(8,128)(2,1)S(1)}, bf16[512,1024]{1,0:T(8,128)(2,1)}, u32[]{:S(2)}) copy-start(bf16[512,1024]{1,0:T(8,128)(2,1)} %copy-done.24) | copy-start | bytes 3145732
  446.5 14.1 %collective-permute-start.3 = (bf16[256,1024]{1,0:T(8,128)(2,1)S(1)}, bf16[256,1024]{1,0:T(8,128)(2,1)S(1)}, u32[]{:S(2)}, u32[]{:S(2)}) collective-permute-start(bf16[256,1024]{1,0:T(8,128)(2,1)S(1)} %slice.279), channel_id=1, source_target_pairs={{0,1},{1,0},{2,3},{3,2},{4,5},{5,4},{6,7},{7,6},{8,9},{9,8},{10,11... | collective-permute-start | bytes 1572872 | tf_op jit(solution)/shard_map/ppermute | solution.py:593
  451.2 9.5 %copy-start.26 = (bf16[512,1024]{1,0:T(8,128)(2,1)S(1)}, bf16[512,1024]{1,0:T(8,128)(2,1)}, u32[]{:S(2)}) copy-start(bf16[512,1024]{1,0:T(8,128)(2,1)} %fusion.52) | copy-start | bytes 3145732
  (10 other events, 18.0 us)
Sparse Core Ops, SparseCore 0:
  13.8 160.3 all-gather.1
  381.5 25.3 reduce-scatter.3
  409.3 25.7 reduce-scatter.5
  438.4 28.3 reduce-scatter.7

commit v3 on v2

--- a/solution.py
+++ b/solution.py
@@ -300,7 +300,7 @@
 
 
 def attend_back_kernel(
-    q_ref, k_ref, v_ref, grad_ref, row_ref, col_ref, stats_ref, d_ref
+    q_ref, k_ref, v_ref, grad_ref, row_ref, col_ref, stats_ref, *rest
 ):
     query, keys, values, grad = q_ref[...], k_ref[...], v_ref[...], grad_ref[...]
     scale = jnp.asarray(HEAD_DIM**-0.5, query.dtype)
@@ -332,38 +332,45 @@
         grad_query += lax.dot_general(
             grad_scores, own_keys, (((0,), (0,)), ((), ())), preferred_element_type=jnp.float32
         )
-    pair, width = pl.program_id(0), d_ref.shape[1] // 3
+    pair, out_ref = pl.program_id(0), rest[-1]
+    width = out_ref.shape[1] // 3
     for place, value in enumerate((grad_query, grad_keys, grad_values)):
         start = pl.multiple_of(place * width + pair * LANES, LANES)
-        d_ref[:, pl.ds(start, LANES)] = value.astype(d_ref.dtype)
-
-
-def attention_specs(rows, pairs):
-    def column(offset):
-        return pl.BlockSpec((rows, LANES), lambda i, offset=offset: (0, offset + i))
-
+        out_ref[:, pl.ds(start, LANES)] = value.astype(out_ref.dtype)
+
+
+def attention_specs(rows, pairs, parts):
+    inner = pairs // parts
+
+    def column(place):
+        return pl.BlockSpec(
+            (rows, LANES),
+            lambda i: (0, (i // inner) * (3 * inner) + place * inner + lax.rem(i, inner)),
+        )
+
+    plain = pl.BlockSpec((rows, LANES), lambda i: (0, i))
     row_ids = pl.BlockSpec((1, rows), lambda i: (0, 0))
     column_ids = pl.BlockSpec((rows, 1), lambda i: (0, 0))
     stats = pl.BlockSpec((1, 2, rows), lambda i: (i, 0, 0))
-    return column, row_ids, column_ids, stats
-
-
-def attend_call(projected, segments):
+    return [column(place) for place in range(3)], plain, [row_ids, column_ids], stats
+
+
+def attend_call(projected, segments, parts):
     rows, width = projected.shape[0], projected.shape[1] // 3
     pairs = width // LANES
-    column, row_ids, column_ids, stats = attention_specs(rows, pairs)
+    columns, plain, ids, stats = attention_specs(rows, pairs, parts)
     return pl.pallas_call(
         attend_kernel,
         grid=(pairs,),
-        in_specs=[column(0), column(pairs), column(2 * pairs), row_ids, column_ids],
-        out_specs=[column(0), stats],
+        in_specs=columns + ids,
+        out_specs=[plain, stats],
         out_shape=[
             jax.ShapeDtypeStruct((rows, width), jnp.bfloat16),
             jax.ShapeDtypeStruct((pairs, 2, rows), jnp.float32),
         ],
-        compiler_params=pltpu.CompilerParams(vmem_limit_bytes=48 * 1024 * 1024),
+        compiler_params=pltpu.CompilerParams(vmem_limit_bytes=24 * 1024 * 1024),
         cost_estimate=pl.CostEstimate(
-            flops=8 * pairs * rows * rows * LANES,
+            flops=16 * pairs * rows * rows * LANES,
             bytes_accessed=8 * rows * width,
             transcendentals=2 * pairs * rows * rows,
         ),
@@ -371,33 +378,47 @@
     )(projected, projected, projected, segments[None, :], segments[:, None])
 
 
-def attend_back_call(projected, grad, segments, stats_in):
+def attend_back_call(projected, grad, segments, stats_in, parts, part, others=None):
     rows, width = grad.shape
-    pairs = width // LANES
-    column, row_ids, column_ids, stats = attention_specs(rows, pairs)
-    whole = pl.BlockSpec((rows, 3 * width), lambda i: (0, 0))
+    inner = width // LANES // parts
+
+    def column(place):
+        return pl.BlockSpec(
+            (rows, LANES), lambda i: (0, part * (3 * inner) + place * inner + i)
+        )
+
+    ids = [pl.BlockSpec((1, rows), lambda i: (0, 0)), pl.BlockSpec((rows, 1), lambda i: (0, 0))]
+    stats = pl.BlockSpec((1, 2, rows), lambda i: (part * inner + i, 0, 0))
+    plain = pl.BlockSpec((rows, LANES), lambda i: (0, part * inner + i))
+    rest = [] if others is None else [others]
     return pl.pallas_call(
         attend_back_kernel,
-        grid=(pairs,),
-        in_specs=[
-            column(0),
-            column(pairs),
-            column(2 * pairs),
-            column(0),
-            row_ids,
-            column_ids,
-            stats,
-        ],
-        out_specs=whole,
+        grid=(inner,),
+        in_specs=[column(place) for place in range(3)]
+        + [plain]
+        + ids
+        + [stats]
+        + [pl.BlockSpec(memory_space=pl.ANY)] * len(rest),
+        out_specs=pl.BlockSpec((rows, 3 * width // parts), lambda i: (0, part)),
         out_shape=jax.ShapeDtypeStruct((rows, 3 * width), jnp.bfloat16),
-        compiler_params=pltpu.CompilerParams(vmem_limit_bytes=48 * 1024 * 1024),
+        input_output_aliases={7: 0} if rest else {},
+        compiler_params=pltpu.CompilerParams(vmem_limit_bytes=24 * 1024 * 1024),
         cost_estimate=pl.CostEstimate(
-            flops=20 * pairs * rows * rows * LANES,
-            bytes_accessed=14 * rows * width,
-            transcendentals=2 * pairs * rows * rows,
+            flops=40 * inner * rows * rows * LANES,
+            bytes_accessed=14 * rows * width // parts,
+            transcendentals=2 * inner * rows * rows,
         ),
         name="attend_back",
-    )(projected, projected, projected, grad, segments[None, :], segments[:, None], stats_in)
+    )(
+        projected,
+        projected,
+        projected,
+        grad,
+        segments[None, :],
+        segments[:, None],
+        stats_in,
+        *rest,
+    )
 
 
 def dot_nn(a, b):
@@ -418,91 +439,12 @@
     return values * cdf, cdf + values * density
 
 
-VMEM_BYTES = 56 * 1024 * 1024
-
-
-def gradient_kernel(row_ref, part_ref, *refs, blocks, pairs, added):
-    lefts, rights = refs[:pairs], refs[pairs : 3 * pairs]
-    received = refs[3 * pairs : 3 * pairs + added]
-    outs = refs[3 * pairs + added :]
-    step = pl.program_id(0)
-    size = outs[0].shape[0]
-    start = pl.multiple_of(row_ref[step] * size, size)
-
-    def products(part):
-        pieces = [
-            dot_tn(lefts[i][:, pl.ds(start, size)], rights[2 * i + part][...])
-            for i in range(pairs)
-        ]
-        total = pieces[0] if pairs == 1 else jnp.concatenate(pieces, axis=1)
-        if added:
-            total = total + received[0][...].astype(jnp.float32)
-        total = total.astype(jnp.bfloat16)
-        if len(outs) == 1:
-            outs[0][...] = total
-        else:
-            for out, (low, high) in zip(outs, blocks):
-                @pl.when((step >= low) & (step < high))
-                def _(out=out):
-                    out[...] = total
-
-    for part in range(2):
-        pl.when(part_ref[step] == part)(functools.partial(products, part))
-
-
-def gradient_blocks(rows, parts, lefts, rights, received=None):
-    count = rows.shape[0]
-    size = lefts[0].shape[1] // count
-    width = sum(pair[0].shape[1] for pair in rights)
-    flat = [item for pair in rights for item in pair]
-    spans = ((0, 2), (2, 3), (3, 4))
-    whole = [
-        pl.BlockSpec(item.shape, lambda i, *_: (0, 0), pipeline_mode=pl.Buffered(1))
-        for item in list(lefts) + flat
-    ]
-    block = pl.BlockSpec((size, width), lambda i, *_: (i, 0))
-    in_specs, operands = whole, list(lefts) + flat
-    if received is None:
-        out_shape = [jax.ShapeDtypeStruct((count * size, width), jnp.bfloat16)]
-        out_specs = [block]
-    else:
-        in_specs, operands = whole + [block], operands + [received]
-        out_shape = [
-            jax.ShapeDtypeStruct(((high - low) * size, width), jnp.bfloat16)
-            for low, high in spans
-        ]
-        out_specs = [
-            pl.BlockSpec(
-                (size, width),
-                lambda i, *_, low=low, high=high: (jnp.clip(i, low, high - 1) - low, 0),
-            )
-            for low, high in spans
-        ]
-    return pl.pallas_call(
-        functools.partial(
-            gradient_kernel,
-            blocks=spans,
-            pairs=len(lefts),
-            added=0 if received is None else 1,
-        ),
-        grid_spec=pltpu.PrefetchScalarGridSpec(
-            num_scalar_prefetch=2,
-            grid=(count,),
-            in_specs=in_specs,
-            out_specs=out_specs,
-        ),
-        out_shape=out_shape,
-        compiler_params=pltpu.CompilerParams(vmem_limit_bytes=VMEM_BYTES),
-        cost_estimate=pl.CostEstimate(
-            flops=2 * count * size * lefts[0].shape[0] * width,
-            bytes_accessed=6 * count * size * width,
-            transcendentals=0,
-        ),
-        name="gradient_blocks",
-    )(rows, parts, *operands)
-
-
-def permutes():
+PLANE = ("x", "c", "y")
+EVERY = ("y", "x", "c", "z")
+SWAP = [(0, 1), (1, 0)]
+
+
+def plane_permutes():
     def index(x, c, y):
         return (x * 2 + c) * 2 + y
 
@@ -511,45 +453,211 @@
     along += [(index(x, 1, y), index(x, 1, 1 - y)) for x, y in cells]
     cross = [(index(x, 0, y), index(1 - x, 1, y)) for x, y in cells]
     cross += [(index(x, 1, y), index(x, 0, 1 - y)) for x, y in cells]
-    return along, cross
-
-
-PLANE = ("x", "c", "y")
-EVERY = ("y", "x", "c", "z")
-SWAP = [(0, 1), (1, 0)]
-
-
-def block_tables(x, c, y):
-    def kept(core):
-        first = jnp.stack([2 - 2 * x, 3 - 2 * x, 2 - 2 * x, 2 * x])
-        second = jnp.stack([2 * x, 2 * x + 1, 3 - 2 * x, 2 * x + 1])
-        parts_first = jnp.stack([y, y, 1 - y, y])
-        parts_second = jnp.stack([1 - y, 1 - y, 1 - y, y])
-        return jnp.where(core == 0, first, second), jnp.where(
-            core == 0, parts_first, parts_second
-        )
-
-    return kept(c), kept(1 - c)
-
-
-def reduce_gradient(lefts, rights, tables, core):
-    own, other = tables
-    sent = gradient_blocks(*other, lefts, rights)[0]
-    received = lax.ppermute(sent, "c", SWAP)
-    main, diagonal, home = gradient_blocks(*own, lefts, rights, received)
-    along, cross = permutes()
-    arrived = lax.ppermute(diagonal, PLANE, cross)
-    size, width = diagonal.shape
-    halves = main.reshape(2, size, width)
-    aimed = lax.broadcasted_iota(jnp.int32, (2, 1, 1), 0) == 1 - core
-    halves = jnp.where(
-        aimed, (halves.astype(jnp.float32) + arrived.astype(jnp.float32)).astype(main.dtype), halves
-    )
-    landed = lax.ppermute(halves, PLANE, along)
-    passed = lax.ppermute(lax.dynamic_index_in_dim(landed, 1 - core, 0, False), "c", SWAP)
-    kept = lax.dynamic_index_in_dim(landed, core, 0, False)
-    total = home.astype(jnp.float32) + kept.astype(jnp.float32) + passed.astype(jnp.float32)
-    return lax.psum_scatter(total.astype(jnp.bfloat16), "z", scatter_dimension=0, tiled=True)
+    return along, cross, [(target, source) for source, target in cross]
+
+
+def after(value, *done):
+    return lax.optimization_barrier((value,) + done)[0]
+
+
+def barrier(*values):
+    return lax.optimization_barrier(values)
+
+
+def place_kernel(table_ref, *refs, widths):
+    pieces = refs[:8]
+    outs, held, arrived, left = refs[8:-3], refs[-3], refs[-2], refs[-1]
+    loads, stores = [], []
+    for i, piece in enumerate(pieces):
+        loads.append(pltpu.make_async_copy(piece, held.at[i], arrived.at[i]))
+        loads[-1].start()
+    for i, piece in enumerate(pieces):
+        size, start = piece.shape[0], 0
+        row = pl.multiple_of(table_ref[i] * size, size)
+        loads[i].wait()
+        for j, (out, width) in enumerate(zip(outs, widths)):
+            column = pl.multiple_of(table_ref[8 + i] * width, width)
+            stores.append(
+                pltpu.make_async_copy(
+                    held.at[i, :, pl.ds(start, width)],
+                    out.at[pl.ds(row, size), pl.ds(column, width)],
+                    left.at[i, j],
+                )
+            )
+            stores[-1].start()
+            start += width
+    for store in stores:
+        store.wait()
+
+
+def place(pieces, table, widths):
+    size = pieces[0].shape[0]
+    anywhere = pl.BlockSpec(memory_space=pl.ANY)
+    return pl.pallas_call(
+        functools.partial(place_kernel, widths=widths),
+        grid_spec=pltpu.PrefetchScalarGridSpec(
+            num_scalar_prefetch=1,
+            grid=(1,),
+            in_specs=[anywhere] * 8,
+            out_specs=[anywhere] * len(widths),
+            scratch_shapes=[
+                pltpu.VMEM((8, size, sum(widths)), jnp.bfloat16),
+                pltpu.SemaphoreType.DMA((8,)),
+                pltpu.SemaphoreType.DMA((8, len(widths))),
+            ],
+        ),
+        out_shape=[jax.ShapeDtypeStruct((4 * size, 2 * w), jnp.bfloat16) for w in widths],
+        compiler_params=pltpu.CompilerParams(vmem_limit_bytes=16 * 1024 * 1024),
+        cost_estimate=pl.CostEstimate(
+            flops=0, bytes_accessed=32 * size * sum(widths), transcendentals=0
+        ),
+        name="place",
+    )(table, *pieces)
+
+
+def plane_spots(core, x, y):
+    main = jnp.where(core == 0, 2 - 2 * x, 2 * x)
+    part = jnp.where(core == 0, y, 1 - y)
+    rows = [2 * x + core, main + core, main + 1 - core, 3 - 2 * x - core]
+    return rows, [y, part, part, 1 - y]
+
+
+def gather_weight(pieces, coords, widths):
+    x, c, y, _ = coords
+    pieces = pieces + [lax.ppermute(item, "c", SWAP) for item in pieces[2:]]
+    (rows, parts), (partner_rows, partner_parts) = (plane_spots(k, x, y) for k in (c, 1 - c))
+    order = [rows[0], partner_rows[0]] + rows[1:] + partner_rows[1:]
+    order += [parts[0], partner_parts[0]] + parts[1:] + partner_parts[1:]
+    return place(pieces, jnp.stack(order).astype(jnp.int32), widths)
+
+
+def scatter_kernel(table_ref, *refs, blocks):
+    pieces, (out, held, arrived, left) = refs[:-4], refs[-4:]
+    size = pieces[0].shape[0] // blocks
+    width = pieces[0].shape[1]
+    loads, stores = [], []
+    for i, piece in enumerate(pieces):
+        for j in range(blocks):
+            rows = pl.ds(j * size, size)
+            loads.append(
+                pltpu.make_async_copy(piece.at[rows], held.at[i, rows], arrived.at[i, j])
+            )
+            loads[-1].start()
+    for i in range(len(pieces)):
+        for j in range(blocks):
+            at = 2 * (i * blocks + j)
+            row = pl.multiple_of(table_ref[at] * size, size)
+            column = pl.multiple_of(table_ref[at + 1] * width, width)
+            loads[i * blocks + j].wait()
+            stores.append(
+                pltpu.make_async_copy(
+                    held.at[i, pl.ds(j * size, size)],
+                    out.at[pl.ds(row, size), pl.ds(column, width)],
+                    left.at[i, j],
+                )
+            )
+            stores[-1].start()
+    for store in stores:
+        store.wait()
+
+
+def finish_plane_first(pieces, coords, count):
+    x, c, y, _ = coords
+    rows, width = pieces[0].shape
+    blocks = 4 * count
+    table = []
+    for core in (c, 1 - c):
+        spots = list(zip(*plane_spots(core, x, y)))
+        for level in range(count):
+            for row, part in spots:
+                table += [row * count + level, part]
+    anywhere = pl.BlockSpec(memory_space=pl.ANY)
+    return pl.pallas_call(
+        functools.partial(scatter_kernel, blocks=blocks),
+        grid_spec=pltpu.PrefetchScalarGridSpec(
+            num_scalar_prefetch=1,
+            grid=(1,),
+            in_specs=[anywhere] * 2,
+            out_specs=anywhere,
+            scratch_shapes=[
+                pltpu.VMEM((2, rows, width), jnp.bfloat16),
+                pltpu.SemaphoreType.DMA((2, blocks)),
+                pltpu.SemaphoreType.DMA((2, blocks)),
+            ],
+        ),
+        out_shape=jax.ShapeDtypeStruct((rows, 2 * width), jnp.bfloat16),
+        compiler_params=pltpu.CompilerParams(vmem_limit_bytes=16 * 1024 * 1024),
+        cost_estimate=pl.CostEstimate(
+            flops=0, bytes_accessed=8 * rows * width, transcendentals=0
+        ),
+        name="scatter",
+    )(jnp.stack(table).astype(jnp.int32), *pieces)
+
+
+def three_parts(values, rows):
+    parts = []
+    for _ in range(3):
+        parts.append(lax.reduce_precision(values, exponent_bits=8, mantissa_bits=7))
+        values = values - parts[-1]
+    tile = jnp.concatenate(parts).astype(jnp.bfloat16).reshape(-1, LANES)
+    return jnp.pad(tile, ((0, rows - tile.shape[0]), (0, 0)))
+
+
+class Reduction:
+    def __init__(self, pairs, coords):
+        self.pairs = pairs
+        self.x, self.c, self.y, _ = coords
+        self.along, self.cross, _ = plane_permutes()
+        x, c, y = self.x, self.c, self.y
+        self.main_row = jnp.where(c == 0, 2 - 2 * x, 2 * x)
+        self.main_part = jnp.where(c == 0, y, 1 - y)
+        self.partner_row = jnp.where(c == 0, 2 * x, 2 - 2 * x)
+        self.partner_part = 1 - self.main_part
+
+    def block(self, row, count, part, extras=()):
+        pieces, start = [], 0
+        pairs, extras = barrier(self.pairs, list(extras))
+        for left, right in pairs:
+            size, width = left.shape[1] // 4, right.shape[1] // 2
+            picked = lax.dynamic_slice_in_dim(left, row * size, count * size, 1)
+            total = dot_tn(picked, lax.dynamic_slice_in_dim(right, part * width, width, 1))
+            for extra, at in extras:
+                if at is not None:
+                    extra = lax.dynamic_slice_in_dim(extra, at * size, count * size, 0)
+                total = total + extra[:, start : start + width].astype(jnp.float32)
+            pieces.append(total.astype(jnp.bfloat16))
+            start += width
+        return pieces[0] if len(pieces) == 1 else jnp.concatenate(pieces, axis=1)
+
+    def send(self):
+        corner = self.block(3 - 2 * self.x - self.c, 1, 1 - self.y)
+        main = self.block(self.partner_row, 2, self.partner_part)
+        self.corner_in = lax.ppermute(corner, "c", SWAP)
+        self.main_in = lax.ppermute(main, "c", SWAP)
+        return corner, main
+
+    def spread(self):
+        x, c, y = self.x, self.c, self.y
+        corner = self.block(2 - 2 * x + c, 1, 1 - y, [(self.corner_in, None)])
+        self.corner_got = lax.ppermute(corner, PLANE, self.cross)
+        main = self.block(self.main_row + c, 1, self.main_part, [(self.main_in, c)])
+        self.kept_got = lax.ppermute(main, PLANE, self.along)
+        return corner, main
+
+    def forward(self):
+        extras = [(self.main_in, 1 - self.c), (self.corner_got, None)]
+        main = self.block(self.main_row + 1 - self.c, 1, self.main_part, extras)
+        self.passed_got = lax.ppermute(main, PLANE, self.along)
+        return main
+
+    def hand_over(self):
+        home = self.block(2 * self.x + 1 - self.c, 1, self.y, [(self.passed_got, None)])
+        self.home_in = lax.ppermute(home, "c", SWAP)
+        return home
+
+    def finish(self):
+        home = self.block(2 * self.x + self.c, 1, self.y, [(self.kept_got, None), (self.home_in, None)])
+        return home, lax.psum_scatter(home, "z", scatter_dimension=0, tiled=True)
 
 
 def sequence_parallel(
@@ -570,11 +678,12 @@
     grid = tuple(lax.axis_size(name) for name in ("x", "c", "z"))
     dp_count = grid[0] * grid[1] * grid[2]
     mine = lax.axis_index("y")
-    core = lax.axis_index("c")
-    tables = block_tables(lax.axis_index("x"), core, mine)
+    coords = tuple(lax.axis_index(name) for name in ("x", "c", "y", "z"))
     half, width = layer_input.shape[1:]
     heads_local = qv_bias.shape[1]
     width_local = heads_local * HEAD_DIM
+    hidden_local = up_weight.shape[1]
+    wide = 3 * width_local
     span = range(parts)
 
     source = jnp.arange(width).reshape(grid[2], grid[0], grid[1], -1)
@@ -585,8 +694,7 @@
     def own_sequence(rows):
         kept = lax.dynamic_index_in_dim(rows, mine, 0, keepdims=False)
         sent = lax.dynamic_index_in_dim(rows, 1 - mine, 0, keepdims=False)
-        rows = jnp.concatenate([kept, lax.ppermute(sent, "y", SWAP)], axis=0)
-        return dot_nn(rows, order).astype(low)
+        return jnp.concatenate([kept, lax.ppermute(sent, "y", SWAP)], axis=0)
 
     def own_rows(rows):
         rows = dot_nt(rows.astype(low), order).astype(low)
@@ -594,29 +702,6 @@
         first = jnp.where(mine == 0, rows[:half], received)
         second = jnp.where(mine == 0, received, rows[:half])
         return jnp.stack([first, second])
-
-    packed = jnp.concatenate(
-        [
-            qkv_weight[0],
-            qkv_weight[1],
-            qkv_weight[2],
-            out_weight.T,
-            up_weight,
-            down_weight.T,
-        ],
-        axis=1,
-    )
-    gathered = lax.all_gather(packed, EVERY, axis=0, tiled=True).reshape(parts, width, -1)
-    wide = 3 * width_local
-    edges = [wide, wide + width_local, wide + width_local + up_weight.shape[1]]
-    qkv_full = gathered[:, :, : edges[0]]
-    out_full = gathered[:, :, edges[0] : edges[1]]
-    up_full = gathered[:, :, edges[1] : edges[2]]
-    down_full = gathered[:, :, edges[2] :]
-
-    rows_in = own_sequence(layer_input)
-    segments = lax.dynamic_index_in_dim(segment_ids, mine, 0, keepdims=False)
-    segments = jnp.where(mine == 0, segments, jnp.roll(segments, -half))
 
     small = jnp.concatenate(
         [
@@ -626,9 +711,57 @@
             row_biases.reshape(-1),
         ]
     )
-    copies = jnp.broadcast_to(small[None], (parts * dp_count, small.shape[0]))
-    small_all = lax.all_to_all(copies, EVERY, 0, 0, tiled=True)
-    small_all = small_all.reshape((parts,) + grid + (small.shape[0],))
+    packed = jnp.concatenate(
+        [
+            qkv_weight[0],
+            qkv_weight[1],
+            qkv_weight[2],
+            out_weight.T,
+            three_parts(small, up_weight.shape[0]),
+        ],
+        axis=1,
+    )
+
+    def lane_of(piece):
+        return lax.all_gather(piece, "z", axis=0, tiled=True)
+
+    along, _, back = plane_permutes()
+
+    def start_plane(lane):
+        other = lax.ppermute(lane, "c", SWAP)
+        main_other = lax.ppermute(other, PLANE, along)
+        return [lane, other, lax.ppermute(lane, PLANE, along), main_other]
+
+    lane = lane_of(packed)
+    up_piece, down_piece, layer_input, cotangent = after(
+        (up_weight, down_weight.T, layer_input, cotangent), packed
+    )
+    lane_up = lane_of(up_piece)
+    down_pieces = start_plane(down_piece)
+    rows_in, grad_output = own_sequence(layer_input), own_sequence(cotangent)
+    down_pieces.append(lax.ppermute(down_pieces[2], PLANE, back))
+    down_own = jnp.concatenate(
+        [down_pieces[0], down_pieces[2], down_pieces[3], down_pieces[4]], axis=0
+    )
+    lane, down_own, rows_in, grad_output = barrier(lane, down_own, rows_in, grad_output)
+    pieces = start_plane(lane)
+    rows_in, grad_output = after((rows_in, grad_output), pieces[1])
+    rows_in, grad_output = (dot_nn(item, order).astype(low) for item in (rows_in, grad_output))
+    pieces[2], pieces[3], lane_up, rows_in, grad_output, down_own = barrier(
+        pieces[2], pieces[3], lane_up, rows_in, grad_output, down_own
+    )
+    lane_down = lane_of(down_own)
+    pieces.append(lax.ppermute(pieces[2], PLANE, back))
+    up_pieces = start_plane(lane_up)
+    pieces[4], up_pieces[1] = barrier(pieces[4], up_pieces[1])
+    qkv_full, out_full, small_all = gather_weight(pieces, coords, (wide, width_local, LANES))
+    segments = lax.dynamic_index_in_dim(segment_ids, mine, 0, keepdims=False)
+    segments = jnp.where(mine == 0, segments, jnp.roll(segments, -half))
+
+    small_all = small_all.reshape(grid + (-1, parts, LANES))[:, :, :, : 3 * small.size // LANES]
+    small_all = small_all.astype(jnp.float32).transpose(4, 0, 1, 2, 3, 5)
+    small_all = small_all.reshape((parts,) + grid + (3, small.size))
+    small_all = small_all[..., 0, :] + small_all[..., 1, :] + small_all[..., 2, :]
     sizes = [qv_bias.size, up_bias.size, norm_gains.size, row_biases.size]
     starts = [0, sizes[0], sum(sizes[:2]), sum(sizes[:3])]
 
@@ -637,68 +770,111 @@
         return values.reshape((parts,) + grid + shard.shape)
 
     qv_all = section(0, qv_bias).transpose(4, 0, 5, 3, 1, 2, 6).reshape(2, parts, width_local)
-    upb_all = section(1, up_bias).transpose(0, 3, 1, 2, 4, 5).reshape(parts, -1)
+    upb_all = section(1, up_bias).transpose(0, 3, 1, 2, 4, 5).reshape(-1)
 
     def whole_rows(i, shard):
         values = section(i, shard).transpose(4, 1, 2, 3, 0, 5)
         return values.reshape(shard.shape[0], width)
 
     gains_all, biases_all = whole_rows(2, norm_gains), whole_rows(3, row_biases)
-
-    rows_wide = rows_in.astype(jnp.float32)
     none = jnp.zeros((width_local,), jnp.float32)
-    projected, contexts, stats = [], [], []
-    for t in span:
-        bias = jnp.concatenate([qv_all[0, t], none, qv_all[1, t]])
-        projected.append((dot_nn(rows_in, qkv_full[t]) + bias).astype(low))
-        context, stat = attend_call(projected[t], segments)
-        contexts.append(context)
-        stats.append(stat)
-    attention = sum(dot_nt(contexts[t], out_full[t]) for t in span)
-    residual_one = rows_wide + attention + biases_all[0]
+    qkv_bias = jnp.concatenate(
+        [item for t in span for item in (qv_all[0, t], none, qv_all[1, t])]
+    )
+
+    up_pieces[2], qkv_full = barrier(up_pieces[2], qkv_full)
+    projected = (dot_nn(rows_in, qkv_full) + qkv_bias).astype(low)
+    up_pieces[3], projected = barrier(up_pieces[3], projected)
+    up_pieces.append(lax.ppermute(after(up_pieces[2], projected), PLANE, back))
+    context, stats = attend_call(projected, segments, parts)
+    attention = dot_nt(context, out_full)
+    residual_one = rows_in.astype(jnp.float32) + attention + biases_all[0]
     hidden, normed_one, inverse_one = normalize(residual_one, gains_all[0], biases_all[1])
     hidden_low = hidden.astype(low)
-    activated, slopes = [], []
-    for t in span:
-        value, slope = gelu_pair(dot_nn(hidden_low, up_full[t]) + upb_all[t])
-        activated.append(value.astype(low))
-        slopes.append(slope)
-    branch = sum(dot_nt(activated[t], down_full[t]) for t in span)
+    (up_full,) = gather_weight(up_pieces, coords, (hidden_local,))
+    activated, slope = gelu_pair(
+        dot_nn(hidden_low, up_full) + upb_all
+    )
+    activated, slope = activated.astype(low), slope.astype(low)
+    lane_down = after(lane_down, activated)
+    lane_other = lax.ppermute(lane_down, "c", SWAP)
+    down_full = finish_plane_first([lane_down, lane_other], coords, grid[2])
+    branch = dot_nt(activated, down_full)
     residual_two = hidden + branch + biases_all[2]
     result, normed_two, inverse_two = normalize(residual_two, gains_all[1], biases_all[3])
 
-    grad_output = own_sequence(cotangent).astype(jnp.float32)
+    grad_output = grad_output.astype(jnp.float32)
+    grad_two = norm_back(grad_output, normed_two, inverse_two, gains_all[1])
+    branch_grad = grad_two.astype(low)
+
+    down = Reduction([(branch_grad, activated)], coords)
+    sent = down.send()
+    columns = [slice(t * hidden_local, (t + 1) * hidden_local) for t in span]
+    branch_late = after(branch_grad, *sent)
+    grad_first = (dot_nn(branch_late, down_full[:, columns[0]]) * slope[:, columns[0]]).astype(low)
+    down.corner_in = after(down.corner_in, grad_first)
+    moved = down.spread()
+    branch_late = after(branch_grad, *moved)
+    grad_second = (dot_nn(branch_late, down_full[:, columns[1]]) * slope[:, columns[1]]).astype(low)
+    grad_upper = jnp.concatenate([grad_first, grad_second], axis=1)
+    up = Reduction([(hidden_low, grad_upper)], coords)
+    sent = up.send()
+    down.corner_got = after(down.corner_got, *sent)
+    moved = down.forward()
+    grad_hidden = grad_two + dot_nt(after(grad_upper, moved), up_full)
+    grad_one = norm_back(grad_hidden, normed_one, inverse_one, gains_all[0])
+    attention_grad = grad_one.astype(low)
+    grad_context = dot_nn(attention_grad, out_full).astype(low)
+    up.corner_in = after(up.corner_in, grad_context, down.kept_got)
+    moved = up.spread()
+    grad_projected = attend_back_call(
+        projected, after(grad_context, *moved), segments, stats, parts, 0
+    )
+    down.passed_got = after(down.passed_got, grad_projected)
+    moved = down.hand_over()
+    up.corner_got = after(up.corner_got, moved)
+    moved = up.forward()
+    down.home_in = after(down.home_in, moved)
+    moved, down_sum = down.finish()
+    grad_projected = attend_back_call(
+        projected, after(grad_context, moved), segments, stats, parts, 1, grad_projected
+    )
+    last = Reduction([(rows_in, grad_projected), (attention_grad, context)], coords)
+    sent = last.send()
+    up.passed_got = after(up.passed_got, *sent)
+    moved = up.hand_over()
+    last.corner_in = after(last.corner_in, moved, up.kept_got)
+    moved = last.spread()
+    up.home_in = after(up.home_in, *moved)
+    moved, up_sum = up.finish()
+    input_grad = grad_one + dot_nt(after(grad_projected, moved), qkv_full)
+    last.corner_got = after(last.corner_got, input_grad)
+    moved = last.forward()
+    grad_output, grad_two, grad_hidden, grad_one, grad_upper, grad_projected = after(
+        (grad_output, grad_two, grad_hidden, grad_one, grad_upper, grad_projected), moved
+    )
     gain_two_grad = jnp.sum(grad_output * normed_two, axis=0)
     shift_two_grad = jnp.sum(grad_output, axis=0)
-    grad_two = norm_back(grad_output, normed_two, inverse_two, gains_all[1])
     down_bias_grad = jnp.sum(grad_two, axis=0)
-    branch_grad = grad_two.astype(low)
-    down_sum = reduce_gradient([branch_grad], [activated], tables, core)
-    outputs = own_rows(result)
-    grad_upper = [(dot_nn(branch_grad, down_full[t]) * slopes[t]).astype(low) for t in span]
-    upb_grad = jnp.stack([jnp.sum(grad_upper[t].astype(jnp.float32), axis=0) for t in span])
-    up_sum = reduce_gradient([hidden_low], [grad_upper], tables, core)
-    grad_hidden = grad_two + sum(dot_nt(grad_upper[t], up_full[t]) for t in span)
     gain_one_grad = jnp.sum(grad_hidden * normed_one, axis=0)
     shift_one_grad = jnp.sum(grad_hidden, axis=0)
-    grad_one = norm_back(grad_hidden, normed_one, inverse_one, gains_all[0])
     out_bias_grad = jnp.sum(grad_one, axis=0)
-    attention_grad = grad_one.astype(low)
-    grad_projected, qv_grads, input_grad = [], [], grad_one
-    for t in span:
-        grad_context = dot_nn(attention_grad, out_full[t]).astype(low)
-        grad_projected.append(attend_back_call(projected[t], grad_context, segments, stats[t]))
-        sums = jnp.sum(grad_projected[t].astype(jnp.float32), axis=0).reshape(3, width_local)
-        qv_grads.append(jnp.stack([sums[0], sums[2]]))
-    last_sum = reduce_gradient(
-        [rows_in, attention_grad], [grad_projected, contexts], tables, core
-    )
-    for t in span:
-        input_grad = input_grad + dot_nt(grad_projected[t], qkv_full[t])
-    input_grads = own_rows(input_grad)
-
+    upb_grad = jnp.sum(grad_upper.astype(jnp.float32), axis=0)
+    qkv_sums = jnp.sum(grad_projected.astype(jnp.float32), axis=0)
+    last.passed_got = after(
+        last.passed_got,
+        *(gain_two_grad, shift_two_grad, down_bias_grad, gain_one_grad),
+        *(shift_one_grad, out_bias_grad, upb_grad, qkv_sums, last.kept_got),
+    )
+    moved = last.hand_over()
+    moved, last_sum = last.finish()
+    input_grads = own_rows(after(input_grad, moved))
+    outputs = own_rows(after(result, moved))
+
+    qkv_sums = qkv_sums.reshape(parts, 3, width_local)
     dp_order = (grid[2], grid[0], grid[1])
-    qv_grads = jnp.stack(qv_grads).reshape((parts, 2, heads_local) + dp_order + (-1,))
+    qv_grads = jnp.stack([qkv_sums[:, 0], qkv_sums[:, 2]], axis=1)
+    qv_grads = qv_grads.reshape((parts, 2, heads_local) + dp_order + (-1,))
     qv_grads = qv_grads.transpose(0, 4, 5, 3, 1, 2, 6).reshape(parts * dp_count, -1)
     upb_grad = upb_grad.reshape((parts,) + dp_order + (-1,))
     upb_grad = upb_grad.transpose(0, 2, 3, 1, 4).reshape(parts * dp_count, -1)

time: 480 us -> 418 us (0.87)
  waiting for transfers between devices: 213 us -> 72.4 us
  matrix products: 80.7 us -> 127 us
  Pallas kernels: 80.5 us -> 41.3 us
  starting transfers between devices: 28.4 us -> 53.8 us
  local copies, waits for them, and re-layouts: 31 us -> 53.4 us
  other arithmetic: 26.8 us -> 46.4 us
    all_gather x1 -> x3, waiting for transfers between devices: 128 us -> 26.5 us  [lane_of(): return lax.all_gather(piece, 'z', axis=0, tiled=True)]
    dot_general x0 -> x28, matrix products: none -> 64.5 us  [dot_tn(): lax.dot_general(a, b, (((0,), (0,)), ((), ())), preferred_element_type=jn...]
    ppermute x14 -> x39, waiting for transfers between devices: 75.4 us -> 30.9 us  [the longest x1 9.37 us: sequence_parallel(): pieces.append(lax.ppermute(pieces[2], PLANE, back))]
    pallas_call x10 -> x6, Pallas kernels: 80.5 us -> 41.3 us  [the longest x2 15.9 us: attend_back_call(): pl.pallas_call(attend_back_kernel, grid=(inner,), in_specs=[column(place)...]
    ppermute x14 -> x39, starting transfers between devices: 14.6 us -> 48.8 us  [the longest x1 20.9 us: sequence_parallel(): down_pieces.append(lax.ppermute(down_pieces[2], PLANE, back))]
    unnamed x79 -> x140, local copies, waits for them, and re-layouts: 11.9 us -> 30.7 us
    dot_general x9 -> x6, matrix products: 42.3 us -> 26 us  [dot_nt(): lax.dot_general(a, b, (((1,), (1,)), ((), ())), preferred_element_type=jn...]
    concatenate x2 -> x12, other arithmetic: 0.09 us -> 11.9 us  [the longest x7 8.17 us: block(): return pieces[0] if len(pieces) == 1 else jnp.concatenate(pieces, axis=1)]
  transfers between devices with their start and end apart: 22 -> 48, of which waited for: 11 -> 14; matrix products, arithmetic and copies ran while one was open for 19% -> 45% of each run, Pallas kernels for 14% -> 9%
where the time goes in v3:
time: 418 us; the launch traced here: 410 us
  matrix products  127 us (30%)
  waiting for transfers between devices  72.4 us (17%)
  starting transfers between devices  53.8 us (13%)
  local copies, waits for them, and re-layouts  53.4 us (13%)
  other arithmetic  46.4 us (11%)
  Pallas kernels  41.3 us (10%)
  between operations  15.4 us (4%)
    dot_general x28, matrix products, dot_tn(): lax.dot_general(a, b, (((0,), (0,)), ((), ())), preferred_element_type=jn...  64.5 us
    dot_general x7, matrix products, dot_nn(): return jnp.dot(a, b, preferred_element_type=jnp.float32)  36.3 us
    unnamed x140, local copies, waits for them, and re-layouts  30.7 us
    all_gather x3, waiting for transfers between devices, lane_of(): return lax.all_gather(piece, 'z', axis=0, tiled=True)  26.5 us
    dot_general x6, matrix products, dot_nt(): lax.dot_general(a, b, (((1,), (1,)), ((), ())), preferred_element_type=jn...  26 us
    ppermute x1, starting transfers between devices, sequence_parallel(): down_pieces.append(lax.ppermute(down_pieces[2], PLANE, back))  20.9 us
    pallas_call x2, Pallas kernels, attend_back_call(): pl.pallas_call(attend_back_kernel, grid=(inner,), in_specs=[column(place)...  15.9 us
    ppermute x2, waiting for transfers between devices, own_rows(): received = lax.ppermute(rows[half:], 'y', SWAP)  14.3 us
  transfers between devices with their start and end apart: 48, of which 14 were waited for; matrix products, arithmetic and copies ran while one was open for 45% of the time, Pallas kernels for 9%

profile of v3, /device:TPU:0, one launch (start us, length us, event | category | flops | bytes accessed | tf_op | source)
XLA Modules:
  0.0 409.5 jit_solution(8442364365509405398)
XLA Ops:
  16.0 3.0 collective-permute-start.5
  21.1 4.5 %collective-permute-done = bf16[64,2048]{1,0:T(8,128)(2,1)S(1)} collective-permute-done((bf16[64,2048]{1,0:T(8,128)(2,1)S(1)}, bf16[64,2048]{1,0:T(8,128)(2,1)S(1)}, u32[]{:S(2)}, u32[]{:S(2)}) %collective-permute-start) | collective-permute-done | bytes 262176 | tf_op jit(solution)/shard_map/ppermute | solution.py:733
  25.6 20.9 %collective-permute-start.3 = (bf16[64,2048]{1,0:T(8,128)(2,1)S(1)}, bf16[64,2048]{1,0:T(8,128)(2,1)S(1)}, u32[]{:S(2)}, u32[]{:S(2)}) collective-permute-start(bf16[64,2048]{1,0:T(8,128)(2,1)S(1)} %collective-permute-done), channel_id=1, source_target_pairs={{6,0},{7,1},{2,4},{3,5},{1,2},{0,3},{5,6},{4,7},{14,8},{15,9},{10,... | collective-permute-start | bytes 786440 | tf_op jit(solution)/shard_map/ppermute | solution.py:742
  50.1 2.6 collective-permute-done.3
  58.8 3.6 fusion.61
  62.4 2.3 fusion.60
  64.6 18.9 %all-gather.6.cloned.1.call-done.refs_0_ = bf16[256,2048]{1,0:T(8,128)(2,1)} async-done(((bf16[64,2048]{1,0:T(8,128)(2,1)}), bf16[256,2048]{1,0:T(8,128)(2,1)}) %all-gather.6.cloned.1.call-update) | async-done | bytes 1048592 | tf_op jit(solution)/shard_map/all_gather | solution.py:726
  85.7 3.5 collective-permute-done.9.refs_1_
  89.1 9.4 %collective-permute-done.12.refs_4_ = bf16[256,2176]{1,0:T(8,128)(2,1)S(1)} collective-permute-done((bf16[256,2176]{1,0:T(8,128)(2,1)S(1)}, bf16[256,2176]{1,0:T(8,128)(2,1)S(1)}, u32[]{:S(2)}, u32[]{:S(2)}) %collective-permute-start.12) | collective-permute-done | bytes 1114144 | tf_op jit(solution)/shard_map/ppermute | solution.py:754
  106.5 4.0 place.2
  110.6 2.6 copy-done.19
  123.2 7.6 %add_convert_fusion.q_ref.k_ref.v_ref = bf16[512,3072]{1,0:T(8,128)(2,1)} fusion(bf16[512,1024]{1,0:T(8,128)(2,1)S(1)} %copy-done.49, bf16[1024,3072]{1,0:T(8,128)(2,1)} %copy-done.19, f32[3072]{0:T(1024)S(1)} %constant_dynamic-update-slice_fusion.4), kind=kOutput, calls=%fused_computation.10 | convolution fusion | flops 3224371200 | bytes 10498048 | tf_op jit(solution)/shard_map/dot_general | solution.py:425
  135.1 13.4 %attend.1 = (bf16[512,1024]{1,0:T(8,128)(2,1)S(1)}, f32[8,2,512]{2,1,0:T(2,128)S(1)}) custom-call(bf16[512,3072]{1,0:T(8,128)(2,1)S(1)} %copy-done.23, bf16[512,3072]{1,0:T(8,128)(2,1)S(1)} %copy-done.23, bf16[512,3072]{1,0:T(8,128)(2,1)S(1)} %copy-done.23, s32[1,512]{1,0:T(1,128)S(1)} %get-tuple-element.349.row_ref, s32[512,1]{1,0:T(8,128)S(1)} %broadcast_select_fusion.col_ref), custom_call_target="tpu_custom_call" | custom-call | flops 4294967296 | bytes 4194304 | tf_op jit(solution)/shard_map/attend/pallas_call | solution.py:362
  152.2 2.2 fusion.52
  156.7 3.5 place.3
  160.2 3.3 copy-done
  163.6 9.3 %fusion.4 = (bf16[512,4096]{1,0:T(8,128)(2,1)}, bf16[512,4096]{1,0:T(8,128)(2,1)}) fusion(f32[4096]{0:T(1024)S(1)} %bitcast.157, bf16[512,1024]{1,0:T(8,128)(2,1)S(1)} %fusion.52, bf16[1024,4096]{1,0:T(8,128)(2,1)S(1)} %place.3), kind=kOutput, calls=%fused_computation.5 | convolution fusion | flops 4320133120 | bytes 17842176 | tf_op jit(solution)/shard_map/dot_general | solution.py:425
  172.8 7.6 %all-gather.8.cloned.1.call-done.refs_0_ = bf16[1024,2048]{1,0:T(8,128)(2,1)} async-done(((bf16[256,2048]{1,0:T(8,128)(2,1)}), bf16[1024,2048]{1,0:T(8,128)(2,1)}) %all-gather.8.cloned.1.call-update) | async-done | bytes 4194320 | tf_op jit(solution)/shard_map/all_gather | solution.py:726
  180.8 7.2 %collective-permute-done.20.refs_1_ = bf16[1024,2048]{1,0:T(8,128)(2,1)} collective-permute-done((bf16[1024,2048]{1,0:T(8,128)(2,1)}, bf16[1024,2048]{1,0:T(8,128)(2,1)}, u32[]{:S(2)}, u32[]{:S(2)}) %collective-permute-start.20) | collective-permute-done | bytes 4194336 | tf_op jit(solution)/shard_map/ppermute | solution.py:800
  188.0 2.2 copy-done.2
  190.2 4.5 %scatter.1 = bf16[1024,4096]{1,0:T(8,128)(2,1)S(1)} custom-call(s32[64]{0:T(128)S(1)} %stack.281.table_ref, bf16[1024,2048]{1,0:T(8,128)(2,1)S(1)} %copy-done.2, bf16[1024,2048]{1,0:T(8,128)(2,1)} %collective-permute-done.20.refs_1_), custom_call_target="tpu_custom_call" | custom-call | bytes 16777216 | tf_op jit(solution)/shard_map/scatter/pallas_call | solution.py:575
  194.7 4.8 %fusion.158 = (f32[512]{0:T(512)S(1)}, f32[512,1024]{1,0:T(8,128)S(1)}) fusion(f32[1024]{0:T(1024)S(1)} %add.516, bf16[512,4096]{1,0:T(8,128)(2,1)S(1)} %copy-done.33, bf16[1024,4096]{1,0:T(8,128)(2,1)S(1)} %scatter.1, f32[1024]{0:T(1024)S(1)} %add.483, f32[1024]{0:T(1024)S(1)} %mul.146, f32[512]{0:T(512)S(1)} %add_rsqrt_fusion.1, ...), kind=kOutput, calls=%fused_computation.280 | convolution fusion | flops 4298636800 | bytes 16795648 | tf_op jit(solution)/shard_map/dot_general | solution.py:429
  205.8 3.5 convolution_convert_fusion.4
  209.7 6.7 %multiply_convert_fusion.2 = bf16[512,2048]{1,0:T(8,128)(2,1)} fusion(bf16[512,4096]{1,0:T(8,128)(2,1)} %get-tuple-element.322, bf16[512,1024]{1,0:T(8,128)(2,1)S(1)} %copy-done.46, bf16[1024,4096]{1,0:T(8,128)(2,1)} %copy-done.1), kind=kOutput, calls=%fused_computation.17 | convolution fusion | flops 2150629376 | bytes 9437184 | tf_op jit(solution)/shard_map/dot_general | solution.py:425
  216.3 2.9 fusion.19
  220.7 3.7 fusion.20
  224.9 4.6 %multiply_convert_fusion.1 = bf16[512,2048]{1,0:T(8,128)(2,1)S(1)} fusion(bf16[512,4096]{1,0:T(8,128)(2,1)S(1)} %copy-done.62, bf16[512,1024]{1,0:T(8,128)(2,1)S(1)} %copy-done.46, bf16[1024,4096]{1,0:T(8,128)(2,1)} %copy-done.1), kind=kOutput, calls=%fused_computation.16 | convolution fusion | flops 2150629376 | bytes 9437184 | tf_op jit(solution)/shard_map/dot_general | solution.py:425
  230.8 2.6 convolution_convert_fusion.1
  235.7 4.2 %fusion.21 = bf16[256,2048]{1,0:T(8,128)(2,1)} fusion(bf16[256,2048]{1,0:T(8,128)(2,1)} %collective-permute-done.23, bf16[512,4096]{1,0:T(8,128)(2,1)} %get-tuple-element.210, s32[]{:T(128)S(6)} %select_n.215, bf16[512,2048]{1,0:T(8,128)(2,1)} %collective-permute-done.22, s32[]{:T(128)S(6)} %select_n.218, bf16[512,1024]{1,0:T(8,128)(2,1)} %copy-done.45, ...), kind=kOutput, calls=%fused_computation.49 | convolution fusion | flops 539492352 | bytes 5505036 | tf_op jit(solution)/shard_map/dot_general | solution.py:433
  241.4 8.9 %multiply_reduce_fusion.6 = (f32[512]{0:T(512)S(1)}, f32[512]{0:T(512)S(1)}, f32[512,1024]{1,0:T(8,128)S(1)}) fusion(f32[1024]{0:T(1024)S(1)} %mul.146, f32[512]{0:T(512)S(1)} %add_rsqrt_fusion.1, f32[512,1024]{1,0:T(8,128)S(1)} %copy-done.39, f32[512]{0:T(512)S(1)} %broadcast_multiply_fusion.5, f32[512,1024]{1,0:T(8,128)} %get-tuple-element.249, ...), kind=kOutput, calls=%fused_computation.99 | convolution fusion | flops 4298636288 | bytes 18886656 | tf_op jit(solution)/shard_map/dot_general | solution.py:429
  253.4 2.3 convolution_convert_fusion.6.grad_ref
  255.7 3.0 fusion.22
  259.8 3.7 fusion.23
  263.6 7.9 %attend_back.2.rest_0_ = bf16[512,3072]{1,0:T(8,128)(2,1)S(1)} custom-call(bf16[512,3072]{1,0:T(8,128)(2,1)S(1)} %copy-done.24, bf16[512,3072]{1,0:T(8,128)(2,1)S(1)} %copy-done.24, bf16[512,3072]{1,0:T(8,128)(2,1)S(1)} %copy-done.24, bf16[512,1024]{1,0:T(8,128)(2,1)S(1)} %copy-done.26, s32[1,512]{1,0:T(1,128)S(1)} %get-tuple-element.349.row_ref, ...), custom_call_target="tpu_custom_call" | custom-call | flops 5368709120 | bytes 3670016 | tf_op jit(solution)/shard_map/attend_back/pallas_call | solution.py:394
  271.5 3.0 fusion.24
  275.9 4.2 %fusion.25 = bf16[256,2048]{1,0:T(8,128)(2,1)} fusion(bf16[256,2048]{1,0:T(8,128)(2,1)} %collective-permute-done.29, bf16[512,4096]{1,0:T(8,128)(2,1)} %copy-done.28, s32[]{:T(128)S(6)} %select_n.215, bf16[512,2048]{1,0:T(8,128)(2,1)} %collective-permute-done.27, s32[]{:T(128)S(6)} %select_n.222, bf16[512,1024]{1,0:T(8,128)(2,1)} %copy-done.43, ...), kind=kOutput, calls=%fused_computation.53 | convolution fusion | flops 539492352 | bytes 5505036 | tf_op jit(solution)/shard_map/dot_general | solution.py:433
  281.5 3.5 fusion.26
  288.1 8.0 %attend_back.3 = bf16[512,3072]{1,0:T(8,128)(2,1)S(1)} custom-call(bf16[512,3072]{1,0:T(8,128)(2,1)S(1)} %copy-done.25, bf16[512,3072]{1,0:T(8,128)(2,1)S(1)} %copy-done.25, bf16[512,3072]{1,0:T(8,128)(2,1)S(1)} %copy-done.25, bf16[512,1024]{1,0:T(8,128)(2,1)S(1)} %copy-done.27, ...), custom_call_target="tpu_custom_call", output_to_operand_aliasing={{}: (7, {})} | custom-call | flops 5368709120 | bytes 3670016 | tf_op jit(solution)/shard_map/attend_back/pallas_call | solution.py:394
  302.3 3.8 fusion.27
  317.6 3.5 fusion.28
  321.1 7.6 %convolution_add_fusion.15 = bf16[512,1024]{1,0:T(8,128)(2,1)} fusion(f32[512,1024]{1,0:T(8,128)} %get-tuple-element.251, bf16[512,3072]{1,0:T(8,128)(2,1)S(1)} %attend_back.3, bf16[1024,3072]{1,0:T(8,128)(2,1)} %copy-done.19), kind=kOutput, calls=%fused_computation.108 | convolution fusion | flops 3222274048 | bytes 12582912 | tf_op jit(solution)/shard_map/dot_general | solution.py:429
  334.1 2.8 convert_element_type.252
  341.1 3.3 convert_reduce_fusion
  344.7 2.1 fusion.145
  353.0 3.0 multiply_add_fusion
  360.0 2.6 all-to-all-start
  380.9 6.5 %collective-permute-done.40 = bf16[256,1024]{1,0:T(8,128)(2,1)} collective-permute-done((bf16[256,1024]{1,0:T(8,128)(2,1)}, bf16[256,1024]{1,0:T(8,128)(2,1)}, u32[]{:S(2)}, u32[]{:S(2)}) %collective-permute-start.40) | collective-permute-done | bytes 524320 | tf_op jit(solution)/shard_map/ppermute | solution.py:701
  389.6 7.8 %collective-permute-done.39 = bf16[256,1024]{1,0:T(8,128)(2,1)} collective-permute-done((bf16[256,1024]{1,0:T(8,128)(2,1)}, bf16[256,1024]{1,0:T(8,128)(2,1)}, u32[]{:S(2)}, u32[]{:S(2)}) %collective-permute-start.39) | collective-permute-done | bytes 524320 | tf_op jit(solution)/shard_map/ppermute | solution.py:701
  (357 shorter events, 137.6 us)
Async XLA Ops:
  7.2 47.3 %all-gather.4.cloned.1.call-start = ((), (), s32[]{:S(2)}) async-start(), calls=%async_computation.4 | async-start | bytes 1392640 | tf_op jit(solution)/shard_map/all_gather | solution.py:726
  14.6 69.0 %all-gather.6.cloned.1.call-start = ((), (), s32[]{:S(2)}) async-start(), calls=%async_computation.5 | async-start | bytes 1310720 | tf_op jit(solution)/shard_map/all_gather | solution.py:726
  16.0 32.1 %collective-permute-start.5 = (bf16[256,1024]{1,0:T(8,128)(2,1)S(1)}, bf16[256,1024]{1,0:T(8,128)(2,1)S(1)}, u32[]{:S(2)}, u32[]{:S(2)}) collective-permute-start(bf16[256,1024]{1,0:T(8,128)(2,1)S(1)} %get-tuple-element.329), channel_id=1, source_target_pairs={{0,1},{1,0},{2,3},{3,2},{4,5},{5,4},{6,7},{7,6},{8,9},{9,8},{10,11... | collective-permute-start | bytes 1572872 | tf_op jit(solution)/shard_map/ppermute | solution.py:697
  19.1 30.0 %collective-permute-start.4 = (bf16[256,1024]{1,0:T(8,128)(2,1)S(1)}, bf16[256,1024]{1,0:T(8,128)(2,1)S(1)}, u32[]{:S(2)}, u32[]{:S(2)}) collective-permute-start(bf16[256,1024]{1,0:T(8,128)(2,1)S(1)} %get-tuple-element.331), channel_id=1, source_target_pairs={{0,1},{1,0},{2,3},{3,2},{4,5},{5,4},{6,7},{7,6},{8,9},{9,8},{10,11... | collective-permute-start | bytes 1572872 | tf_op jit(solution)/shard_map/ppermute | solution.py:697
  19.2 6.4 %collective-permute-start = (bf16[64,2048]{1,0:T(8,128)(2,1)S(1)}, bf16[64,2048]{1,0:T(8,128)(2,1)S(1)}, u32[]{:S(2)}, u32[]{:S(2)}) collective-permute-start(bf16[64,2048]{1,0:T(8,128)(2,1)S(1)} %bitcast.151), channel_id=1, source_target_pairs={{0,4},{1,5},{4,0},{5,1},{2,3},{3,2},{6,7},{7,6},{8,12},{9,13},{12,... | collective-permute-start | bytes 786440 | tf_op jit(solution)/shard_map/ppermute | solution.py:733
  21.1 25.4 %collective-permute-start.1 = (bf16[64,2048]{1,0:T(8,128)(2,1)S(1)}, bf16[64,2048]{1,0:T(8,128)(2,1)S(1)}, u32[]{:S(2)}, u32[]{:S(2)}) collective-permute-start(bf16[64,2048]{1,0:T(8,128)(2,1)S(1)} %bitcast.152), channel_id=1, source_target_pairs={{0,2},{2,0},{1,3},{3,1},{4,6},{6,4},{5,7},{7,5},{8,10},{10,8},{9,1... | collective-permute-start | bytes 786440 | tf_op jit(solution)/shard_map/ppermute | solution.py:731
  25.6 27.1 %collective-permute-start.3 = (bf16[64,2048]{1,0:T(8,128)(2,1)S(1)}, bf16[64,2048]{1,0:T(8,128)(2,1)S(1)}, u32[]{:S(2)}, u32[]{:S(2)}) collective-permute-start(bf16[64,2048]{1,0:T(8,128)(2,1)S(1)} %collective-permute-done), channel_id=1, source_target_pairs={{6,0},{7,1},{2,4},{3,5},{1,2},{0,3},{5,6},{4,7},{14,8},{15,9},{10,... | collective-permute-start | bytes 786440 | tf_op jit(solution)/shard_map/ppermute | solution.py:742
  46.5 6.8 %collective-permute-start.2 = (bf16[64,2048]{1,0:T(8,128)(2,1)S(1)}, bf16[64,2048]{1,0:T(8,128)(2,1)S(1)}, u32[]{:S(2)}, u32[]{:S(2)}) collective-permute-start(bf16[64,2048]{1,0:T(8,128)(2,1)S(1)} %collective-permute-done.1), channel_id=1, source_target_pairs={{0,4},{1,5},{4,0},{5,1},{2,3},{3,2},{6,7},{7,6},{8,12},{9,13},{12,... | collective-permute-start | bytes 786440 | tf_op jit(solution)/shard_map/ppermute | solution.py:732
  54.5 3.0 collective-permute-start.7
  54.6 125.8 %all-gather.8.cloned.1.call-start = ((), (), s32[]{:S(2)}) async-start(), calls=%async_computation.6 | async-start | bytes 5242880 | tf_op jit(solution)/shard_map/all_gather | solution.py:726
  54.7 28.9 %collective-permute-start.6 = (bf16[256,2176]{1,0:T(8,128)(2,1)}, bf16[256,2176]{1,0:T(8,128)(2,1)S(1)}, u32[]{:S(2)}, u32[]{:S(2)}) collective-permute-start(bf16[256,2176]{1,0:T(8,128)(2,1)} %all-gather.4.cloned.1.call-done.refs_0_), channel_id=1, source_target_pairs={{0,4},{1,5},{4,0},{5,1},{2,3},{3,2},{6,7},{7,6},{8,12},{9,13},{12,... | collective-permute-start | bytes 3342344 | tf_op jit(solution)/shard_map/ppermute | solution.py:733
  57.4 26.1 %collective-permute-start.8 = (bf16[256,2176]{1,0:T(8,128)(2,1)S(1)}, bf16[256,2176]{1,0:T(8,128)(2,1)}, u32[]{:S(2)}, u32[]{:S(2)}) collective-permute-start(bf16[256,2176]{1,0:T(8,128)(2,1)S(1)} %collective-permute-done.7.refs_1_), channel_id=1, source_target_pairs={{0,4},{1,5},{4,0},{5,1},{2,3},{3,2},{6,7},{7,6},{8,12},{9,13},{12,... | collective-permute-start | bytes 3342344 | tf_op jit(solution)/shard_map/ppermute | solution.py:732
  83.5 15.0 %collective-permute-start.12 = (bf16[256,2176]{1,0:T(8,128)(2,1)S(1)}, bf16[256,2176]{1,0:T(8,128)(2,1)S(1)}, u32[]{:S(2)}, u32[]{:S(2)}) collective-permute-start(bf16[256,2176]{1,0:T(8,128)(2,1)S(1)} %collective-permute-done.6.refs_2_), channel_id=1, source_target_pairs={{6,0},{7,1},{2,4},{3,5},{1,2},{0,3},{5,6},{4,7},{14,8},{15,9},{10,... | collective-permute-start | bytes 3342344 | tf_op jit(solution)/shard_map/ppermute | solution.py:754
  84.4 4.8 %collective-permute-start.9 = (bf16[256,2048]{1,0:T(8,128)(2,1)}, bf16[256,2048]{1,0:T(8,128)(2,1)S(1)}, u32[]{:S(2)}, u32[]{:S(2)}) collective-permute-start(bf16[256,2048]{1,0:T(8,128)(2,1)} %all-gather.6.cloned.1.call-done.refs_0_), channel_id=1, source_target_pairs={{0,2},{2,0},{1,3},{3,1},{4,6},{6,4},{5,7},{7,5},{8,10},{10,8},{9,1... | collective-permute-start | bytes 3145736 | tf_op jit(solution)/shard_map/ppermute | solution.py:731
  85.2 16.2 %collective-permute-start.13 = (bf16[256,2176]{1,0:T(8,128)(2,1)S(1)}, bf16[256,2176]{1,0:T(8,128)(2,1)}, u32[]{:S(2)}, u32[]{:S(2)}) collective-permute-start(bf16[256,2176]{1,0:T(8,128)(2,1)S(1)} %collective-permute-done.6.refs_2_), channel_id=1, source_target_pairs={{0,2},{2,0},{1,3},{3,1},{4,6},{6,4},{5,7},{7,5},{8,10},{10,8},{9,1... | collective-permute-start | bytes 3342344 | tf_op jit(solution)/shard_map/ppermute | solution.py:527
  85.2 16.2 %collective-permute-start.14 = (bf16[256,2176]{1,0:T(8,128)(2,1)}, bf16[256,2176]{1,0:T(8,128)(2,1)}, u32[]{:S(2)}, u32[]{:S(2)}) collective-permute-start(bf16[256,2176]{1,0:T(8,128)(2,1)} %collective-permute-done.8.refs_3_), channel_id=1, source_target_pairs={{0,2},{2,0},{1,3},{3,1},{4,6},{6,4},{5,7},{7,5},{8,10},{10,8},{9,1... | collective-permute-start | bytes 3342344 | tf_op jit(solution)/shard_map/ppermute | solution.py:527
  98.5 2.9 collective-permute-start.15
  99.2 24.0 %collective-permute-start.11 = (bf16[256,2048]{1,0:T(8,128)(2,1)}, bf16[256,2048]{1,0:T(8,128)(2,1)}, u32[]{:S(2)}, u32[]{:S(2)}) collective-permute-start(bf16[256,2048]{1,0:T(8,128)(2,1)} %all-gather.6.cloned.1.call-done.refs_0_), channel_id=1, source_target_pairs={{0,4},{1,5},{4,0},{5,1},{2,3},{3,2},{6,7},{7,6},{8,12},{9,13},{12,... | collective-permute-start | bytes 3145736 | tf_op jit(solution)/shard_map/ppermute | solution.py:733
  100.8 266.9 %reduce-scatter.8.cloned.1.call-start = ((), (), s32[]{:S(2)}) async-start(), calls=%async_computation.9 | async-start | bytes 1310720 | tf_op jit(solution)/shard_map/reduce_scatter | solution.py:660
  100.8 30.0 %collective-permute-start.10 = (bf16[256,2048]{1,0:T(8,128)(2,1)}, bf16[256,2048]{1,0:T(8,128)(2,1)}, u32[]{:S(2)}, u32[]{:S(2)}) collective-permute-start(bf16[256,2048]{1,0:T(8,128)(2,1)} %copy-done.11), channel_id=1, source_target_pairs={{0,4},{1,5},{4,0},{5,1},{2,3},{3,2},{6,7},{7,6},{8,12},{9,13},{12,... | collective-permute-start | bytes 3145736 | tf_op jit(solution)/shard_map/ppermute | solution.py:732
  130.8 23.6 %collective-permute-start.17 = (bf16[256,2048]{1,0:T(8,128)(2,1)}, bf16[256,2048]{1,0:T(8,128)(2,1)}, u32[]{:S(2)}, u32[]{:S(2)}) collective-permute-start(bf16[256,2048]{1,0:T(8,128)(2,1)} %collective-permute-done.11.refs_2_), channel_id=1, source_target_pairs={{0,2},{2,0},{1,3},{3,1},{4,6},{6,4},{5,7},{7,5},{8,10},{10,8},{9,1... | collective-permute-start | bytes 3145736 | tf_op jit(solution)/shard_map/ppermute | solution.py:527
  130.9 19.6 %collective-permute-start.16 = (bf16[256,2048]{1,0:T(8,128)(2,1)}, bf16[256,2048]{1,0:T(8,128)(2,1)}, u32[]{:S(2)}, u32[]{:S(2)}) collective-permute-start(bf16[256,2048]{1,0:T(8,128)(2,1)} %collective-permute-done.11.refs_2_), channel_id=1, source_target_pairs={{6,0},{7,1},{2,4},{3,5},{1,2},{0,3},{5,6},{4,7},{14,8},{15,9},{10,... | collective-permute-start | bytes 3145736 | tf_op jit(solution)/shard_map/ppermute | solution.py:788
  132.5 21.8 %collective-permute-start.18 = (bf16[256,2048]{1,0:T(8,128)(2,1)}, bf16[256,2048]{1,0:T(8,128)(2,1)}, u32[]{:S(2)}, u32[]{:S(2)}) collective-permute-start(bf16[256,2048]{1,0:T(8,128)(2,1)} %collective-permute-done.10.refs_3_), channel_id=1, source_target_pairs={{0,2},{2,0},{1,3},{3,1},{4,6},{6,4},{5,7},{7,5},{8,10},{10,8},{9,1... | collective-permute-start | bytes 3145736 | tf_op jit(solution)/shard_map/ppermute | solution.py:527
  150.5 3.9 collective-permute-start.19
  180.5 7.5 %collective-permute-start.20 = (bf16[1024,2048]{1,0:T(8,128)(2,1)}, bf16[1024,2048]{1,0:T(8,128)(2,1)}, u32[]{:S(2)}, u32[]{:S(2)}) collective-permute-start(bf16[1024,2048]{1,0:T(8,128)(2,1)} %all-gather.8.cloned.1.call-done.refs_0_), channel_id=1, source_target_pairs={{0,2},{2,0},{1,3},{3,1},{4,6},{6,4},{5,7},{7,5},{8,10},{10,8},{9,1... | collective-permute-start | bytes 12582920 | tf_op jit(solution)/shard_map/ppermute | solution.py:800
  205.6 15.1 %collective-permute-start.22 = (bf16[512,2048]{1,0:T(8,128)(2,1)S(1)}, bf16[512,2048]{1,0:T(8,128)(2,1)}, u32[]{:S(2)}, u32[]{:S(2)}) collective-permute-start(bf16[512,2048]{1,0:T(8,128)(2,1)S(1)} %convolution_convert_fusion.2), channel_id=1, source_target_pairs={{0,2},{2,0},{1,3},{3,1},{4,6},{6,4},{5,7},{7,5},{8,10},{10,8},{9,1... | collective-permute-start | bytes 6291464 | tf_op jit(solution)/shard_map/ppermute | solution.py:636
  209.3 7.0 %collective-permute-start.21 = (bf16[256,2048]{1,0:T(8,128)(2,1)}, bf16[256,2048]{1,0:T(8,128)(2,1)}, u32[]{:S(2)}, u32[]{:S(2)}) collective-permute-start(bf16[256,2048]{1,0:T(8,128)(2,1)} %convolution_convert_fusion.4), channel_id=1, source_target_pairs={{0,2},{2,0},{1,3},{3,1},{4,6},{6,4},{5,7},{7,5},{8,10},{10,8},{9,1... | collective-permute-start | bytes 3145736 | tf_op jit(solution)/shard_map/ppermute | solution.py:635
  219.3 16.5 %collective-permute-start.23 = (bf16[256,2048]{1,0:T(8,128)(2,1)}, bf16[256,2048]{1,0:T(8,128)(2,1)}, u32[]{:S(2)}, u32[]{:S(2)}) collective-permute-start(bf16[256,2048]{1,0:T(8,128)(2,1)} %fusion.19), channel_id=1, source_target_pairs={{0,6},{1,7},{4,2},{5,3},{2,1},{3,0},{6,5},{7,4},{8,14},{9,15},{12,... | collective-permute-start | bytes 3145736 | tf_op jit(solution)/shard_map/ppermute | solution.py:642
  224.4 31.3 %collective-permute-start.24 = (bf16[256,2048]{1,0:T(8,128)(2,1)}, bf16[256,2048]{1,0:T(8,128)(2,1)}, u32[]{:S(2)}, u32[]{:S(2)}) collective-permute-start(bf16[256,2048]{1,0:T(8,128)(2,1)} %fusion.20), channel_id=1, source_target_pairs={{0,4},{1,5},{4,0},{5,1},{2,3},{3,2},{6,7},{7,6},{8,12},{9,13},{12,... | collective-permute-start | bytes 3145736 | tf_op jit(solution)/shard_map/ppermute | solution.py:644
  233.5 26.3 %collective-permute-start.27 = (bf16[512,2048]{1,0:T(8,128)(2,1)}, bf16[512,2048]{1,0:T(8,128)(2,1)}, u32[]{:S(2)}, u32[]{:S(2)}) collective-permute-start(bf16[512,2048]{1,0:T(8,128)(2,1)} %convolution_convert_fusion.1), channel_id=1, source_target_pairs={{0,2},{2,0},{1,3},{3,1},{4,6},{6,4},{5,7},{7,5},{8,10},{10,8},{9,1... | collective-permute-start | bytes 6291464 | tf_op jit(solution)/shard_map/ppermute | solution.py:636
  235.3 20.4 %collective-permute-start.26 = (bf16[256,2048]{1,0:T(8,128)(2,1)}, bf16[256,2048]{1,0:T(8,128)(2,1)}, u32[]{:S(2)}, u32[]{:S(2)}) collective-permute-start(bf16[256,2048]{1,0:T(8,128)(2,1)} %convolution_convert_fusion.3), channel_id=1, source_target_pairs={{0,2},{2,0},{1,3},{3,1},{4,6},{6,4},{5,7},{7,5},{8,10},{10,8},{9,1... | collective-permute-start | bytes 3145736 | tf_op jit(solution)/shard_map/ppermute | solution.py:635
  240.0 31.6 %collective-permute-start.25 = (bf16[256,2048]{1,0:T(8,128)(2,1)}, bf16[256,2048]{1,0:T(8,128)(2,1)}, u32[]{:S(2)}, u32[]{:S(2)}) collective-permute-start(bf16[256,2048]{1,0:T(8,128)(2,1)} %fusion.21), channel_id=1, source_target_pairs={{0,4},{1,5},{4,0},{5,1},{2,3},{3,2},{6,7},{7,6},{8,12},{9,13},{12,... | collective-permute-start | bytes 3145736 | tf_op jit(solution)/shard_map/ppermute | solution.py:650
  258.7 17.2 %collective-permute-start.29 = (bf16[256,2048]{1,0:T(8,128)(2,1)}, bf16[256,2048]{1,0:T(8,128)(2,1)}, u32[]{:S(2)}, u32[]{:S(2)}) collective-permute-start(bf16[256,2048]{1,0:T(8,128)(2,1)} %fusion.22), channel_id=1, source_target_pairs={{0,6},{1,7},{4,2},{5,3},{2,1},{3,0},{6,5},{7,4},{8,14},{9,15},{12,... | collective-permute-start | bytes 3145736 | tf_op jit(solution)/shard_map/ppermute | solution.py:642
  274.5 6.9 %collective-permute-start.28 = (bf16[256,2048]{1,0:T(8,128)(2,1)}, bf16[256,2048]{1,0:T(8,128)(2,1)}, u32[]{:S(2)}, u32[]{:S(2)}) collective-permute-start(bf16[256,2048]{1,0:T(8,128)(2,1)} %fusion.24), channel_id=1, source_target_pairs={{0,2},{2,0},{1,3},{3,1},{4,6},{6,4},{5,7},{7,5},{8,10},{10,8},{9,1... | collective-permute-start | bytes 3145736 | tf_op jit(solution)/shard_map/ppermute | solution.py:655
  275.2 30.9 %collective-permute-start.34 = (bf16[256,2048]{1,0:T(8,128)(2,1)}, bf16[256,2048]{1,0:T(8,128)(2,1)}, u32[]{:S(2)}, u32[]{:S(2)}) collective-permute-start(bf16[256,2048]{1,0:T(8,128)(2,1)} %fusion.23), channel_id=1, source_target_pairs={{0,4},{1,5},{4,0},{5,1},{2,3},{3,2},{6,7},{7,6},{8,12},{9,13},{12,... | collective-permute-start | bytes 3145736 | tf_op jit(solution)/shard_map/ppermute | solution.py:644
  280.1 22.2 %collective-permute-start.33 = (bf16[256,2048]{1,0:T(8,128)(2,1)}, bf16[256,2048]{1,0:T(8,128)(2,1)}, u32[]{:S(2)}, u32[]{:S(2)}) collective-permute-start(bf16[256,2048]{1,0:T(8,128)(2,1)} %fusion.25), channel_id=1, source_target_pairs={{0,4},{1,5},{4,0},{5,1},{2,3},{3,2},{6,7},{7,6},{8,12},{9,13},{12,... | collective-permute-start | bytes 3145736 | tf_op jit(solution)/shard_map/ppermute | solution.py:650
  300.3 11.2 %collective-permute-start.30 = (bf16[512,2048]{1,0:T(8,128)(2,1)}, bf16[512,2048]{1,0:T(8,128)(2,1)}, u32[]{:S(2)}, u32[]{:S(2)}) collective-permute-start(bf16[512,2048]{1,0:T(8,128)(2,1)} %pad_maximum_fusion.1), channel_id=1, source_target_pairs={{0,2},{2,0},{1,3},{3,1},{4,6},{6,4},{5,7},{7,5},{8,10},{10,8},{9,1... | collective-permute-start | bytes 6291464 | tf_op jit(solution)/shard_map/ppermute | solution.py:636
  301.7 4.5 %collective-permute-start.32 = (bf16[256,2048]{1,0:T(8,128)(2,1)}, bf16[256,2048]{1,0:T(8,128)(2,1)}, u32[]{:S(2)}, u32[]{:S(2)}) collective-permute-start(bf16[256,2048]{1,0:T(8,128)(2,1)} %pad_maximum_fusion.6), channel_id=1, source_target_pairs={{0,2},{2,0},{1,3},{3,1},{4,6},{6,4},{5,7},{7,5},{8,10},{10,8},{9,1... | collective-permute-start | bytes 3145736 | tf_op jit(solution)/shard_map/ppermute | solution.py:635
  302.2 76.9 %reduce-scatter.6.cloned.1.call-start = ((), (), s32[]{:S(2)}) async-start(), calls=%async_computation.8 | async-start | bytes 1310720 | tf_op jit(solution)/shard_map/reduce_scatter | solution.py:660
  306.1 11.5 %collective-permute-start.36 = (bf16[256,2048]{1,0:T(8,128)(2,1)}, bf16[256,2048]{1,0:T(8,128)(2,1)}, u32[]{:S(2)}, u32[]{:S(2)}) collective-permute-start(bf16[256,2048]{1,0:T(8,128)(2,1)} %fusion.27), channel_id=1, source_target_pairs={{0,2},{2,0},{1,3},{3,1},{4,6},{6,4},{5,7},{7,5},{8,10},{10,8},{9,1... | collective-permute-start | bytes 3145736 | tf_op jit(solution)/shard_map/ppermute | solution.py:655
  310.6 18.1 %collective-permute-start.35 = (bf16[256,2048]{1,0:T(8,128)(2,1)}, bf16[256,2048]{1,0:T(8,128)(2,1)}, u32[]{:S(2)}, u32[]{:S(2)}) collective-permute-start(bf16[256,2048]{1,0:T(8,128)(2,1)} %pad_maximum_fusion.7), channel_id=1, source_target_pairs={{0,6},{1,7},{4,2},{5,3},{2,1},{3,0},{6,5},{7,4},{8,14},{9,15},{12,... | collective-permute-start | bytes 3145736 | tf_op jit(solution)/shard_map/ppermute | solution.py:642
  316.1 30.7 %collective-permute-start.31 = (bf16[256,2048]{1,0:T(8,128)(2,1)}, bf16[256,2048]{1,0:T(8,128)(2,1)}, u32[]{:S(2)}, u32[]{:S(2)}) collective-permute-start(bf16[256,2048]{1,0:T(8,128)(2,1)} %pad_maximum_fusion.5), channel_id=1, source_target_pairs={{0,4},{1,5},{4,0},{5,1},{2,3},{3,2},{6,7},{7,6},{8,12},{9,13},{12,... | collective-permute-start | bytes 3145736 | tf_op jit(solution)/shard_map/ppermute | solution.py:644
  333.5 15.1 %collective-permute-start.37 = (bf16[256,2048]{1,0:T(8,128)(2,1)}, bf16[256,2048]{1,0:T(8,128)(2,1)}, u32[]{:S(2)}, u32[]{:S(2)}) collective-permute-start(bf16[256,2048]{1,0:T(8,128)(2,1)} %pad_maximum_fusion.8), channel_id=1, source_target_pairs={{0,4},{1,5},{4,0},{5,1},{2,3},{3,2},{6,7},{7,6},{8,12},{9,13},{12,... | collective-permute-start | bytes 3145736 | tf_op jit(solution)/shard_map/ppermute | solution.py:650
  353.0 9.8 %collective-permute-start.38 = (bf16[256,2048]{1,0:T(8,128)(2,1)}, bf16[256,2048]{1,0:T(8,128)(2,1)}, u32[]{:S(2)}, u32[]{:S(2)}) collective-permute-start(bf16[256,2048]{1,0:T(8,128)(2,1)} %pad_maximum_fusion.9), channel_id=1, source_target_pairs={{0,2},{2,0},{1,3},{3,1},{4,6},{6,4},{5,7},{7,5},{8,10},{10,8},{9,1... | collective-permute-start | bytes 3145736 | tf_op jit(solution)/shard_map/ppermute | solution.py:655
  360.0 10.0 %all-to-all-start = ((f32[32,1,384]{2,1,0:T(1,128)}), f32[32,1,384]{2,1,0:T(1,128)S(1)}, u32[]{:S(2)}, u32[]{:S(2)}) async-start(f32[32,1,384]{2,1,0:T(1,128)} %copy.70), calls=%async_computation.1 | async-start | bytes 98304 | tf_op jit(solution)/shard_map/all_to_all | solution.py:896
  362.6 37.0 %reduce-scatter.4.cloned.1.call-start = ((), (), s32[]{:S(2)}) async-start(), calls=%async_computation.7 | async-start | bytes 1310720 | tf_op jit(solution)/shard_map/reduce_scatter | solution.py:660
  372.3 15.1 %collective-permute-start.40 = (bf16[256,1024]{1,0:T(8,128)(2,1)}, bf16[256,1024]{1,0:T(8,128)(2,1)}, u32[]{:S(2)}, u32[]{:S(2)}) collective-permute-start(bf16[256,1024]{1,0:T(8,128)(2,1)} %slice.275), channel_id=1, source_target_pairs={{0,1},{1,0},{2,3},{3,2},{4,5},{5,4},{6,7},{7,6},{8,9},{9,8},{10,11... | collective-permute-start | bytes 1572872 | tf_op jit(solution)/shard_map/ppermute | solution.py:701
  375.6 21.8 %collective-permute-start.39 = (bf16[256,1024]{1,0:T(8,128)(2,1)}, bf16[256,1024]{1,0:T(8,128)(2,1)}, u32[]{:S(2)}, u32[]{:S(2)}) collective-permute-start(bf16[256,1024]{1,0:T(8,128)(2,1)} %slice.273), channel_id=1, source_target_pairs={{0,1},{1,0},{2,3},{3,2},{4,5},{5,4},{6,7},{7,6},{8,9},{9,8},{10,11... | collective-permute-start | bytes 1572872 | tf_op jit(solution)/shard_map/ppermute | solution.py:701
  (64 other events, 320.6 us)
Sparse Core Ops, SparseCore 0:
  14.7 31.6 all-gather.3
  54.7 28.7 all-gather.5
  100.9 79.5 all-gather.7
  302.4 23.8 reduce-scatter.7
  337.0 24.6 reduce-scatter.5
  367.8 28.3 reduce-scatter.3
